TPU v7x, 512 devices: a whole 4x4x16 slice. The times are simulated.
512 devices in a mesh: rows: 32 (over y_lo, z), filt: 16 (over y_hi, x, core).
Axes of the slice: x: 4, y: 4 (y_hi: 2, y_lo: 2; y = y_hi * 2 + y_lo), z: 16, core: 2. Of those that a mesh axis runs over, the one named last changes fastest.
Arguments:
- features: bfloat16 [512, 32, 512], P('filt', 'rows'), may hold values from -6 to 6
- first_weight: bfloat16 [512, 3, 3, 512], P('filt'), may hold values from -0.09375 to 0.09375
- second_weight: bfloat16 [512, 3, 3, 512], P('filt'), may hold values from -0.09375 to 0.09375
- out_grad: bfloat16 [512, 32, 512], P('filt', 'rows'), may hold values from -0.046875 to 0.046875
Outputs:
- block_out: bfloat16 [512, 32, 512], P('filt', 'rows')
- first_grad: float32 [512, 3, 3, 512], P('filt')
- second_grad: float32 [512, 3, 3, 512], P('filt')
All inputs are finite; a program needn't handle non-finite values.
Results may differ from a plain program's by a relative error of at most 0.024.
The roundings to bfloat16 on the way count: a program that leaves them out, or rounds other values in their place, can miss the bound.
Values may be sent and summed in bfloat16 or wider, within the bound.
A program may use at most 64 MiB of HBM per device.

v0:
```python
import jax
import jax.numpy as jnp
from jax import lax
from jax.sharding import PartitionSpec as P


def extended(cells, sides, width):
    for axis, dim in sides:
        count = lax.axis_size(axis)
        ends = count - 1
        head = lax.slice_in_dim(cells, 0, width, axis=dim)
        tail = lax.slice_in_dim(cells, cells.shape[dim] - width, cells.shape[dim], axis=dim)
        cells = jnp.concatenate(
            [
                lax.ppermute(tail, axis, [(i, (i + 1) % count) for i in range(ends)]),
                cells,
                lax.ppermute(head, axis, [((i + 1) % count, i) for i in range(ends)]),
            ],
            axis=dim,
        )
    return cells


def shift_cols(value, offset):
    if offset == 0:
        return value
    if offset > 0:
        return jnp.pad(value[..., offset:], ((0, 0), (0, 0), (0, offset)))
    return jnp.pad(value[..., :offset], ((0, 0), (0, 0), (-offset, 0)))


def conv_forward(weight, padded, count):
    total = jnp.zeros((weight.shape[0], count, padded.shape[2]), jnp.float32)
    for a in range(3):
        for b in range(3):
            part = jnp.einsum(
                "oi,ihw->ohw",
                weight[:, a, b, :],
                padded[:, a : a + count, :],
                preferred_element_type=jnp.float32,
            )
            total = total + shift_cols(part, b - 1)
    return total


def conv_backward(weight, padded, count):
    total = jnp.zeros((weight.shape[3], count, padded.shape[2]), jnp.float32)
    for a in range(3):
        for b in range(3):
            part = jnp.einsum(
                "oi,ohw->ihw",
                weight[:, a, b, :],
                padded[:, 2 - a : 2 - a + count, :],
                preferred_element_type=jnp.float32,
            )
            total = total + shift_cols(part, 1 - b)
    return total


def weight_terms(grad, padded, count):
    rows_out = []
    for a in range(3):
        cols_out = []
        for b in range(3):
            moved = shift_cols(grad, 1 - b)
            cols_out.append(
                jnp.einsum(
                    "ohw,ihw->oi",
                    moved,
                    padded[:, a : a + count, :],
                    preferred_element_type=jnp.float32,
                )
            )
        rows_out.append(jnp.stack(cols_out, axis=1))
    return jnp.stack(rows_out, axis=1)


def with_rims(value):
    return extended(value, (("rows", 1),), 1)


def all_channels(value):
    return lax.all_gather(with_rims(value), "filt", axis=0, tiled=True)


def per_device(features, first_weight, second_weight, out_grad):
    count = features.shape[1]
    padded_in = all_channels(features)
    pre_first = conv_forward(first_weight, padded_in, count)
    hidden = jnp.maximum(pre_first, 0.0).astype(jnp.bfloat16)
    padded_hidden = all_channels(hidden)
    pre_second = conv_forward(second_weight, padded_hidden, count) + features.astype(jnp.float32)
    block_out = jnp.maximum(pre_second, 0.0).astype(jnp.bfloat16)
    grad_second = jnp.where(pre_second > 0, out_grad.astype(jnp.float32), 0.0).astype(jnp.bfloat16)
    rimmed_grad = with_rims(grad_second)
    terms = conv_backward(second_weight, rimmed_grad, count)
    hidden_grad = lax.psum_scatter(terms, "filt", scatter_dimension=0, tiled=True)
    grad_first = jnp.where(pre_first > 0, hidden_grad, 0.0).astype(jnp.bfloat16)
    second_local = weight_terms(grad_second, padded_hidden, count)
    first_local = weight_terms(grad_first, padded_in, count)
    first_grad, second_grad = lax.psum((first_local, second_local), "rows")
    return (block_out, first_grad, second_grad)


def solution(mesh):
    in_specs = (
        P("filt", "rows", None),
        P("filt", None, None, None),
        P("filt", None, None, None),
        P("filt", "rows", None),
    )
    out_specs = (P("filt", "rows", None), P("filt", None, None, None), P("filt", None, None, None))
    return jax.shard_map(
        per_device, mesh=mesh, in_specs=in_specs, out_specs=out_specs, check_vma=False
    )
```

profile of v0, /device:TPU:6, one launch (start us, length us, event | category | flops | bytes accessed | tf_op | source)
XLA Modules:
  0.0 543.6 jit_solution(2598938622587336115)
XLA Ops:
  7.2 4.0 collective-permute-start
  11.2 1.3 collective-permute-start.1
  12.5 0.6 collective-permute-done
  13.1 4.1 collective-permute-done.1
  17.2 1.4 pad_maximum_fusion.2
  18.7 66.2 %all-gather.3.cloned.1.call-done = bf16[512,3,512]{2,0,1:T(8,128)(2,1)} async-done(((bf16[32,3,512]{2,0,1:T(8,128)(2,1)}), bf16[512,3,512]{2,0,1:T(8,128)(2,1)}) %all-gather.3.cloned.1.call-update) | async-done | bytes 1572880 | tf_op jit(solution)/shard_map/all_gather | solution.py:83
  84.9 1.4 convolution_bitcast_fusion.24
  86.3 1.3 convolution_bitcast_fusion.21
  87.7 1.2 convolution_bitcast_fusion.18
  89.2 0.2 convolution_bitcast_fusion.26
  89.4 0.2 convolution_bitcast_fusion.20
  89.6 0.2 fusion.9
  89.8 0.2 fusion.11
  90.0 0.8 maximum_convert_fusion.1
  90.9 3.4 collective-permute-start.2
  94.3 1.3 collective-permute-start.3
  95.6 0.3 collective-permute-done.2
  95.9 4.2 collective-permute-done.3
  100.1 0.7 pad_maximum_fusion.3
  100.9 61.3 %all-gather.5.cloned.1.call-done = bf16[512,3,512]{2,0,1:T(8,128)(2,1)} async-done(((bf16[32,3,512]{2,0,1:T(8,128)(2,1)}), bf16[512,3,512]{2,0,1:T(8,128)(2,1)}) %all-gather.5.cloned.1.call-update) | async-done | bytes 1572880 | tf_op jit(solution)/shard_map/all_gather | solution.py:83
  162.2 1.3 convolution_bitcast_fusion.15
  163.6 1.2 convolution_bitcast_fusion.12
  164.9 1.2 convolution_bitcast_fusion.9
  166.9 0.2 fusion.14
  167.3 0.8 maximum_convert_fusion
  168.2 1.3 collective-permute-start.4
  169.5 4.5 collective-permute-start.5
  174.1 0.3 convolution_bitcast_fusion.5
  174.4 0.3 convolution_bitcast_fusion.3
  174.8 0.3 convolution_bitcast_fusion.4
  175.1 0.3 slice.251
  175.5 0.3 convolution_bitcast_fusion.8
  175.8 0.3 slice.249
  176.1 0.3 convolution_bitcast_fusion.2
  176.5 0.3 slice.253
  176.8 0.3 convolution_bitcast_fusion
  177.2 0.3 convolution_bitcast_fusion.6
  177.5 0.3 convolution_bitcast_fusion.7
  177.9 2.0 fusion.1
  180.0 0.2 convolution_bitcast_fusion.27
  180.2 0.3 convolution_bitcast_fusion.29
  180.5 0.3 convolution_bitcast_fusion.28
  180.8 0.2 convolution_bitcast_fusion.30
  181.0 0.3 convolution_bitcast_fusion.32
  181.3 0.3 convolution_bitcast_fusion.33
  181.6 0.3 convolution_bitcast_fusion.35
  181.8 0.3 convolution_bitcast_fusion.31
  182.1 0.3 convolution_bitcast_fusion.34
  182.4 0.9 pad_maximum_fusion.1
  183.3 87.1 %reduce-scatter.2.cloned.1.call-done = f32[32,1,512]{2,0,1:T(8,128)} async-done(((f32[512,1,512]{2,0,1:T(8,128)}), f32[32,1,512]{2,0,1:T(8,128)}) %reduce-scatter.2.cloned.1.call-update) | async-done | bytes 65552 | tf_op jit(solution)/shard_map/reduce_scatter | solution.py:97
  270.4 0.8 select_convert_fusion
  271.3 0.2 convolution_bitcast_fusion.37
  271.5 0.3 convolution_bitcast_fusion.38
  271.8 0.3 convolution_bitcast_fusion.36
  272.1 0.2 convolution_bitcast_fusion.39
  272.3 0.3 convolution_bitcast_fusion.41
  272.6 0.3 convolution_bitcast_fusion.42
  272.9 0.3 convolution_bitcast_fusion.44
  273.2 0.3 convolution_bitcast_fusion.40
  273.4 0.3 convolution_bitcast_fusion.43
  273.8 0.9 pad_maximum_fusion
  274.6 259.6 %all-reduce.25.cloned.1.call-done = (f32[32,3,3,512]{3,0,2,1:T(8,128)}, f32[32,3,3,512]{3,0,2,1:T(8,128)}) async-done(((f32[32,3,3,512]{3,0,2,1:T(8,128)}, f32[32,3,3,512]{3,0,2,1:T(8,128)}), (f32[32,3,3,512]{3,0,2,1:T(8,128)}, f32[32,3,3,512]{3,0,2,1:T(8,128)})) %all-reduce.25.cloned.1.call-update) | async-done | bytes 1179664 | tf_op jit(solution)/shard_map/psum | solution.py:101
  534.3 2.0 copy.27
  536.2 0.8 copy.28
  (44 shorter events, 2.1 us)
Async XLA Ops:
  7.2 80.5 %copy-start.4 = (bf16[32,3,3,512]{3,0,2,1:T(8,128)(2,1)S(1)}, bf16[32,3,3,512]{3,0,2,1:T(8,128)(2,1)}, u32[]{:S(2)}) copy-start(bf16[32,3,3,512]{3,0,2,1:T(8,128)(2,1)} %param.5) | copy-start | bytes 884740
  7.2 77.7 %all-gather.3.cloned.1.call-start = ((), (), s32[]{:S(2)}) async-start(), calls=%async_computation.1 | async-start | bytes 1671168 | tf_op jit(solution)/shard_map/all_gather | solution.py:83
  7.2 5.9 %collective-permute-start = (bf16[32,1,512]{2,0,1:T(8,128)(2,1)}, bf16[32,1,512]{2,0,1:T(8,128)(2,1)S(1)}, u32[]{:S(2)}, u32[]{:S(2)}) collective-permute-start(bf16[32,1,512]{2,0,1:T(8,128)(2,1)} %param.4), channel_id=1, source_target_pairs={{0,16},{16,32},{32,48},{48,64},{64,80},{80,96},{96,112},{112,128},... | collective-permute-start | bytes 98312 | tf_op jit(solution)/shard_map/ppermute | solution.py:15
  11.2 6.0 %collective-permute-start.1 = (bf16[32,1,512]{2,0,1:T(8,128)(2,1)}, bf16[32,1,512]{2,0,1:T(8,128)(2,1)S(1)}, u32[]{:S(2)}, u32[]{:S(2)}) collective-permute-start(bf16[32,1,512]{2,0,1:T(8,128)(2,1)} %param.4), channel_id=1, source_target_pairs={{16,0},{32,16},{48,32},{64,48},{80,64},{96,80},{112,96},{128,112},... | collective-permute-start | bytes 98312 | tf_op jit(solution)/shard_map/ppermute | solution.py:17
  18.6 143.5 %all-gather.5.cloned.1.call-start = ((), (), s32[]{:S(2)}) async-start(), calls=%async_computation.2 | async-start | bytes 1671168 | tf_op jit(solution)/shard_map/all_gather | solution.py:83
  84.9 4.1 copy-start
  89.4 72.8 %copy-start.2 = (bf16[32,3,3,512]{3,0,2,1:T(8,128)(2,1)S(1)}, bf16[32,3,3,512]{3,0,2,1:T(8,128)(2,1)}, u32[]{:S(2)}) copy-start(bf16[32,3,3,512]{3,0,2,1:T(8,128)(2,1)} %param.6) | copy-start | bytes 884740
  90.9 5.0 collective-permute-start.2
  94.3 5.8 %collective-permute-start.3 = (bf16[32,1,512]{2,0,1:T(8,128)(2,1)S(1)}, bf16[32,1,512]{2,0,1:T(8,128)(2,1)S(1)}, u32[]{:S(2)}, u32[]{:S(2)}) collective-permute-start(bf16[32,1,512]{2,0,1:T(8,128)(2,1)S(1)} %get-tuple-element.9), channel_id=1, source_target_pairs={{16,0},{32,16},{48,32},{64,48},{80,64},{96,80},{112,96},{128,112},... | collective-permute-start | bytes 98312 | tf_op jit(solution)/shard_map/ppermute | solution.py:17
  100.8 169.5 %reduce-scatter.2.cloned.1.call-start = ((), (), s32[]{:S(2)}) async-start(), calls=%async_computation.3 | async-start | bytes 1114112 | tf_op jit(solution)/shard_map/reduce_scatter | solution.py:97
  162.2 4.1 copy-start.1
  166.5 0.8 copy-start.6
  166.7 1.5 copy-start.7
  168.2 7.2 %collective-permute-start.4 = (bf16[32,1,512]{2,0,1:T(8,128)(2,1)S(1)}, bf16[32,1,512]{2,0,1:T(8,128)(2,1)S(1)}, u32[]{:S(2)}, u32[]{:S(2)}) collective-permute-start(bf16[32,1,512]{2,0,1:T(8,128)(2,1)S(1)} %select_convert_fusion.1), channel_id=1, source_target_pairs={{16,0},{32,16},{48,32},{64,48},{80,64},{96,80},{112,96},{128,112},... | collective-permute-start | bytes 98312 | tf_op jit(solution)/shard_map/ppermute | solution.py:17
  169.5 6.6 %collective-permute-start.5 = (bf16[32,1,512]{2,0,1:T(8,128)(2,1)S(1)}, bf16[32,1,512]{2,0,1:T(8,128)(2,1)S(1)}, u32[]{:S(2)}, u32[]{:S(2)}) collective-permute-start(bf16[32,1,512]{2,0,1:T(8,128)(2,1)S(1)} %select_convert_fusion.1), channel_id=1, source_target_pairs={{0,16},{16,32},{32,48},{48,64},{64,80},{80,96},{96,112},{112,128},... | collective-permute-start | bytes 98312 | tf_op jit(solution)/shard_map/ppermute | solution.py:15
  179.9 354.3 %all-reduce.25.cloned.1.call-start = ((), (), s32[]{:S(2)}) async-start(), calls=%async_computation.4 | async-start | bytes 2359296 | tf_op jit(solution)/shard_map/psum | solution.py:101
  181.8 88.5 %copy-start.5 = (f32[32,1,512]{2,0,1:T(8,128)S(1)}, f32[32,1,512]{2,0,1:T(8,128)}, u32[]{:S(2)}) copy-start(f32[32,1,512]{2,0,1:T(8,128)} %get-tuple-element.10) | copy-start | bytes 196612
  534.3 2.0 copy-start.3
Sparse Core Ops, SparseCore 0:
  18.8 66.0 all-gather.2
  100.9 61.2 all-gather.4
  180.0 90.2 reduce-scatter.1
  274.8 259.4 all-reduce.24
where the time goes:
time: 544 us
  waiting for transfers between devices  483 us (89%)
  matrix products  20.8 us (4%)
  starting transfers between devices  16 us (3%)
  between operations  14 us (3%)
    psum x1, waiting for transfers between devices, per_device(): first_grad, second_grad = lax.psum((first_local, second_local), 'rows')  260 us
    all_gather x2, waiting for transfers between devices, all_channels(): return lax.all_gather(with_rims(value), 'filt', axis=0, tiled=True)  128 us
    reduce_scatter x1, waiting for transfers between devices, per_device(): lax.psum_scatter(terms, 'filt', scatter_dimension=0, tiled=True)  87.1 us
    ppermute x3, starting transfers between devices, extended(): lax.ppermute(tail, axis, [(i, (i + 1) % count) for i in range(ends)])  12 us
    dot_general x18, matrix products, conv_forward(): jnp.einsum('oi,ihw->ohw', weight[:, a, b, :], padded[:, a:a + count, :],...  11.3 us
  transfers between devices with their start and end apart: 10, of which 8 were waited for; matrix products, arithmetic and copies ran while one was open for 1% of the time, Pallas kernels for 0%

commit v1 on v0

v1 whole, which is shorter than its diff:
```python
import jax
import jax.numpy as jnp
from jax import lax
from jax.sharding import PartitionSpec as P


def shift_cols(value, offset):
    if offset == 0:
        return value
    pad = [(0, 0)] * (value.ndim - 1)
    if offset > 0:
        return jnp.pad(value[..., offset:], pad + [(0, offset)])
    return jnp.pad(value[..., :offset], pad + [(-offset, 0)])


def from_prev(value):
    count = lax.axis_size("rows")
    return lax.ppermute(value, "rows", [(i, i + 1) for i in range(count - 1)])


def from_next(value):
    count = lax.axis_size("rows")
    return lax.ppermute(value, "rows", [(i + 1, i) for i in range(count - 1)])


def conv_row(weight, row):
    o = weight.shape[0]
    flat = weight.reshape(o, 9, weight.shape[3])
    parts = jnp.einsum("oki,iw->kow", flat, row, preferred_element_type=jnp.float32)
    return [sum(shift_cols(parts[a * 3 + b], b - 1) for b in range(3)) for a in range(3)]


def conv_forward(weight, row):
    p0, p1, p2 = conv_row(weight, row)
    return p1 + from_prev(p0) + from_next(p2)


def grad_rows(grad):
    return jnp.stack([from_next(grad), grad, from_prev(grad)])


def weight_terms(rows3, full_row):
    cols = []
    for b in range(3):
        moved = shift_cols(rows3, 1 - b)
        cols.append(jnp.einsum("aow,iw->oai", moved, full_row, preferred_element_type=jnp.float32))
    return jnp.stack(cols, axis=2)


def hidden_terms(weight, rows3):
    total = None
    for b in range(3):
        part = jnp.einsum("oai,aow->iw", weight[:, :, b, :], rows3, preferred_element_type=jnp.float32)
        part = shift_cols(part, 1 - b)
        total = part if total is None else total + part
    return total


def per_device(features, first_weight, second_weight, out_grad):
    feat = features[:, 0, :]
    og = out_grad[:, 0, :]
    x_row = lax.all_gather(feat, "filt", axis=0, tiled=True)
    pre_first = conv_forward(first_weight, x_row)
    hidden = jnp.maximum(pre_first, 0.0).astype(jnp.bfloat16)
    h_row = lax.all_gather(hidden, "filt", axis=0, tiled=True)
    pre_second = conv_forward(second_weight, h_row) + feat.astype(jnp.float32)
    block_out = jnp.maximum(pre_second, 0.0).astype(jnp.bfloat16)
    grad_second = jnp.where(pre_second > 0, og.astype(jnp.float32), 0.0).astype(jnp.bfloat16)
    gs3 = grad_rows(grad_second)
    terms = hidden_terms(second_weight, gs3)
    hidden_grad = lax.psum_scatter(terms, "filt", scatter_dimension=0, tiled=True)
    grad_first = jnp.where(pre_first > 0, hidden_grad, 0.0).astype(jnp.bfloat16)
    gf3 = grad_rows(grad_first)
    second_local = weight_terms(gs3, h_row)
    first_local = weight_terms(gf3, x_row)
    first_grad, second_grad = lax.psum((first_local, second_local), "rows")
    return (block_out[:, None, :], first_grad, second_grad)


def solution(mesh):
    in_specs = (
        P("filt", "rows", None),
        P("filt", None, None, None),
        P("filt", None, None, None),
        P("filt", "rows", None),
    )
    out_specs = (P("filt", "rows", None), P("filt", None, None, None), P("filt", None, None, None))
    return jax.shard_map(
        per_device, mesh=mesh, in_specs=in_specs, out_specs=out_specs, check_vma=False
    )
```

time: 544 us -> 461 us (0.85)
  waiting for transfers between devices: 483 us -> 368 us
  blocking collectives: 0 us -> 43.3 us
  matrix products: 20.8 us -> 4.49 us
  starting transfers between devices: 16 us -> 22.5 us
    all_gather x2 -> x0, waiting for transfers between devices: 128 us -> none  [all_channels(): return lax.all_gather(with_rims(value), 'filt', axis=0, tiled=True)]
    all_gather x0 -> x2, blocking collectives: none -> 43.3 us  [the longest x1 22.3 us: per_device(): x_row = lax.all_gather(feat, 'filt', axis=0, tiled=True)]
    dot_general x45 -> x11, matrix products: 20.8 us -> 4.49 us  [the longest x3 2.1 us: hidden_terms(): jnp.einsum('oai,aow->iw', weight[:, :, b, :], rows3, preferred_element_ty...]
    reduce_scatter x1, waiting for transfers between devices: 87.1 us -> 97.5 us  [per_device(): lax.psum_scatter(terms, 'filt', scatter_dimension=0, tiled=True)]
    ppermute x6 -> x8, starting transfers between devices: 15.8 us -> 22.4 us  [the longest x4 17.3 us: from_prev(): return lax.ppermute(value, 'rows', [(i, i + 1) for i in range(count - 1)])]
    ppermute x6 -> x8, waiting for transfers between devices: 9.23 us -> 11.9 us  [the longest x4 8.87 us: from_next(): return lax.ppermute(value, 'rows', [(i + 1, i) for i in range(count - 1)])]
  transfers between devices with their start and end apart: 10 -> 10, of which waited for: 8 -> 9; matrix products, arithmetic and copies ran while one was open for 1% -> 1% of each run, Pallas kernels for 0% -> 0%
where the time goes in v1:
time: 461 us; the launch traced here: 460 us
  waiting for transfers between devices  368 us (80%)
  blocking collectives  43.3 us (9%)
  starting transfers between devices  22.5 us (5%)
  between operations  14.3 us (3%)
    psum x1, waiting for transfers between devices, per_device(): first_grad, second_grad = lax.psum((first_local, second_local), 'rows')  259 us
    reduce_scatter x1, waiting for transfers between devices, per_device(): lax.psum_scatter(terms, 'filt', scatter_dimension=0, tiled=True)  97.5 us
    all_gather x1, blocking collectives, per_device(): x_row = lax.all_gather(feat, 'filt', axis=0, tiled=True)  22.3 us
    all_gather x1, blocking collectives, per_device(): h_row = lax.all_gather(hidden, 'filt', axis=0, tiled=True)  20.9 us
    ppermute x4, starting transfers between devices, from_prev(): return lax.ppermute(value, 'rows', [(i, i + 1) for i in range(count - 1)])  17.3 us
  transfers between devices with their start and end apart: 10, of which 9 were waited for; matrix products, arithmetic and copies ran while one was open for 1% of the time, Pallas kernels for 0%

profile of v1, /device:TPU:6, one launch (start us, length us, event | category | flops | bytes accessed | tf_op | source)
XLA Modules:
  0.0 460.3 jit_solution(7706754737106029447)
XLA Ops:
  7.2 0.0 copy-start
  7.2 0.0 reduce-scatter.2.cloned.1.call-start
  7.2 22.3 %all-gather = bf16[512,1,512]{2,0,1:T(8,128)(2,1)S(1)} all-gather(bf16[32,1,512]{2,0,1:T(8,128)(2,1)} %param.4), channel_id=2, replica_groups=mesh['rows'=32,'filt'=16] {'filt'}, dimensions={0}, use_global_device_ids=true | all-gather | bytes 557056 | tf_op jit(solution)/shard_map/all_gather | solution.py:62
  29.6 0.0 copy-done
  29.6 0.3 convolution_bitcast_fusion.4
  29.9 0.1 slice.165
  30.0 0.1 slice.170
  30.1 0.1 fusion.32
  30.2 1.3 collective-permute-start.1
  31.5 4.5 collective-permute-start
  36.1 0.1 slice.160
  36.1 0.3 collective-permute-done.1
  36.5 1.5 collective-permute-done
  38.0 0.1 maximum_convert_fusion.1
  38.1 0.0 copy-start.2
  38.1 20.9 %all_gather.7 = bf16[512,512]{1,0:T(8,128)(2,1)S(1)} all-gather(bf16[32,512]{1,0:T(8,128)(2,1)S(1)} %get-tuple-element.10), channel_id=1, replica_groups=mesh['rows'=32,'filt'=16] {'filt'}, dimensions={0}, use_global_device_ids=true | all-gather | bytes 557056 | tf_op jit(solution)/shard_map/all_gather | solution.py:65
  59.0 0.0 copy-done.2
  59.0 0.3 convolution_bitcast_fusion.3
  59.3 0.1 slice.180
  59.4 0.1 slice.185
  59.5 0.1 fusion.23
  59.6 1.3 collective-permute-start.3
  60.9 4.9 %collective-permute-start.2 = (f32[32,512]{1,0:T(8,128)S(1)}, f32[32,512]{1,0:T(8,128)S(1)}, u32[]{:S(2)}, u32[]{:S(2)}) collective-permute-start(f32[32,512]{1,0:T(8,128)S(1)} %get-tuple-element.18), channel_id=1, source_target_pairs={{0,16},{16,32},{32,48},{48,64},{64,80},{80,96},{96,112},{112,128},... | collective-permute-start | bytes 196616 | tf_op jit(solution)/shard_map/ppermute | solution.py:18
  65.8 0.0 copy-start.3
  65.8 0.0 copy-start.4
  65.9 0.1 slice.175
  65.9 0.6 collective-permute-done.3
  66.5 1.2 collective-permute-done.2
  67.7 0.0 copy-done.3
  67.7 0.0 copy-done.4
  67.7 0.1 fusion.37
  67.8 4.3 collective-permute-start.5
  72.2 1.3 collective-permute-start.4
  73.5 0.3 collective-permute-done.5
  73.8 4.4 collective-permute-done.4
  78.1 0.3 convolution_bitcast_fusion
  78.5 0.3 convolution_bitcast_fusion.2
  78.8 0.3 slice.186
  79.2 1.4 fusion.1
  80.6 0.0 reduce-scatter.2.cloned.1.call-update
  80.6 0.0 all-reduce.21.cloned.1.call-start
  80.7 0.1 fusion.45
  80.8 0.3 convolution_bitcast_fusion.5
  81.1 0.3 convolution_bitcast_fusion.7
  81.4 0.3 convolution_bitcast_fusion.6
  81.7 97.5 %reduce-scatter.2.cloned.1.call-done = f32[32,512]{1,0:T(8,128)} async-done(((f32[512,512]{1,0:T(8,128)}), f32[32,512]{1,0:T(8,128)}) %reduce-scatter.2.cloned.1.call-update) | async-done | bytes 65552 | tf_op jit(solution)/shard_map/reduce_scatter | solution.py:71
  179.2 0.8 select_convert_fusion
  180.0 3.5 collective-permute-start.7
  183.5 1.3 collective-permute-start.6
  184.8 0.9 pad_maximum_fusion.1
  185.6 0.0 collective-permute-done.7
  185.7 3.6 collective-permute-done.6
  189.3 0.3 convolution_bitcast_fusion.9
  189.6 0.1 fusion.46
  189.7 0.3 convolution_bitcast_fusion.8
  190.0 0.3 convolution_bitcast_fusion.10
  190.3 0.9 pad_maximum_fusion
  191.2 0.0 all-reduce.21.cloned.1.call-update
  191.2 0.6 fusion.38
  191.8 258.8 %all-reduce.21.cloned.1.call-done = (f32[32,3,3,512]{3,0,1,2:T(8,128)}, f32[32,3,3,512]{3,0,1,2:T(8,128)}) async-done(((f32[32,3,3,512]{3,0,1,2:T(8,128)}, f32[32,3,3,512]{3,0,1,2:T(8,128)}), (f32[32,3,3,512]{3,0,1,2:T(8,128)}, f32[32,3,3,512]{3,0,1,2:T(8,128)})) %all-reduce.21.cloned.1.call-update) | async-done | bytes 1179664 | tf_op jit(solution)/shard_map/psum | solution.py:76
  450.6 0.0 copy-start.1
  450.6 2.0 copy.13
  452.6 0.0 copy-done.1
  452.6 0.9 copy.14
  (4 shorter events, 0.1 us)
Async XLA Ops:
  7.2 22.4 %copy-start = (bf16[32,3,3,512]{3,0,2,1:T(8,128)(2,1)S(1)}, bf16[32,3,3,512]{3,0,2,1:T(8,128)(2,1)}, u32[]{:S(2)}) copy-start(bf16[32,3,3,512]{3,0,2,1:T(8,128)(2,1)} %param.5) | copy-start | bytes 884740
  7.2 172.0 %reduce-scatter.2.cloned.1.call-start = ((), (), s32[]{:S(2)}) async-start(), calls=%async_computation.1 | async-start | bytes 1114112 | tf_op jit(solution)/shard_map/reduce_scatter | solution.py:71
  30.2 6.2 %collective-permute-start.1 = (f32[32,512]{1,0:T(8,128)S(1)}, f32[32,512]{1,0:T(8,128)S(1)}, u32[]{:S(2)}, u32[]{:S(2)}) collective-permute-start(f32[32,512]{1,0:T(8,128)S(1)} %get-tuple-element.27), channel_id=1, source_target_pairs={{16,0},{32,16},{48,32},{64,48},{80,64},{96,80},{112,96},{128,112},... | collective-permute-start | bytes 196616 | tf_op jit(solution)/shard_map/ppermute | solution.py:23
  31.5 6.4 %collective-permute-start = (f32[32,512]{1,0:T(8,128)S(1)}, f32[32,512]{1,0:T(8,128)S(1)}, u32[]{:S(2)}, u32[]{:S(2)}) collective-permute-start(f32[32,512]{1,0:T(8,128)S(1)} %get-tuple-element.26), channel_id=1, source_target_pairs={{0,16},{16,32},{32,48},{48,64},{64,80},{80,96},{96,112},{112,128},... | collective-permute-start | bytes 196616 | tf_op jit(solution)/shard_map/ppermute | solution.py:18
  38.1 20.9 %copy-start.2 = (bf16[32,3,3,512]{3,0,2,1:T(8,128)(2,1)S(1)}, bf16[32,3,3,512]{3,0,2,1:T(8,128)(2,1)}, u32[]{:S(2)}) copy-start(bf16[32,3,3,512]{3,0,2,1:T(8,128)(2,1)} %param.6) | copy-start | bytes 884740
  59.6 6.9 %collective-permute-start.3 = (f32[32,512]{1,0:T(8,128)S(1)}, f32[32,512]{1,0:T(8,128)S(1)}, u32[]{:S(2)}, u32[]{:S(2)}) collective-permute-start(f32[32,512]{1,0:T(8,128)S(1)} %get-tuple-element.19), channel_id=1, source_target_pairs={{16,0},{32,16},{48,32},{64,48},{80,64},{96,80},{112,96},{128,112},... | collective-permute-start | bytes 196616 | tf_op jit(solution)/shard_map/ppermute | solution.py:23
  60.9 6.8 %collective-permute-start.2 = (f32[32,512]{1,0:T(8,128)S(1)}, f32[32,512]{1,0:T(8,128)S(1)}, u32[]{:S(2)}, u32[]{:S(2)}) collective-permute-start(f32[32,512]{1,0:T(8,128)S(1)} %get-tuple-element.18), channel_id=1, source_target_pairs={{0,16},{16,32},{32,48},{48,64},{64,80},{80,96},{96,112},{112,128},... | collective-permute-start | bytes 196616 | tf_op jit(solution)/shard_map/ppermute | solution.py:18
  65.8 1.9 copy-start.3
  65.8 1.9 copy-start.4
  67.8 5.9 %collective-permute-start.5 = (bf16[32,512]{1,0:T(8,128)(2,1)S(1)}, bf16[32,512]{1,0:T(8,128)(2,1)S(1)}, u32[]{:S(2)}, u32[]{:S(2)}) collective-permute-start(bf16[32,512]{1,0:T(8,128)(2,1)S(1)} %get-tuple-element.8), channel_id=1, source_target_pairs={{0,16},{16,32},{32,48},{48,64},{64,80},{80,96},{96,112},{112,128},... | collective-permute-start | bytes 98312 | tf_op jit(solution)/shard_map/ppermute | solution.py:18
  72.2 6.0 %collective-permute-start.4 = (bf16[32,512]{1,0:T(8,128)(2,1)S(1)}, bf16[32,512]{1,0:T(8,128)(2,1)S(1)}, u32[]{:S(2)}, u32[]{:S(2)}) collective-permute-start(bf16[32,512]{1,0:T(8,128)(2,1)S(1)} %get-tuple-element.8), channel_id=1, source_target_pairs={{16,0},{32,16},{48,32},{64,48},{80,64},{96,80},{112,96},{128,112},... | collective-permute-start | bytes 98312 | tf_op jit(solution)/shard_map/ppermute | solution.py:23
  80.6 370.0 %all-reduce.21.cloned.1.call-start = ((), (), s32[]{:S(2)}) async-start(), calls=%async_computation.2 | async-start | bytes 2359296 | tf_op jit(solution)/shard_map/psum | solution.py:76
  180.0 5.6 %collective-permute-start.7 = (bf16[32,512]{1,0:T(8,128)(2,1)S(1)}, bf16[32,512]{1,0:T(8,128)(2,1)S(1)}, u32[]{:S(2)}, u32[]{:S(2)}) collective-permute-start(bf16[32,512]{1,0:T(8,128)(2,1)S(1)} %select_convert_fusion), channel_id=1, source_target_pairs={{0,16},{16,32},{32,48},{48,64},{64,80},{80,96},{96,112},{112,128},... | collective-permute-start | bytes 98312 | tf_op jit(solution)/shard_map/ppermute | solution.py:18
  183.5 5.8 %collective-permute-start.6 = (bf16[32,512]{1,0:T(8,128)(2,1)S(1)}, bf16[32,512]{1,0:T(8,128)(2,1)S(1)}, u32[]{:S(2)}, u32[]{:S(2)}) collective-permute-start(bf16[32,512]{1,0:T(8,128)(2,1)S(1)} %select_convert_fusion), channel_id=1, source_target_pairs={{16,0},{32,16},{48,32},{64,48},{80,64},{96,80},{112,96},{128,112},... | collective-permute-start | bytes 98312 | tf_op jit(solution)/shard_map/ppermute | solution.py:23
  450.6 2.0 copy-start.1
Sparse Core Ops, SparseCore 0:
  80.7 98.3 reduce-scatter.1
  191.3 259.2 all-reduce.20

commit v2 on v1

--- a/solution.py
+++ b/solution.py
@@ -1,7 +1,113 @@
+import functools
+
 import jax
 import jax.numpy as jnp
 from jax import lax
+from jax.experimental import pallas as pl
+from jax.experimental.pallas import tpu as pltpu
 from jax.sharding import PartitionSpec as P
+
+MESH = pl.DeviceIdType.MESH
+
+
+def peer_id(axis, j):
+    if axis == "rows":
+        return (j, lax.axis_index("filt"))
+    return (lax.axis_index("rows"), j)
+
+
+def exchange_kernel(axis, n, mode, *refs):
+    me = lax.axis_index(axis)
+
+    def each_peer(body):
+        def step(k, carry):
+            body(lax.rem(me + k, n), lax.rem(me + n - k, n))
+            return carry
+
+        lax.fori_loop(1, n, step, 0)
+
+    barrier = pltpu.get_barrier_semaphore()
+
+    def greet(j, s):
+        pl.semaphore_signal(barrier, 1, device_id=peer_id(axis, j), device_id_type=MESH)
+
+    each_peer(greet)
+    pl.semaphore_wait(barrier, n - 1)
+
+    def gather(src, out_ref, send, recv):
+        def copy(j, s):
+            return pltpu.make_async_remote_copy(
+                src, out_ref.at[me], send.at[j], recv.at[me], device_id=peer_id(axis, j), device_id_type=MESH
+            )
+
+        def incoming(j, s):
+            return pltpu.make_async_remote_copy(
+                src, out_ref.at[s], send.at[s], recv.at[s], device_id=peer_id(axis, s), device_id_type=MESH
+            )
+
+        each_peer(lambda j, s: copy(j, s).start())
+        return copy, incoming
+
+    def reduce(x_ref, buf, send, recv):
+        def copy(j, s):
+            return pltpu.make_async_remote_copy(
+                x_ref.at[j], buf.at[me], send.at[j], recv.at[me], device_id=peer_id(axis, j), device_id_type=MESH
+            )
+
+        def incoming(j, s):
+            return pltpu.make_async_remote_copy(
+                x_ref.at[s], buf.at[s], send.at[s], recv.at[s], device_id=peer_id(axis, s), device_id_type=MESH
+            )
+
+        each_peer(lambda j, s: copy(j, s).start())
+        each_peer(lambda j, s: incoming(j, s).wait_recv())
+        acc = x_ref[me].astype(jnp.float32)
+
+        def add(k, acc):
+            return acc + buf[lax.rem(me + k, n)].astype(jnp.float32)
+
+        acc = lax.fori_loop(1, n, add, acc)
+        each_peer(lambda j, s: copy(j, s).wait_send())
+        return acc
+
+    if mode == "ag":
+        x_ref, out_ref, send, recv = refs
+        copy, incoming = gather(x_ref, out_ref, send, recv)
+        out_ref[me] = x_ref[...]
+        each_peer(lambda j, s: incoming(j, s).wait_recv())
+        each_peer(lambda j, s: copy(j, s).wait_send())
+    elif mode == "rs":
+        x_ref, out_ref, buf, send, recv = refs
+        out_ref[...] = reduce(x_ref, buf, send, recv).astype(out_ref.dtype)
+    else:
+        x_ref, out_ref, buf, send, recv, send2, recv2 = refs
+        out_ref[me] = reduce(x_ref, buf, send, recv).astype(out_ref.dtype)
+        copy, incoming = gather(out_ref.at[me], out_ref, send2, recv2)
+        each_peer(lambda j, s: incoming(j, s).wait_recv())
+        each_peer(lambda j, s: copy(j, s).wait_send())
+
+
+def exchange(x, axis, mode, collective_id, out_dtype=None):
+    n = lax.axis_size(axis)
+    out_dtype = out_dtype or x.dtype
+    sems = [pltpu.SemaphoreType.DMA((n,)), pltpu.SemaphoreType.DMA((n,))]
+    if mode == "ag":
+        out_shape = (n,) + x.shape
+        scratch = sems
+    elif mode == "rs":
+        out_shape = x.shape[1:]
+        scratch = [pltpu.VMEM(x.shape, x.dtype)] + sems
+    else:
+        out_shape = x.shape
+        scratch = [pltpu.VMEM(x.shape, x.dtype)] + sems + sems
+    return pl.pallas_call(
+        functools.partial(exchange_kernel, axis, n, mode),
+        out_shape=jax.ShapeDtypeStruct(out_shape, out_dtype),
+        in_specs=[pl.BlockSpec(memory_space=pltpu.VMEM)],
+        out_specs=pl.BlockSpec(memory_space=pltpu.VMEM),
+        scratch_shapes=scratch,
+        compiler_params=pltpu.CompilerParams(collective_id=collective_id, has_side_effects=True),
+    )(x)
 
 
 def shift_cols(value, offset):
@@ -73,7 +179,10 @@
     gf3 = grad_rows(grad_first)
     second_local = weight_terms(gs3, h_row)
     first_local = weight_terms(gf3, x_row)
-    first_grad, second_grad = lax.psum((first_local, second_local), "rows")
+    both = jnp.stack([first_local, second_local])
+    n_rows = lax.axis_size("rows")
+    summed = exchange(both.reshape(n_rows, -1, 128), "rows", "ar", 0)
+    first_grad, second_grad = summed.reshape(both.shape)
     return (block_out[:, None, :], first_grad, second_grad)
 
 

time: 461 us -> 322 us (0.70)
  waiting for transfers between devices: 368 us -> 108 us
  Pallas kernels: 0 us -> 120 us
    psum x1 -> x0, waiting for transfers between devices: 259 us -> none  [per_device(): first_grad, second_grad = lax.psum((first_local, second_local), 'rows')]
    pallas_call x0 -> x1, Pallas kernels: none -> 120 us  [exchange(): pl.pallas_call(functools.partial(exchange_kernel, axis, n, mode), out_sha...]
  transfers between devices with their start and end apart: 10 -> 9, of which waited for: 9 -> 7; matrix products, arithmetic and copies ran while one was open for 1% -> 1% of each run, Pallas kernels for 0% -> 0%
where the time goes in v2:
time: 322 us
  Pallas kernels  120 us (37%)
  waiting for transfers between devices  108 us (34%)
  blocking collectives  45.2 us (14%)
  starting transfers between devices  21 us (7%)
  between operations  14.3 us (4%)
  local copies, waits for them, and re-layouts  7.19 us (2%)
  matrix products  4.48 us (1%)
    pallas_call x1, Pallas kernels, exchange(): pl.pallas_call(functools.partial(exchange_kernel, axis, n, mode), out_sha...  120 us
    reduce_scatter x1, waiting for transfers between devices, per_device(): lax.psum_scatter(terms, 'filt', scatter_dimension=0, tiled=True)  93.9 us
    all_gather x1, blocking collectives, per_device(): h_row = lax.all_gather(hidden, 'filt', axis=0, tiled=True)  22.9 us
    all_gather x1, blocking collectives, per_device(): x_row = lax.all_gather(feat, 'filt', axis=0, tiled=True)  22.3 us
    ppermute x4, starting transfers between devices, from_prev(): return lax.ppermute(value, 'rows', [(i, i + 1) for i in range(count - 1)])  15.8 us
    ppermute x4, waiting for transfers between devices, from_next(): return lax.ppermute(value, 'rows', [(i + 1, i) for i in range(count - 1)])  9.72 us
  transfers between devices with their start and end apart: 9, of which 7 were waited for; matrix products, arithmetic and copies ran while one was open for 1% of the time, Pallas kernels for 0%

profile of v2, /device:TPU:6, one launch (start us, length us, event | category | flops | bytes accessed | tf_op | source)
XLA Modules:
  0.0 321.7 jit_solution(17732111166373715138)
XLA Ops:
  7.2 0.0 copy-start
  7.2 0.0 reduce-scatter.2.cloned.1.call-start
  7.2 22.3 %all-gather = bf16[512,1,512]{2,0,1:T(8,128)(2,1)S(1)} all-gather(bf16[32,1,512]{2,0,1:T(8,128)(2,1)} %param.4), channel_id=2, replica_groups=mesh['rows'=32,'filt'=16] {'filt'}, dimensions={0}, use_global_device_ids=true | all-gather | bytes 557056 | tf_op jit(solution)/shard_map/all_gather | solution.py:168
  29.6 0.0 copy-done
  29.6 0.3 convolution_bitcast_fusion.4
  29.9 0.0 copy-start.1
  29.9 0.1 slice.167
  30.0 0.1 slice.172
  30.1 0.1 fusion.32
  30.2 1.7 collective-permute-start
  31.9 1.3 collective-permute-start.1
  33.2 0.1 slice.162
  33.3 0.5 collective-permute-done
  33.8 4.3 %collective-permute-done.1 = f32[32,512]{1,0:T(8,128)S(1)} collective-permute-done((f32[32,512]{1,0:T(8,128)S(1)}, f32[32,512]{1,0:T(8,128)S(1)}, u32[]{:S(2)}, u32[]{:S(2)}) %collective-permute-start.1) | collective-permute-done | bytes 65568 | tf_op jit(solution)/shard_map/ppermute | solution.py:129
  38.1 0.1 maximum_convert_fusion.1
  38.2 22.9 %all_gather.7 = bf16[512,512]{1,0:T(8,128)(2,1)S(1)} all-gather(bf16[32,512]{1,0:T(8,128)(2,1)S(1)} %get-tuple-element.11), channel_id=1, replica_groups=mesh['rows'=32,'filt'=16] {'filt'}, dimensions={0}, use_global_device_ids=true | all-gather | bytes 557056 | tf_op jit(solution)/shard_map/all_gather | solution.py:171
  61.1 0.0 copy-done.1
  61.1 0.3 convolution_bitcast_fusion.3
  61.4 0.0 copy-start.2
  61.4 0.0 copy-start.3
  61.5 0.1 slice.182
  61.5 0.1 slice.187
  61.6 0.1 fusion.23
  61.8 3.8 %collective-permute-start.2 = (f32[32,512]{1,0:T(8,128)S(1)}, f32[32,512]{1,0:T(8,128)S(1)}, u32[]{:S(2)}, u32[]{:S(2)}) collective-permute-start(f32[32,512]{1,0:T(8,128)S(1)} %get-tuple-element.21), channel_id=1, source_target_pairs={{0,16},{16,32},{32,48},{48,64},{64,80},{80,96},{96,112},{112,128},... | collective-permute-start | bytes 196616 | tf_op jit(solution)/shard_map/ppermute | solution.py:124
  65.6 1.3 collective-permute-start.3
  66.9 0.1 slice.177
  67.0 0.5 collective-permute-done.2
  67.5 5.4 %collective-permute-done.3 = f32[32,512]{1,0:T(8,128)S(1)} collective-permute-done((f32[32,512]{1,0:T(8,128)S(1)}, f32[32,512]{1,0:T(8,128)S(1)}, u32[]{:S(2)}, u32[]{:S(2)}) %collective-permute-start.3) | collective-permute-done | bytes 65568 | tf_op jit(solution)/shard_map/ppermute | solution.py:129
  72.9 0.0 copy-done.3
  72.9 0.1 fusion.37
  73.0 1.3 collective-permute-start.4
  74.3 5.7 %collective-permute-start.5 = (bf16[32,512]{1,0:T(8,128)(2,1)S(1)}, bf16[32,512]{1,0:T(8,128)(2,1)S(1)}, u32[]{:S(2)}, u32[]{:S(2)}) collective-permute-start(bf16[32,512]{1,0:T(8,128)(2,1)S(1)} %get-tuple-element.9), channel_id=1, source_target_pairs={{0,16},{16,32},{32,48},{48,64},{64,80},{80,96},{96,112},{112,128},... | collective-permute-start | bytes 98312 | tf_op jit(solution)/shard_map/ppermute | solution.py:124
  80.0 0.0 collective-permute-done.4
  80.0 1.6 collective-permute-done.5
  81.6 0.3 convolution_bitcast_fusion.2
  82.0 0.3 convolution_bitcast_fusion
  82.3 0.3 slice.188
  82.6 1.4 fusion.1
  84.1 0.0 reduce-scatter.2.cloned.1.call-update
  84.1 0.6 fusion.38
  84.7 0.1 fusion.47
  84.8 0.3 convolution_bitcast_fusion.7
  85.1 0.3 convolution_bitcast_fusion.5
  85.4 0.3 convolution_bitcast_fusion.6
  85.7 93.9 %reduce-scatter.2.cloned.1.call-done = f32[32,512]{1,0:T(8,128)} async-done(((f32[512,512]{1,0:T(8,128)}), f32[32,512]{1,0:T(8,128)}) %reduce-scatter.2.cloned.1.call-update) | async-done | bytes 65552 | tf_op jit(solution)/shard_map/reduce_scatter | solution.py:177
  179.6 0.8 select_convert_fusion
  180.5 1.3 collective-permute-start.6
  181.8 4.5 %collective-permute-start.7 = (bf16[32,512]{1,0:T(8,128)(2,1)S(1)}, bf16[32,512]{1,0:T(8,128)(2,1)S(1)}, u32[]{:S(2)}, u32[]{:S(2)}) collective-permute-start(bf16[32,512]{1,0:T(8,128)(2,1)S(1)} %select_convert_fusion), channel_id=1, source_target_pairs={{0,16},{16,32},{32,48},{48,64},{64,80},{80,96},{96,112},{112,128},... | collective-permute-start | bytes 98312 | tf_op jit(solution)/shard_map/ppermute | solution.py:124
  186.4 0.0 collective-permute-done.6
  186.4 1.5 collective-permute-done.7
  187.9 0.3 convolution_bitcast_fusion.9
  188.2 0.1 fusion.46
  188.3 0.3 convolution_bitcast_fusion.10
  188.6 0.3 convolution_bitcast_fusion.8
  188.9 0.1 maximum_bitcast_fusion
  189.0 0.1 pad_maximum_fusion
  189.1 0.8 copy.22
  189.9 1.5 reshape.24.refs_0_
  191.4 119.6 %shard_map.67 = f32[32,72,128]{2,1,0:T(8,128)} custom-call(f32[32,72,128]{2,1,0:T(8,128)} %reshape.24.refs_0_), custom_call_target="tpu_custom_call" | custom-call | tf_op jit(solution)/shard_map/pallas_call | solution.py:103
  311.0 1.3 fusion.45
  312.3 0.2 unstack.13
  312.6 1.0 copy.23
  313.6 0.2 unstack.15
  313.8 1.0 copy.24
  (6 shorter events, 0.1 us)
Async XLA Ops:
  7.2 22.4 %copy-start = (bf16[32,3,3,512]{3,0,2,1:T(8,128)(2,1)S(1)}, bf16[32,3,3,512]{3,0,2,1:T(8,128)(2,1)}, u32[]{:S(2)}) copy-start(bf16[32,3,3,512]{3,0,2,1:T(8,128)(2,1)} %param.5) | copy-start | bytes 884740
  7.2 172.5 %reduce-scatter.2.cloned.1.call-start = ((), (), s32[]{:S(2)}) async-start(), calls=%async_computation.1 | async-start | bytes 1114112 | tf_op jit(solution)/shard_map/reduce_scatter | solution.py:177
  29.9 31.2 %copy-start.1 = (bf16[32,3,3,512]{3,0,2,1:T(8,128)(2,1)S(1)}, bf16[32,3,3,512]{3,0,2,1:T(8,128)(2,1)}, u32[]{:S(2)}) copy-start(bf16[32,3,3,512]{3,0,2,1:T(8,128)(2,1)} %param.6) | copy-start | bytes 884740
  30.2 3.6 %collective-permute-start = (f32[32,512]{1,0:T(8,128)S(1)}, f32[32,512]{1,0:T(8,128)S(1)}, u32[]{:S(2)}, u32[]{:S(2)}) collective-permute-start(f32[32,512]{1,0:T(8,128)S(1)} %get-tuple-element.29), channel_id=1, source_target_pairs={{0,16},{16,32},{32,48},{48,64},{64,80},{80,96},{96,112},{112,128},... | collective-permute-start | bytes 196616 | tf_op jit(solution)/shard_map/ppermute | solution.py:124
  31.9 6.2 %collective-permute-start.1 = (f32[32,512]{1,0:T(8,128)S(1)}, f32[32,512]{1,0:T(8,128)S(1)}, u32[]{:S(2)}, u32[]{:S(2)}) collective-permute-start(f32[32,512]{1,0:T(8,128)S(1)} %get-tuple-element.30), channel_id=1, source_target_pairs={{16,0},{32,16},{48,32},{64,48},{80,64},{96,80},{112,96},{128,112},... | collective-permute-start | bytes 196616 | tf_op jit(solution)/shard_map/ppermute | solution.py:129
  61.4 11.5 %copy-start.2 = (bf16[32,1,512]{2,0,1:T(8,128)(2,1)S(1)}, bf16[32,1,512]{2,0,1:T(8,128)(2,1)}, u32[]{:S(2)}) copy-start(bf16[32,1,512]{2,0,1:T(8,128)(2,1)} %param.4) | copy-start | bytes 98308
  61.4 11.5 %copy-start.3 = (bf16[32,1,512]{2,0,1:T(8,128)(2,1)S(1)}, bf16[32,1,512]{2,0,1:T(8,128)(2,1)}, u32[]{:S(2)}) copy-start(bf16[32,1,512]{2,0,1:T(8,128)(2,1)} %param.7) | copy-start | bytes 98308
  61.8 5.7 %collective-permute-start.2 = (f32[32,512]{1,0:T(8,128)S(1)}, f32[32,512]{1,0:T(8,128)S(1)}, u32[]{:S(2)}, u32[]{:S(2)}) collective-permute-start(f32[32,512]{1,0:T(8,128)S(1)} %get-tuple-element.21), channel_id=1, source_target_pairs={{0,16},{16,32},{32,48},{48,64},{64,80},{80,96},{96,112},{112,128},... | collective-permute-start | bytes 196616 | tf_op jit(solution)/shard_map/ppermute | solution.py:124
  65.6 7.3 %collective-permute-start.3 = (f32[32,512]{1,0:T(8,128)S(1)}, f32[32,512]{1,0:T(8,128)S(1)}, u32[]{:S(2)}, u32[]{:S(2)}) collective-permute-start(f32[32,512]{1,0:T(8,128)S(1)} %get-tuple-element.22), channel_id=1, source_target_pairs={{16,0},{32,16},{48,32},{64,48},{80,64},{96,80},{112,96},{128,112},... | collective-permute-start | bytes 196616 | tf_op jit(solution)/shard_map/ppermute | solution.py:129
  73.0 7.0 %collective-permute-start.4 = (bf16[32,512]{1,0:T(8,128)(2,1)S(1)}, bf16[32,512]{1,0:T(8,128)(2,1)S(1)}, u32[]{:S(2)}, u32[]{:S(2)}) collective-permute-start(bf16[32,512]{1,0:T(8,128)(2,1)S(1)} %get-tuple-element.9), channel_id=1, source_target_pairs={{16,0},{32,16},{48,32},{64,48},{80,64},{96,80},{112,96},{128,112},... | collective-permute-start | bytes 98312 | tf_op jit(solution)/shard_map/ppermute | solution.py:129
  74.3 7.3 %collective-permute-start.5 = (bf16[32,512]{1,0:T(8,128)(2,1)S(1)}, bf16[32,512]{1,0:T(8,128)(2,1)S(1)}, u32[]{:S(2)}, u32[]{:S(2)}) collective-permute-start(bf16[32,512]{1,0:T(8,128)(2,1)S(1)} %get-tuple-element.9), channel_id=1, source_target_pairs={{0,16},{16,32},{32,48},{48,64},{64,80},{80,96},{96,112},{112,128},... | collective-permute-start | bytes 98312 | tf_op jit(solution)/shard_map/ppermute | solution.py:124
  180.5 5.9 %collective-permute-start.6 = (bf16[32,512]{1,0:T(8,128)(2,1)S(1)}, bf16[32,512]{1,0:T(8,128)(2,1)S(1)}, u32[]{:S(2)}, u32[]{:S(2)}) collective-permute-start(bf16[32,512]{1,0:T(8,128)(2,1)S(1)} %select_convert_fusion), channel_id=1, source_target_pairs={{16,0},{32,16},{48,32},{64,48},{80,64},{96,80},{112,96},{128,112},... | collective-permute-start | bytes 98312 | tf_op jit(solution)/shard_map/ppermute | solution.py:129
  181.8 6.1 %collective-permute-start.7 = (bf16[32,512]{1,0:T(8,128)(2,1)S(1)}, bf16[32,512]{1,0:T(8,128)(2,1)S(1)}, u32[]{:S(2)}, u32[]{:S(2)}) collective-permute-start(bf16[32,512]{1,0:T(8,128)(2,1)S(1)} %select_convert_fusion), channel_id=1, source_target_pairs={{0,16},{16,32},{32,48},{48,64},{64,80},{80,96},{96,112},{112,128},... | collective-permute-start | bytes 98312 | tf_op jit(solution)/shard_map/ppermute | solution.py:124
Sparse Core Ops, SparseCore 0:
  84.2 95.3 reduce-scatter.1

commit v3 on v2

--- a/solution.py
+++ b/solution.py
@@ -165,16 +165,17 @@
 def per_device(features, first_weight, second_weight, out_grad):
     feat = features[:, 0, :]
     og = out_grad[:, 0, :]
-    x_row = lax.all_gather(feat, "filt", axis=0, tiled=True)
+    n_filt = lax.axis_size("filt")
+    x_row = exchange(feat, "filt", "ag", 1).reshape(-1, feat.shape[1])
     pre_first = conv_forward(first_weight, x_row)
     hidden = jnp.maximum(pre_first, 0.0).astype(jnp.bfloat16)
-    h_row = lax.all_gather(hidden, "filt", axis=0, tiled=True)
+    h_row = exchange(hidden, "filt", "ag", 2).reshape(-1, hidden.shape[1])
     pre_second = conv_forward(second_weight, h_row) + feat.astype(jnp.float32)
     block_out = jnp.maximum(pre_second, 0.0).astype(jnp.bfloat16)
     grad_second = jnp.where(pre_second > 0, og.astype(jnp.float32), 0.0).astype(jnp.bfloat16)
     gs3 = grad_rows(grad_second)
     terms = hidden_terms(second_weight, gs3)
-    hidden_grad = lax.psum_scatter(terms, "filt", scatter_dimension=0, tiled=True)
+    hidden_grad = exchange(terms.reshape(n_filt, -1, terms.shape[1]), "filt", "rs", 3)
     grad_first = jnp.where(pre_first > 0, hidden_grad, 0.0).astype(jnp.bfloat16)
     gf3 = grad_rows(grad_first)
     second_local = weight_terms(gs3, h_row)

time: 322 us -> 239 us (0.74)
  waiting for transfers between devices: 108 us -> 11.2 us
  Pallas kernels: 120 us -> 185 us
  blocking collectives: 45.2 us -> 0 us
  between operations: 14.3 us -> 0.96 us
    reduce_scatter x1 -> x0, waiting for transfers between devices: 93.9 us -> none  [per_device(): lax.psum_scatter(terms, 'filt', scatter_dimension=0, tiled=True)]
    pallas_call x1 -> x4, Pallas kernels: 120 us -> 185 us  [exchange(): pl.pallas_call(functools.partial(exchange_kernel, axis, n, mode), out_sha...]
    all_gather x2 -> x0, blocking collectives: 45.2 us -> none  [the longest x1 22.9 us: per_device(): h_row = lax.all_gather(hidden, 'filt', axis=0, tiled=True)]
  transfers between devices with their start and end apart: 9 -> 8, of which waited for: 7 -> 6; matrix products, arithmetic and copies ran while one was open for 1% -> 1% of each run, Pallas kernels for 0% -> 0%
where the time goes in v3:
time: 239 us; the launch traced here: 236 us
  Pallas kernels  185 us (77%)
  starting transfers between devices  22.9 us (10%)
  waiting for transfers between devices  11.2 us (5%)
  local copies, waits for them, and re-layouts  7.21 us (3%)
  matrix products  6.57 us (3%)
  other arithmetic  2.78 us (1%)
    pallas_call x4, Pallas kernels, exchange(): pl.pallas_call(functools.partial(exchange_kernel, axis, n, mode), out_sha...  185 us
    ppermute x4, starting transfers between devices, from_prev(): return lax.ppermute(value, 'rows', [(i, i + 1) for i in range(count - 1)])  17.8 us
    ppermute x4, waiting for transfers between devices, from_next(): return lax.ppermute(value, 'rows', [(i + 1, i) for i in range(count - 1)])  8.47 us
    ppermute x4, starting transfers between devices, from_next(): return lax.ppermute(value, 'rows', [(i + 1, i) for i in range(count - 1)])  5.17 us
  transfers between devices with their start and end apart: 8, of which 6 were waited for; matrix products, arithmetic and copies ran while one was open for 1% of the time, Pallas kernels for 0%

profile of v3, /device:TPU:6, one launch (start us, length us, event | category | flops | bytes accessed | tf_op | source)
XLA Modules:
  0.0 236.2 jit_solution(1972730221399664391)
XLA Ops:
  0.6 0.0 copy-start
  0.6 18.6 %shard_map.67 = bf16[16,32,512]{2,1,0:T(8,128)(2,1)} custom-call(bf16[32,512]{1,0:T(8,128)(2,1)} %bitcast.210), custom_call_target="tpu_custom_call" | custom-call | tf_op jit(solution)/shard_map/pallas_call | solution.py:103
  19.2 0.0 copy-done
  19.2 1.4 convolution_bitcast_fusion.4
  20.6 0.0 copy-start.3
  20.6 0.1 slice.167
  20.7 0.1 slice.172
  20.8 0.1 fusion.24
  20.9 1.3 collective-permute-start.1
  22.2 4.5 %collective-permute-start = (f32[32,512]{1,0:T(8,128)S(1)}, f32[32,512]{1,0:T(8,128)S(1)}, u32[]{:S(2)}, u32[]{:S(2)}) collective-permute-start(f32[32,512]{1,0:T(8,128)S(1)} %get-tuple-element.29), channel_id=1, source_target_pairs={{0,16},{16,32},{32,48},{48,64},{64,80},{80,96},{96,112},{112,128},... | collective-permute-start | bytes 196616 | tf_op jit(solution)/shard_map/ppermute | solution.py:124
  26.8 0.1 slice.162
  26.9 0.5 collective-permute-done.1
  27.3 1.3 collective-permute-done
  28.7 0.7 maximum_convert_fusion.1
  29.4 14.9 %shard_map.68 = bf16[16,32,512]{2,1,0:T(8,128)(2,1)} custom-call(bf16[32,512]{1,0:T(8,128)(2,1)} %get-tuple-element.11.refs_0_), custom_call_target="tpu_custom_call" | custom-call | tf_op jit(solution)/shard_map/pallas_call | solution.py:103
  44.3 0.0 copy-done.3
  44.3 1.4 convolution_bitcast_fusion.3
  45.7 0.0 copy-start.4
  45.7 0.0 copy-start.5
  45.7 0.1 slice.182
  45.8 0.1 slice.187
  45.9 0.1 fusion.15
  46.0 1.3 collective-permute-start.3
  47.3 4.7 %collective-permute-start.2 = (f32[32,512]{1,0:T(8,128)S(1)}, f32[32,512]{1,0:T(8,128)S(1)}, u32[]{:S(2)}, u32[]{:S(2)}) collective-permute-start(f32[32,512]{1,0:T(8,128)S(1)} %get-tuple-element.21), channel_id=1, source_target_pairs={{0,16},{16,32},{32,48},{48,64},{64,80},{80,96},{96,112},{112,128},... | collective-permute-start | bytes 196616 | tf_op jit(solution)/shard_map/ppermute | solution.py:124
  52.0 0.1 slice.177
  52.1 0.4 collective-permute-done.3
  52.5 1.4 collective-permute-done.2
  53.9 0.0 copy-done.4
  53.9 0.1 fusion.29
  54.0 4.3 %collective-permute-start.5 = (bf16[32,512]{1,0:T(8,128)(2,1)S(1)}, bf16[32,512]{1,0:T(8,128)(2,1)S(1)}, u32[]{:S(2)}, u32[]{:S(2)}) collective-permute-start(bf16[32,512]{1,0:T(8,128)(2,1)S(1)} %get-tuple-element.9), channel_id=1, source_target_pairs={{0,16},{16,32},{32,48},{48,64},{64,80},{80,96},{96,112},{112,128},... | collective-permute-start | bytes 98312 | tf_op jit(solution)/shard_map/ppermute | solution.py:124
  58.3 1.3 collective-permute-start.4
  59.6 0.6 fusion.30
  60.2 0.0 collective-permute-done.5
  60.2 3.9 %collective-permute-done.4 = bf16[32,512]{1,0:T(8,128)(2,1)S(1)} collective-permute-done((bf16[32,512]{1,0:T(8,128)(2,1)S(1)}, bf16[32,512]{1,0:T(8,128)(2,1)S(1)}, u32[]{:S(2)}, u32[]{:S(2)}) %collective-permute-start.4) | collective-permute-done | bytes 32800 | tf_op jit(solution)/shard_map/ppermute | solution.py:129
  64.1 0.3 convolution_bitcast_fusion
  64.4 0.3 convolution_bitcast_fusion.2
  64.8 0.3 slice.188
  65.1 1.4 fusion.1
  66.5 21.3 %shard_map.69 = f32[32,512]{1,0:T(8,128)} custom-call(f32[16,32,512]{2,1,0:T(8,128)} %bitcast.185), custom_call_target="tpu_custom_call" | custom-call | tf_op jit(solution)/shard_map/pallas_call | solution.py:103
  87.8 0.9 select_convert_fusion
  88.7 4.3 %collective-permute-start.7 = (bf16[32,512]{1,0:T(8,128)(2,1)S(1)}, bf16[32,512]{1,0:T(8,128)(2,1)S(1)}, u32[]{:S(2)}, u32[]{:S(2)}) collective-permute-start(bf16[32,512]{1,0:T(8,128)(2,1)S(1)} %select_convert_fusion), channel_id=1, source_target_pairs={{0,16},{16,32},{32,48},{48,64},{64,80},{80,96},{96,112},{112,128},... | collective-permute-start | bytes 98312 | tf_op jit(solution)/shard_map/ppermute | solution.py:124
  92.9 1.3 collective-permute-start.6
  94.3 0.0 copy-done.2
  94.3 0.3 convolution_bitcast_fusion.6
  94.5 0.0 copy-start.1
  94.6 0.1 fusion.39
  94.7 0.3 convolution_bitcast_fusion.5
  95.0 0.3 convolution_bitcast_fusion.7
  95.3 0.0 collective-permute-done.7
  95.3 3.7 %collective-permute-done.6 = bf16[32,512]{1,0:T(8,128)(2,1)S(1)} collective-permute-done((bf16[32,512]{1,0:T(8,128)(2,1)S(1)}, bf16[32,512]{1,0:T(8,128)(2,1)S(1)}, u32[]{:S(2)}, u32[]{:S(2)}) %collective-permute-start.6) | collective-permute-done | bytes 32800 | tf_op jit(solution)/shard_map/ppermute | solution.py:129
  99.0 0.3 convolution_bitcast_fusion.9
  99.3 0.1 fusion.38
  99.4 0.3 convolution_bitcast_fusion.8
  99.7 0.3 convolution_bitcast_fusion.10
  100.0 0.1 maximum_bitcast_fusion
  100.1 0.1 pad_maximum_fusion
  100.2 0.8 copy.16
  101.1 1.5 reshape.36.refs_0_
  102.6 129.9 %shard_map.70 = f32[32,72,128]{2,1,0:T(8,128)} custom-call(f32[32,72,128]{2,1,0:T(8,128)} %reshape.36.refs_0_), custom_call_target="tpu_custom_call" | custom-call | tf_op jit(solution)/shard_map/pallas_call | solution.py:103
  232.4 1.3 fusion.37
  233.8 0.2 unstack.13
  234.0 1.0 copy.17
  235.0 0.2 unstack.15
  235.3 1.0 copy.18
  (7 shorter events, 0.1 us)
Async XLA Ops:
  0.6 18.6 %copy-start = (bf16[32,3,3,512]{3,0,2,1:T(8,128)(2,1)S(1)}, bf16[32,3,3,512]{3,0,2,1:T(8,128)(2,1)}, u32[]{:S(2)}) copy-start(bf16[32,3,3,512]{3,0,2,1:T(8,128)(2,1)} %param.5) | copy-start | bytes 884740
  20.6 23.7 %copy-start.3 = (bf16[32,3,3,512]{3,0,2,1:T(8,128)(2,1)S(1)}, bf16[32,3,3,512]{3,0,2,1:T(8,128)(2,1)}, u32[]{:S(2)}) copy-start(bf16[32,3,3,512]{3,0,2,1:T(8,128)(2,1)} %param.6) | copy-start | bytes 884740
  20.9 6.4 %collective-permute-start.1 = (f32[32,512]{1,0:T(8,128)S(1)}, f32[32,512]{1,0:T(8,128)S(1)}, u32[]{:S(2)}, u32[]{:S(2)}) collective-permute-start(f32[32,512]{1,0:T(8,128)S(1)} %get-tuple-element.30), channel_id=1, source_target_pairs={{16,0},{32,16},{48,32},{64,48},{80,64},{96,80},{112,96},{128,112},... | collective-permute-start | bytes 196616 | tf_op jit(solution)/shard_map/ppermute | solution.py:129
  22.2 6.4 %collective-permute-start = (f32[32,512]{1,0:T(8,128)S(1)}, f32[32,512]{1,0:T(8,128)S(1)}, u32[]{:S(2)}, u32[]{:S(2)}) collective-permute-start(f32[32,512]{1,0:T(8,128)S(1)} %get-tuple-element.29), channel_id=1, source_target_pairs={{0,16},{16,32},{32,48},{48,64},{64,80},{80,96},{96,112},{112,128},... | collective-permute-start | bytes 196616 | tf_op jit(solution)/shard_map/ppermute | solution.py:124
  45.7 8.2 %copy-start.4 = (bf16[32,1,512]{2,0,1:T(8,128)(2,1)S(1)}, bf16[32,1,512]{2,0,1:T(8,128)(2,1)}, u32[]{:S(2)}) copy-start(bf16[32,1,512]{2,0,1:T(8,128)(2,1)} %param.4) | copy-start | bytes 98308
  45.7 8.2 %copy-start.5 = (bf16[32,1,512]{2,0,1:T(8,128)(2,1)S(1)}, bf16[32,1,512]{2,0,1:T(8,128)(2,1)}, u32[]{:S(2)}) copy-start(bf16[32,1,512]{2,0,1:T(8,128)(2,1)} %param.7) | copy-start | bytes 98308
  46.0 6.5 %collective-permute-start.3 = (f32[32,512]{1,0:T(8,128)S(1)}, f32[32,512]{1,0:T(8,128)S(1)}, u32[]{:S(2)}, u32[]{:S(2)}) collective-permute-start(f32[32,512]{1,0:T(8,128)S(1)} %get-tuple-element.22), channel_id=1, source_target_pairs={{16,0},{32,16},{48,32},{64,48},{80,64},{96,80},{112,96},{128,112},... | collective-permute-start | bytes 196616 | tf_op jit(solution)/shard_map/ppermute | solution.py:129
  47.3 6.6 %collective-permute-start.2 = (f32[32,512]{1,0:T(8,128)S(1)}, f32[32,512]{1,0:T(8,128)S(1)}, u32[]{:S(2)}, u32[]{:S(2)}) collective-permute-start(f32[32,512]{1,0:T(8,128)S(1)} %get-tuple-element.21), channel_id=1, source_target_pairs={{0,16},{16,32},{32,48},{48,64},{64,80},{80,96},{96,112},{112,128},... | collective-permute-start | bytes 196616 | tf_op jit(solution)/shard_map/ppermute | solution.py:124
  54.0 6.2 %collective-permute-start.5 = (bf16[32,512]{1,0:T(8,128)(2,1)S(1)}, bf16[32,512]{1,0:T(8,128)(2,1)S(1)}, u32[]{:S(2)}, u32[]{:S(2)}) collective-permute-start(bf16[32,512]{1,0:T(8,128)(2,1)S(1)} %get-tuple-element.9), channel_id=1, source_target_pairs={{0,16},{16,32},{32,48},{48,64},{64,80},{80,96},{96,112},{112,128},... | collective-permute-start | bytes 98312 | tf_op jit(solution)/shard_map/ppermute | solution.py:124
  58.3 5.8 %collective-permute-start.4 = (bf16[32,512]{1,0:T(8,128)(2,1)S(1)}, bf16[32,512]{1,0:T(8,128)(2,1)S(1)}, u32[]{:S(2)}, u32[]{:S(2)}) collective-permute-start(bf16[32,512]{1,0:T(8,128)(2,1)S(1)} %get-tuple-element.9), channel_id=1, source_target_pairs={{16,0},{32,16},{48,32},{64,48},{80,64},{96,80},{112,96},{128,112},... | collective-permute-start | bytes 98312 | tf_op jit(solution)/shard_map/ppermute | solution.py:129
  66.5 27.7 %copy-start.2 = (bf16[16,32,512]{2,1,0:T(8,128)(2,1)S(1)}, bf16[16,32,512]{2,1,0:T(8,128)(2,1)}, u32[]{:S(2)}) copy-start(bf16[16,32,512]{2,1,0:T(8,128)(2,1)} %shard_map.68) | copy-start | bytes 1572868
  88.7 6.6 %collective-permute-start.7 = (bf16[32,512]{1,0:T(8,128)(2,1)S(1)}, bf16[32,512]{1,0:T(8,128)(2,1)S(1)}, u32[]{:S(2)}, u32[]{:S(2)}) collective-permute-start(bf16[32,512]{1,0:T(8,128)(2,1)S(1)} %select_convert_fusion), channel_id=1, source_target_pairs={{0,16},{16,32},{32,48},{48,64},{64,80},{80,96},{96,112},{112,128},... | collective-permute-start | bytes 98312 | tf_op jit(solution)/shard_map/ppermute | solution.py:124
  92.9 6.0 %collective-permute-start.6 = (bf16[32,512]{1,0:T(8,128)(2,1)S(1)}, bf16[32,512]{1,0:T(8,128)(2,1)S(1)}, u32[]{:S(2)}, u32[]{:S(2)}) collective-permute-start(bf16[32,512]{1,0:T(8,128)(2,1)S(1)} %select_convert_fusion), channel_id=1, source_target_pairs={{16,0},{32,16},{48,32},{64,48},{80,64},{96,80},{112,96},{128,112},... | collective-permute-start | bytes 98312 | tf_op jit(solution)/shard_map/ppermute | solution.py:129
  94.5 4.4 %copy-start.1 = (bf16[16,32,512]{2,1,0:T(8,128)(2,1)S(1)}, bf16[16,32,512]{2,1,0:T(8,128)(2,1)}, u32[]{:S(2)}) copy-start(bf16[16,32,512]{2,1,0:T(8,128)(2,1)} %shard_map.67) | copy-start | bytes 1572868

commit v4 on v3

--- a/solution.py
+++ b/solution.py
@@ -85,6 +85,93 @@
         copy, incoming = gather(out_ref.at[me], out_ref, send2, recv2)
         each_peer(lambda j, s: incoming(j, s).wait_recv())
         each_peer(lambda j, s: copy(j, s).wait_send())
+
+
+def row_sum_kernel(n, x_ref, out_ref, half_buf, half_b, part_buf, sems):
+    zn = n // 2
+    me = lax.axis_index("rows")
+    my_y, my_z = me // zn, lax.rem(me, zn)
+    other = lax.rem(me + zn, n)
+    mine, theirs = my_y * zn, (1 - my_y) * zn
+
+    def dev(j):
+        return (j, lax.axis_index("filt"))
+
+    def each_z(body):
+        def step(k, carry):
+            body(lax.rem(my_z + k, zn), lax.rem(my_z + zn - k, zn))
+            return carry
+
+        lax.fori_loop(1, zn, step, 0)
+
+    barrier = pltpu.get_barrier_semaphore()
+    pl.semaphore_signal(barrier, 1, device_id=dev(other), device_id_type=MESH)
+    each_z(lambda j, s: pl.semaphore_signal(barrier, 1, device_id=dev(mine + j), device_id_type=MESH))
+    pl.semaphore_wait(barrier, zn)
+
+    def rcopy(src, dst, send, recv, j):
+        return pltpu.make_async_remote_copy(src, dst, send, recv, device_id=dev(j), device_id_type=MESH)
+
+    swap = rcopy(x_ref.at[pl.ds(theirs, zn)], half_buf, sems.at[0, 0], sems.at[0, 1], other)
+    swap.start()
+    swap.wait_recv()
+
+    def add_half(t, carry):
+        half_b[t] = (x_ref[mine + t].astype(jnp.float32) + half_buf[t].astype(jnp.float32)).astype(half_b.dtype)
+        return carry
+
+    lax.fori_loop(0, zn, add_half, 0)
+    swap.wait_send()
+
+    def part_out(j, s):
+        return rcopy(half_b.at[j], part_buf.at[my_z], sems.at[1, j], sems.at[2, my_z], mine + j)
+
+    def part_in(j, s):
+        return rcopy(half_b.at[s], part_buf.at[s], sems.at[1, s], sems.at[2, s], mine + s)
+
+    each_z(lambda j, s: part_out(j, s).start())
+    each_z(lambda j, s: part_in(j, s).wait_recv())
+    acc = (x_ref[me].astype(jnp.float32) + half_buf[my_z].astype(jnp.float32))
+
+    def add_part(k, acc):
+        return acc + part_buf[lax.rem(my_z + k, zn)].astype(jnp.float32)
+
+    acc = lax.fori_loop(1, zn, add_part, acc)
+    out_ref[me] = acc.astype(out_ref.dtype)
+    each_z(lambda j, s: part_out(j, s).wait_send())
+
+    def sum_out(j, s):
+        return rcopy(out_ref.at[me], out_ref.at[me], sems.at[3, j], sems.at[4, my_z], mine + j)
+
+    def sum_in(j, s):
+        return rcopy(out_ref.at[mine + s], out_ref.at[mine + s], sems.at[3, s], sems.at[4, s], mine + s)
+
+    each_z(lambda j, s: sum_out(j, s).start())
+    each_z(lambda j, s: sum_in(j, s).wait_recv())
+    each_z(lambda j, s: sum_out(j, s).wait_send())
+    back = rcopy(out_ref.at[pl.ds(mine, zn)], out_ref.at[pl.ds(mine, zn)], sems.at[5, 0], sems.at[5, 1], other)
+    back.start()
+    back.wait_recv()
+    back.wait_send()
+
+
+def row_sum(x, collective_id):
+    n = x.shape[0]
+    zn = n // 2
+    blk = x.shape[1:]
+    return pl.pallas_call(
+        functools.partial(row_sum_kernel, n),
+        out_shape=jax.ShapeDtypeStruct(x.shape, x.dtype),
+        in_specs=[pl.BlockSpec(memory_space=pltpu.VMEM)],
+        out_specs=pl.BlockSpec(memory_space=pltpu.VMEM),
+        scratch_shapes=[
+            pltpu.VMEM((zn,) + blk, x.dtype),
+            pltpu.VMEM((zn,) + blk, x.dtype),
+            pltpu.VMEM((zn,) + blk, x.dtype),
+            pltpu.SemaphoreType.DMA((6, zn)),
+        ],
+        compiler_params=pltpu.CompilerParams(collective_id=collective_id, has_side_effects=True),
+    )(x)
 
 
 def exchange(x, axis, mode, collective_id, out_dtype=None):
@@ -175,15 +262,17 @@
     grad_second = jnp.where(pre_second > 0, og.astype(jnp.float32), 0.0).astype(jnp.bfloat16)
     gs3 = grad_rows(grad_second)
     terms = hidden_terms(second_weight, gs3)
-    hidden_grad = exchange(terms.reshape(n_filt, -1, terms.shape[1]), "filt", "rs", 3)
+    hidden_grad = exchange(
+        terms.astype(jnp.bfloat16).reshape(n_filt, -1, terms.shape[1]), "filt", "rs", 3, jnp.float32
+    )
     grad_first = jnp.where(pre_first > 0, hidden_grad, 0.0).astype(jnp.bfloat16)
     gf3 = grad_rows(grad_first)
     second_local = weight_terms(gs3, h_row)
     first_local = weight_terms(gf3, x_row)
     both = jnp.stack([first_local, second_local])
     n_rows = lax.axis_size("rows")
-    summed = exchange(both.reshape(n_rows, -1, 128), "rows", "ar", 0)
-    first_grad, second_grad = summed.reshape(both.shape)
+    summed = row_sum(both.astype(jnp.bfloat16).reshape(n_rows, -1, 128), 0)
+    first_grad, second_grad = summed.astype(jnp.float32).reshape(both.shape)
     return (block_out[:, None, :], first_grad, second_grad)
 
 

time: 239 us -> 161 us (0.67)
  Pallas kernels: 185 us -> 107 us
  waiting for transfers between devices: 11.2 us -> 18.6 us
  starting transfers between devices: 22.9 us -> 18 us
    pallas_call x4 -> x3, Pallas kernels: 185 us -> 48.2 us  [exchange(): pl.pallas_call(functools.partial(exchange_kernel, axis, n, mode), out_sha...]
    pallas_call x0 -> x1, Pallas kernels: none -> 58.7 us  [row_sum(): pl.pallas_call(functools.partial(row_sum_kernel, n), out_shape=jax.ShapeD...]
    ppermute x4, waiting for transfers between devices: 8.47 us -> 17.2 us  [from_next(): return lax.ppermute(value, 'rows', [(i + 1, i) for i in range(count - 1)])]
    ppermute x4, starting transfers between devices: 17.8 us -> 12.9 us  [from_prev(): return lax.ppermute(value, 'rows', [(i, i + 1) for i in range(count - 1)])]
where the time goes in v4:
time: 161 us; the launch traced here: 160 us
  Pallas kernels  107 us (66%)
  waiting for transfers between devices  18.6 us (12%)
  starting transfers between devices  18 us (11%)
  local copies, waits for them, and re-layouts  6.45 us (4%)
  matrix products  6.37 us (4%)
  other arithmetic  2.65 us (2%)
    pallas_call x1, Pallas kernels, row_sum(): pl.pallas_call(functools.partial(row_sum_kernel, n), out_shape=jax.ShapeD...  58.7 us
    pallas_call x3, Pallas kernels, exchange(): pl.pallas_call(functools.partial(exchange_kernel, axis, n, mode), out_sha...  48.2 us
    ppermute x4, waiting for transfers between devices, from_next(): return lax.ppermute(value, 'rows', [(i + 1, i) for i in range(count - 1)])  17.2 us
    ppermute x4, starting transfers between devices, from_prev(): return lax.ppermute(value, 'rows', [(i, i + 1) for i in range(count - 1)])  12.9 us
    ppermute x4, starting transfers between devices, from_next(): return lax.ppermute(value, 'rows', [(i + 1, i) for i in range(count - 1)])  5.17 us
  transfers between devices with their start and end apart: 8, of which 6 were waited for; matrix products, arithmetic and copies ran while one was open for 1% of the time, Pallas kernels for 0%

profile of v4, /device:TPU:6, one launch (start us, length us, event | category | flops | bytes accessed | tf_op | source)
XLA Modules:
  0.0 160.0 jit_solution(1494658620007339529)
XLA Ops:
  0.6 0.0 copy-start
  0.6 18.6 %shard_map.67 = bf16[16,32,512]{2,1,0:T(8,128)(2,1)} custom-call(bf16[32,512]{1,0:T(8,128)(2,1)} %bitcast.212), custom_call_target="tpu_custom_call" | custom-call | tf_op jit(solution)/shard_map/pallas_call | solution.py:190
  19.2 0.0 copy-done
  19.2 1.4 convolution_bitcast_fusion.4
  20.6 0.1 slice.172
  20.7 0.1 slice.167
  20.8 0.1 fusion.31
  20.9 1.3 collective-permute-start
  22.2 1.3 collective-permute-start.1
  23.5 0.1 slice.162
  23.6 0.9 collective-permute-done
  24.5 4.1 %collective-permute-done.1 = f32[32,512]{1,0:T(8,128)S(1)} collective-permute-done((f32[32,512]{1,0:T(8,128)S(1)}, f32[32,512]{1,0:T(8,128)S(1)}, u32[]{:S(2)}, u32[]{:S(2)}) %collective-permute-start.1) | collective-permute-done | bytes 65568 | tf_op jit(solution)/shard_map/ppermute | solution.py:216
  28.6 0.7 maximum_convert_fusion.1
  29.3 14.8 %shard_map.68 = bf16[16,32,512]{2,1,0:T(8,128)(2,1)} custom-call(bf16[32,512]{1,0:T(8,128)(2,1)} %get-tuple-element.11.refs_0_), custom_call_target="tpu_custom_call" | custom-call | tf_op jit(solution)/shard_map/pallas_call | solution.py:190
  44.1 0.0 copy-done.3
  44.1 1.4 convolution_bitcast_fusion.3
  45.5 0.1 slice.187
  45.6 0.1 slice.182
  45.7 0.0 copy-start.2
  45.7 0.1 fusion.22
  45.8 2.6 %collective-permute-start.2 = (f32[32,512]{1,0:T(8,128)S(1)}, f32[32,512]{1,0:T(8,128)S(1)}, u32[]{:S(2)}, u32[]{:S(2)}) collective-permute-start(f32[32,512]{1,0:T(8,128)S(1)} %get-tuple-element.21), channel_id=1, source_target_pairs={{0,16},{16,32},{32,48},{48,64},{64,80},{80,96},{96,112},{112,128},... | collective-permute-start | bytes 196616 | tf_op jit(solution)/shard_map/ppermute | solution.py:211
  48.4 1.3 collective-permute-start.3
  49.7 0.0 copy-start.4
  49.8 0.0 copy-start.5
  49.8 0.1 slice.177
  49.8 0.6 collective-permute-done.2
  50.4 5.4 %collective-permute-done.3 = f32[32,512]{1,0:T(8,128)S(1)} collective-permute-done((f32[32,512]{1,0:T(8,128)S(1)}, f32[32,512]{1,0:T(8,128)S(1)}, u32[]{:S(2)}, u32[]{:S(2)}) %collective-permute-start.3) | collective-permute-done | bytes 65568 | tf_op jit(solution)/shard_map/ppermute | solution.py:216
  55.8 0.0 copy-done.4
  55.8 0.0 copy-done.5
  55.8 0.1 fusion.36
  55.9 5.1 %collective-permute-start.5 = (bf16[32,512]{1,0:T(8,128)(2,1)S(1)}, bf16[32,512]{1,0:T(8,128)(2,1)S(1)}, u32[]{:S(2)}, u32[]{:S(2)}) collective-permute-start(bf16[32,512]{1,0:T(8,128)(2,1)S(1)} %get-tuple-element.9), channel_id=1, source_target_pairs={{0,16},{16,32},{32,48},{48,64},{64,80},{80,96},{96,112},{112,128},... | collective-permute-start | bytes 98312 | tf_op jit(solution)/shard_map/ppermute | solution.py:211
  61.1 1.3 collective-permute-start.4
  62.4 0.6 fusion.37
  63.0 0.0 collective-permute-done.5
  63.0 3.9 %collective-permute-done.4 = bf16[32,512]{1,0:T(8,128)(2,1)S(1)} collective-permute-done((bf16[32,512]{1,0:T(8,128)(2,1)S(1)}, bf16[32,512]{1,0:T(8,128)(2,1)S(1)}, u32[]{:S(2)}, u32[]{:S(2)}) %collective-permute-start.4) | collective-permute-done | bytes 32800 | tf_op jit(solution)/shard_map/ppermute | solution.py:216
  66.9 0.0 copy-done.2
  66.9 0.3 fusion.7
  67.2 0.3 convolution_bitcast_fusion.2
  67.5 0.3 convolution_bitcast_fusion
  67.9 0.3 slice.188
  68.2 1.2 fusion.2
  69.4 14.8 %shard_map.69 = f32[32,512]{1,0:T(8,128)} custom-call(bf16[16,32,512]{2,1,0:T(8,128)(2,1)} %bitcast.187), custom_call_target="tpu_custom_call" | custom-call | tf_op jit(solution)/shard_map/pallas_call | solution.py:190
  84.3 0.9 select_convert_fusion
  85.1 3.8 %collective-permute-start.7 = (bf16[32,512]{1,0:T(8,128)(2,1)S(1)}, bf16[32,512]{1,0:T(8,128)(2,1)S(1)}, u32[]{:S(2)}, u32[]{:S(2)}) collective-permute-start(bf16[32,512]{1,0:T(8,128)(2,1)S(1)} %select_convert_fusion), channel_id=1, source_target_pairs={{0,16},{16,32},{32,48},{48,64},{64,80},{80,96},{96,112},{112,128},... | collective-permute-start | bytes 98312 | tf_op jit(solution)/shard_map/ppermute | solution.py:211
  89.0 1.3 collective-permute-start.6
  90.3 0.1 fusion.46
  90.4 0.3 fusion.6
  90.7 0.3 fusion.8
  91.0 0.0 collective-permute-done.7
  91.0 3.8 %collective-permute-done.6 = bf16[32,512]{1,0:T(8,128)(2,1)S(1)} collective-permute-done((bf16[32,512]{1,0:T(8,128)(2,1)S(1)}, bf16[32,512]{1,0:T(8,128)(2,1)S(1)}, u32[]{:S(2)}, u32[]{:S(2)}) %collective-permute-start.6) | collective-permute-done | bytes 32800 | tf_op jit(solution)/shard_map/ppermute | solution.py:216
  94.8 0.3 fusion.4
  95.1 0.1 fusion.45
  95.2 0.3 fusion.3
  95.5 0.3 fusion.5
  95.8 0.1 maximum_bitcast_fusion
  95.9 0.1 pad_maximum_fusion
  95.9 0.5 copy.16
  96.4 1.2 convert_element_type.64.x_ref
  97.7 58.7 %shard_map.70 = bf16[32,72,128]{2,1,0:T(8,128)(2,1)} custom-call(bf16[32,72,128]{2,1,0:T(8,128)(2,1)} %convert_element_type.64.x_ref), custom_call_target="tpu_custom_call" | custom-call | tf_op jit(solution)/shard_map/pallas_call | solution.py:162
  156.4 1.1 fusion.44
  157.5 0.2 unstack.15
  157.8 1.0 copy.18
  158.8 0.2 unstack.13
  159.0 1.0 copy.17
  (7 shorter events, 0.1 us)
Async XLA Ops:
  0.6 18.6 %copy-start = (bf16[32,3,3,512]{3,0,2,1:T(8,128)(2,1)S(1)}, bf16[32,3,3,512]{3,0,2,1:T(8,128)(2,1)}, u32[]{:S(2)}) copy-start(bf16[32,3,3,512]{3,0,2,1:T(8,128)(2,1)} %param.5) | copy-start | bytes 884740
  20.9 3.6 %collective-permute-start = (f32[32,512]{1,0:T(8,128)S(1)}, f32[32,512]{1,0:T(8,128)S(1)}, u32[]{:S(2)}, u32[]{:S(2)}) collective-permute-start(f32[32,512]{1,0:T(8,128)S(1)} %get-tuple-element.29), channel_id=1, source_target_pairs={{0,16},{16,32},{32,48},{48,64},{64,80},{80,96},{96,112},{112,128},... | collective-permute-start | bytes 196616 | tf_op jit(solution)/shard_map/ppermute | solution.py:211
  22.2 6.4 %collective-permute-start.1 = (f32[32,512]{1,0:T(8,128)S(1)}, f32[32,512]{1,0:T(8,128)S(1)}, u32[]{:S(2)}, u32[]{:S(2)}) collective-permute-start(f32[32,512]{1,0:T(8,128)S(1)} %get-tuple-element.30), channel_id=1, source_target_pairs={{16,0},{32,16},{48,32},{64,48},{80,64},{96,80},{112,96},{128,112},... | collective-permute-start | bytes 196616 | tf_op jit(solution)/shard_map/ppermute | solution.py:216
  29.3 14.8 %copy-start.3 = (bf16[32,3,3,512]{3,0,2,1:T(8,128)(2,1)S(1)}, bf16[32,3,3,512]{3,0,2,1:T(8,128)(2,1)}, u32[]{:S(2)}) copy-start(bf16[32,3,3,512]{3,0,2,1:T(8,128)(2,1)} %param.6) | copy-start | bytes 884740
  45.7 21.2 %copy-start.2 = (bf16[16,32,512]{2,1,0:T(8,128)(2,1)S(1)}, bf16[16,32,512]{2,1,0:T(8,128)(2,1)}, u32[]{:S(2)}) copy-start(bf16[16,32,512]{2,1,0:T(8,128)(2,1)} %shard_map.68) | copy-start | bytes 1572868
  45.8 4.6 %collective-permute-start.2 = (f32[32,512]{1,0:T(8,128)S(1)}, f32[32,512]{1,0:T(8,128)S(1)}, u32[]{:S(2)}, u32[]{:S(2)}) collective-permute-start(f32[32,512]{1,0:T(8,128)S(1)} %get-tuple-element.21), channel_id=1, source_target_pairs={{0,16},{16,32},{32,48},{48,64},{64,80},{80,96},{96,112},{112,128},... | collective-permute-start | bytes 196616 | tf_op jit(solution)/shard_map/ppermute | solution.py:211
  48.4 7.4 %collective-permute-start.3 = (f32[32,512]{1,0:T(8,128)S(1)}, f32[32,512]{1,0:T(8,128)S(1)}, u32[]{:S(2)}, u32[]{:S(2)}) collective-permute-start(f32[32,512]{1,0:T(8,128)S(1)} %get-tuple-element.22), channel_id=1, source_target_pairs={{16,0},{32,16},{48,32},{64,48},{80,64},{96,80},{112,96},{128,112},... | collective-permute-start | bytes 196616 | tf_op jit(solution)/shard_map/ppermute | solution.py:216
  49.7 6.1 %copy-start.4 = (bf16[32,1,512]{2,0,1:T(8,128)(2,1)S(1)}, bf16[32,1,512]{2,0,1:T(8,128)(2,1)}, u32[]{:S(2)}) copy-start(bf16[32,1,512]{2,0,1:T(8,128)(2,1)} %param.4) | copy-start | bytes 98308
  49.8 6.1 %copy-start.5 = (bf16[32,1,512]{2,0,1:T(8,128)(2,1)S(1)}, bf16[32,1,512]{2,0,1:T(8,128)(2,1)}, u32[]{:S(2)}) copy-start(bf16[32,1,512]{2,0,1:T(8,128)(2,1)} %param.7) | copy-start | bytes 98308
  55.9 7.1 %collective-permute-start.5 = (bf16[32,512]{1,0:T(8,128)(2,1)S(1)}, bf16[32,512]{1,0:T(8,128)(2,1)S(1)}, u32[]{:S(2)}, u32[]{:S(2)}) collective-permute-start(bf16[32,512]{1,0:T(8,128)(2,1)S(1)} %get-tuple-element.9), channel_id=1, source_target_pairs={{0,16},{16,32},{32,48},{48,64},{64,80},{80,96},{96,112},{112,128},... | collective-permute-start | bytes 98312 | tf_op jit(solution)/shard_map/ppermute | solution.py:211
  61.1 5.8 %collective-permute-start.4 = (bf16[32,512]{1,0:T(8,128)(2,1)S(1)}, bf16[32,512]{1,0:T(8,128)(2,1)S(1)}, u32[]{:S(2)}, u32[]{:S(2)}) collective-permute-start(bf16[32,512]{1,0:T(8,128)(2,1)S(1)} %get-tuple-element.9), channel_id=1, source_target_pairs={{16,0},{32,16},{48,32},{64,48},{80,64},{96,80},{112,96},{128,112},... | collective-permute-start | bytes 98312 | tf_op jit(solution)/shard_map/ppermute | solution.py:216
  85.1 5.8 %collective-permute-start.7 = (bf16[32,512]{1,0:T(8,128)(2,1)S(1)}, bf16[32,512]{1,0:T(8,128)(2,1)S(1)}, u32[]{:S(2)}, u32[]{:S(2)}) collective-permute-start(bf16[32,512]{1,0:T(8,128)(2,1)S(1)} %select_convert_fusion), channel_id=1, source_target_pairs={{0,16},{16,32},{32,48},{48,64},{64,80},{80,96},{96,112},{112,128},... | collective-permute-start | bytes 98312 | tf_op jit(solution)/shard_map/ppermute | solution.py:211
  89.0 5.8 %collective-permute-start.6 = (bf16[32,512]{1,0:T(8,128)(2,1)S(1)}, bf16[32,512]{1,0:T(8,128)(2,1)S(1)}, u32[]{:S(2)}, u32[]{:S(2)}) collective-permute-start(bf16[32,512]{1,0:T(8,128)(2,1)S(1)} %select_convert_fusion), channel_id=1, source_target_pairs={{16,0},{32,16},{48,32},{64,48},{80,64},{96,80},{112,96},{128,112},... | collective-permute-start | bytes 98312 | tf_op jit(solution)/shard_map/ppermute | solution.py:216
  90.7 4.1 %copy-start.1 = (bf16[16,32,512]{2,1,0:T(8,128)(2,1)S(1)}, bf16[16,32,512]{2,1,0:T(8,128)(2,1)}, u32[]{:S(2)}) copy-start(bf16[16,32,512]{2,1,0:T(8,128)(2,1)} %shard_map.67) | copy-start | bytes 1572868

commit v5 on v4

--- a/solution.py
+++ b/solution.py
@@ -172,6 +172,72 @@
         ],
         compiler_params=pltpu.CompilerParams(collective_id=collective_id, has_side_effects=True),
     )(x)
+
+
+def halo_kernel(n, down_ref, up_ref, from_prev, from_next, sems):
+    me = lax.axis_index("rows")
+    has_prev, has_next = me > 0, me < n - 1
+
+    def dev(j):
+        return (j, lax.axis_index("filt"))
+
+    barrier = pltpu.get_barrier_semaphore()
+
+    @pl.when(has_prev)
+    def _():
+        pl.semaphore_signal(barrier, 1, device_id=dev(me - 1), device_id_type=MESH)
+
+    @pl.when(has_next)
+    def _():
+        pl.semaphore_signal(barrier, 1, device_id=dev(me + 1), device_id_type=MESH)
+
+    pl.semaphore_wait(barrier, (me + n - 1) // n + (2 * n - 2 - me) // n)
+
+    def down(j):
+        return pltpu.make_async_remote_copy(down_ref, from_prev, sems.at[0], sems.at[1], device_id=dev(j), device_id_type=MESH)
+
+    def up(j):
+        return pltpu.make_async_remote_copy(up_ref, from_next, sems.at[2], sems.at[3], device_id=dev(j), device_id_type=MESH)
+
+    @pl.when(has_next)
+    def _():
+        down(me + 1).start()
+
+    @pl.when(has_prev)
+    def _():
+        up(me - 1).start()
+
+    @pl.when(me == 0)
+    def _():
+        from_prev[...] = jnp.zeros(from_prev.shape, from_prev.dtype)
+
+    @pl.when(me == n - 1)
+    def _():
+        from_next[...] = jnp.zeros(from_next.shape, from_next.dtype)
+
+    @pl.when(has_prev)
+    def _():
+        down(me - 1).wait_recv()
+        up(me - 1).wait_send()
+
+    @pl.when(has_next)
+    def _():
+        up(me + 1).wait_recv()
+        down(me + 1).wait_send()
+
+
+def halo(down, up, collective_id):
+    n = lax.axis_size("rows")
+    spec = pl.BlockSpec(memory_space=pltpu.VMEM)
+    shape = jax.ShapeDtypeStruct(down.shape, down.dtype)
+    return pl.pallas_call(
+        functools.partial(halo_kernel, n),
+        out_shape=(shape, shape),
+        in_specs=[spec, spec],
+        out_specs=(spec, spec),
+        scratch_shapes=[pltpu.SemaphoreType.DMA((4,))],
+        compiler_params=pltpu.CompilerParams(collective_id=collective_id, has_side_effects=True),
+    )(down, up)
 
 
 def exchange(x, axis, mode, collective_id, out_dtype=None):
@@ -206,16 +272,6 @@
     return jnp.pad(value[..., :offset], pad + [(-offset, 0)])
 
 
-def from_prev(value):
-    count = lax.axis_size("rows")
-    return lax.ppermute(value, "rows", [(i, i + 1) for i in range(count - 1)])
-
-
-def from_next(value):
-    count = lax.axis_size("rows")
-    return lax.ppermute(value, "rows", [(i + 1, i) for i in range(count - 1)])
-
-
 def conv_row(weight, row):
     o = weight.shape[0]
     flat = weight.reshape(o, 9, weight.shape[3])
@@ -223,13 +279,15 @@
     return [sum(shift_cols(parts[a * 3 + b], b - 1) for b in range(3)) for a in range(3)]
 
 
-def conv_forward(weight, row):
+def conv_forward(weight, row, collective_id):
     p0, p1, p2 = conv_row(weight, row)
-    return p1 + from_prev(p0) + from_next(p2)
-
-
-def grad_rows(grad):
-    return jnp.stack([from_next(grad), grad, from_prev(grad)])
+    prev_p0, next_p2 = halo(p0, p2, collective_id)
+    return p1 + prev_p0 + next_p2
+
+
+def grad_rows(grad, collective_id):
+    prev_g, next_g = halo(grad, grad, collective_id)
+    return jnp.stack([next_g, grad, prev_g])
 
 
 def weight_terms(rows3, full_row):
@@ -254,19 +312,19 @@
     og = out_grad[:, 0, :]
     n_filt = lax.axis_size("filt")
     x_row = exchange(feat, "filt", "ag", 1).reshape(-1, feat.shape[1])
-    pre_first = conv_forward(first_weight, x_row)
+    pre_first = conv_forward(first_weight, x_row, 4)
     hidden = jnp.maximum(pre_first, 0.0).astype(jnp.bfloat16)
     h_row = exchange(hidden, "filt", "ag", 2).reshape(-1, hidden.shape[1])
-    pre_second = conv_forward(second_weight, h_row) + feat.astype(jnp.float32)
+    pre_second = conv_forward(second_weight, h_row, 5) + feat.astype(jnp.float32)
     block_out = jnp.maximum(pre_second, 0.0).astype(jnp.bfloat16)
     grad_second = jnp.where(pre_second > 0, og.astype(jnp.float32), 0.0).astype(jnp.bfloat16)
-    gs3 = grad_rows(grad_second)
+    gs3 = grad_rows(grad_second, 6)
     terms = hidden_terms(second_weight, gs3)
     hidden_grad = exchange(
         terms.astype(jnp.bfloat16).reshape(n_filt, -1, terms.shape[1]), "filt", "rs", 3, jnp.float32
     )
     grad_first = jnp.where(pre_first > 0, hidden_grad, 0.0).astype(jnp.bfloat16)
-    gf3 = grad_rows(grad_first)
+    gf3 = grad_rows(grad_first, 7)
     second_local = weight_terms(gs3, h_row)
     first_local = weight_terms(gf3, x_row)
     both = jnp.stack([first_local, second_local])

time: 161 us -> 163 us (1.012)
  Pallas kernels: 107 us -> 139 us
  waiting for transfers between devices: 18.6 us -> 0 us
  starting transfers between devices: 18 us -> 0 us
  other arithmetic: 2.65 us -> 6.07 us
  local copies, waits for them, and re-layouts: 6.45 us -> 8.2 us
  matrix products: 6.37 us -> 8.04 us
    pallas_call x0 -> x4, Pallas kernels: none -> 31.8 us  [halo(): pl.pallas_call(functools.partial(halo_kernel, n), out_shape=(shape, shape...]
    ppermute x8 -> x0, waiting for transfers between devices: 18.6 us -> none  [the longest x4 17.2 us: from_next(): return lax.ppermute(value, 'rows', [(i + 1, i) for i in range(count - 1)])]
    ppermute x8 -> x0, starting transfers between devices: 18 us -> none  [the longest x4 12.9 us: from_prev(): return lax.ppermute(value, 'rows', [(i, i + 1) for i in range(count - 1)])]
    unnamed x14 -> x30, local copies, waits for them, and re-layouts: 2.03 us -> 3.78 us
    dot_general x6, matrix products: 1.75 us -> 3.4 us  [weight_terms(): jnp.einsum('aow,iw->oai', moved, full_row, preferred_element_type=jnp.flo...]
  transfers between devices with their start and end apart: 8 -> 0, of which waited for: 6 -> 0; matrix products, arithmetic and copies ran while one was open for 1% -> 0% of each run, Pallas kernels for 0% -> 0%
where the time goes in v5:
time: 163 us; the launch traced here: 162 us
  Pallas kernels  139 us (85%)
  local copies, waits for them, and re-layouts  8.2 us (5%)
  matrix products  8.04 us (5%)
  other arithmetic  6.07 us (4%)
    pallas_call x1, Pallas kernels, row_sum(): pl.pallas_call(functools.partial(row_sum_kernel, n), out_shape=jax.ShapeD...  58.5 us
    pallas_call x3, Pallas kernels, exchange(): pl.pallas_call(functools.partial(exchange_kernel, axis, n, mode), out_sha...  48.2 us
    pallas_call x4, Pallas kernels, halo(): pl.pallas_call(functools.partial(halo_kernel, n), out_shape=(shape, shape...  31.8 us
    unnamed x30, local copies, waits for them, and re-layouts  3.78 us
    dot_general x6, matrix products, weight_terms(): jnp.einsum('aow,iw->oai', moved, full_row, preferred_element_type=jnp.flo...  3.4 us

profile of v5, /device:TPU:6, one launch (start us, length us, event | category | flops | bytes accessed | tf_op | source)
XLA Modules:
  0.0 161.8 jit_solution(905717208820586432)
XLA Ops:
  0.6 0.0 copy-start
  0.6 1.0 copy-done
  1.6 18.4 %shard_map.67 = bf16[16,32,512]{2,1,0:T(8,128)(2,1)} custom-call(bf16[32,512]{1,0:T(8,128)(2,1)} %bitcast.212), custom_call_target="tpu_custom_call" | custom-call | tf_op jit(solution)/shard_map/pallas_call | solution.py:256
  20.0 1.4 convolution_bitcast_fusion.4
  21.4 0.1 slice.172
  21.5 0.1 slice.167
  21.6 0.8 fusion.29
  22.4 6.7 %shard_map.68 = (f32[32,512]{1,0:T(8,128)}, f32[32,512]{1,0:T(8,128)}) custom-call(f32[32,512]{1,0:T(8,128)} %get-tuple-element.46.down_ref, f32[32,512]{1,0:T(8,128)} %get-tuple-element.45.up_ref), custom_call_target="tpu_custom_call" | custom-call | tf_op jit(solution)/shard_map/pallas_call | solution.py:233
  29.1 0.0 copy-start.11
  29.1 0.0 copy-start.12
  29.2 0.1 slice.162
  29.2 0.7 copy-done.11
  30.0 0.0 copy-done.12
  30.0 0.7 maximum_convert_fusion.1
  30.7 14.8 %shard_map.69 = bf16[16,32,512]{2,1,0:T(8,128)(2,1)} custom-call(bf16[32,512]{1,0:T(8,128)(2,1)} %get-tuple-element.27.refs_0_), custom_call_target="tpu_custom_call" | custom-call | tf_op jit(solution)/shard_map/pallas_call | solution.py:256
  45.5 0.0 copy-done.7
  45.6 1.4 convolution_bitcast_fusion.3
  47.0 0.1 slice.187
  47.0 0.1 slice.182
  47.1 0.0 copy-start.8
  47.1 0.0 copy-start.13
  47.1 0.8 fusion.20
  47.9 7.8 %shard_map.70 = (f32[32,512]{1,0:T(8,128)}, f32[32,512]{1,0:T(8,128)}) custom-call(f32[32,512]{1,0:T(8,128)} %get-tuple-element.38.down_ref, f32[32,512]{1,0:T(8,128)} %get-tuple-element.37.up_ref), custom_call_target="tpu_custom_call" | custom-call | tf_op jit(solution)/shard_map/pallas_call | solution.py:233
  55.7 0.1 slice.177
  55.8 0.0 copy-done.8
  55.8 0.0 copy-done.13
  55.8 1.6 fusion.36
  57.4 0.6 fusion.37
  58.0 8.0 %shard_map.71 = (bf16[32,512]{1,0:T(8,128)(2,1)}, bf16[32,512]{1,0:T(8,128)(2,1)}) custom-call(bf16[32,512]{1,0:T(8,128)(2,1)} %get-tuple-element.25.down_ref.up_ref, bf16[32,512]{1,0:T(8,128)(2,1)} %get-tuple-element.25.down_ref.up_ref), custom_call_target="tpu_custom_call" | custom-call | tf_op jit(solution)/shard_map/pallas_call | solution.py:233
  66.0 0.0 copy-done.2
  66.0 0.0 copy-done.3
  66.0 0.0 copy-start.5
  66.1 0.0 copy-start.6
  66.1 1.1 fusion.7
  67.2 0.0 copy-done.5
  67.2 0.0 copy-done.6
  67.2 0.1 fusion.46
  67.3 0.3 fusion.6
  67.6 0.3 fusion.8
  67.9 0.3 convolution_bitcast_fusion.2
  68.3 0.3 slice.188
  68.6 0.3 convolution_bitcast_fusion
  69.0 1.2 fusion.2
  70.2 15.0 %shard_map.72 = f32[32,512]{1,0:T(8,128)} custom-call(bf16[16,32,512]{2,1,0:T(8,128)(2,1)} %bitcast.187), custom_call_target="tpu_custom_call" | custom-call | tf_op jit(solution)/shard_map/pallas_call | solution.py:256
  85.2 1.5 select_convert_fusion.down_ref.up_ref
  86.6 9.3 %shard_map.73 = (bf16[32,512]{1,0:T(8,128)(2,1)}, bf16[32,512]{1,0:T(8,128)(2,1)}) custom-call(bf16[32,512]{1,0:T(8,128)(2,1)} %select_convert_fusion.down_ref.up_ref, bf16[32,512]{1,0:T(8,128)(2,1)} %select_convert_fusion.down_ref.up_ref), custom_call_target="tpu_custom_call" | custom-call | tf_op jit(solution)/shard_map/pallas_call | solution.py:233
  95.9 0.0 copy-done.1
  95.9 0.0 copy-done.4
  96.0 1.1 fusion.4
  97.1 0.0 copy-done.9
  97.1 0.0 copy-done.10
  97.1 0.1 fusion.45
  97.2 0.3 fusion.3
  97.5 0.3 fusion.5
  97.8 0.1 maximum_bitcast_fusion
  97.9 0.1 pad_maximum_fusion
  98.0 0.5 copy.16
  98.5 1.2 convert_element_type.64.x_ref
  99.7 58.5 %shard_map.74 = bf16[32,72,128]{2,1,0:T(8,128)(2,1)} custom-call(bf16[32,72,128]{2,1,0:T(8,128)(2,1)} %convert_element_type.64.x_ref), custom_call_target="tpu_custom_call" | custom-call | tf_op jit(solution)/shard_map/pallas_call | solution.py:162
  158.2 1.1 fusion.44
  159.3 0.2 unstack.15
  159.6 1.0 copy.18
  160.6 0.2 unstack.13
  160.8 1.0 copy.17
  (11 shorter events, 0.1 us)
Async XLA Ops:
  0.6 1.0 copy-start
  29.1 0.8 copy-start.11
  29.1 0.9 copy-start.12
  30.7 14.8 %copy-start.7 = (bf16[32,3,3,512]{3,0,2,1:T(8,128)(2,1)S(1)}, bf16[32,3,3,512]{3,0,2,1:T(8,128)(2,1)}, u32[]{:S(2)}) copy-start(bf16[32,3,3,512]{3,0,2,1:T(8,128)(2,1)} %param.6) | copy-start | bytes 884740
  47.1 8.6 %copy-start.8 = (bf16[32,1,512]{2,0,1:T(8,128)(2,1)S(1)}, bf16[32,1,512]{2,0,1:T(8,128)(2,1)}, u32[]{:S(2)}) copy-start(bf16[32,1,512]{2,0,1:T(8,128)(2,1)} %param.4) | copy-start | bytes 98308
  47.1 8.6 %copy-start.13 = (bf16[32,1,512]{2,0,1:T(8,128)(2,1)S(1)}, bf16[32,1,512]{2,0,1:T(8,128)(2,1)}, u32[]{:S(2)}) copy-start(bf16[32,1,512]{2,0,1:T(8,128)(2,1)} %param.7) | copy-start | bytes 98308
  47.9 18.1 %copy-start.2 = (bf16[16,32,512]{2,1,0:T(8,128)(2,1)S(1)}, bf16[16,32,512]{2,1,0:T(8,128)(2,1)}, u32[]{:S(2)}) copy-start(bf16[16,32,512]{2,1,0:T(8,128)(2,1)} %shard_map.69) | copy-start | bytes 1572868
  58.0 8.0 %copy-start.3 = (bf16[32,512]{1,0:T(8,128)(2,1)S(1)}, bf16[32,512]{1,0:T(8,128)(2,1)}, u32[]{:S(2)}) copy-start(bf16[32,512]{1,0:T(8,128)(2,1)} %get-tuple-element.25.down_ref.up_ref) | copy-start | bytes 98308
  66.0 1.1 copy-start.5
  66.1 1.1 copy-start.6
  70.2 25.8 %copy-start.1 = (bf16[16,32,512]{2,1,0:T(8,128)(2,1)S(1)}, bf16[16,32,512]{2,1,0:T(8,128)(2,1)}, u32[]{:S(2)}) copy-start(bf16[16,32,512]{2,1,0:T(8,128)(2,1)} %shard_map.67) | copy-start | bytes 1572868
  86.6 9.3 %copy-start.4 = (bf16[32,512]{1,0:T(8,128)(2,1)S(1)}, bf16[32,512]{1,0:T(8,128)(2,1)}, u32[]{:S(2)}) copy-start(bf16[32,512]{1,0:T(8,128)(2,1)} %select_convert_fusion.down_ref.up_ref) | copy-start | bytes 98308
  95.9 1.1 copy-start.9
  96.0 1.1 copy-start.10

commit v6 on v4

--- a/solution.py
+++ b/solution.py
@@ -172,6 +172,168 @@
         ],
         compiler_params=pltpu.CompilerParams(collective_id=collective_id, has_side_effects=True),
     )(x)
+
+
+def row_dev(j):
+    return (j, lax.axis_index("filt"))
+
+
+def filt_dev(j):
+    return (lax.axis_index("rows"), j)
+
+
+def rcopy(src, dst, send, recv, dev):
+    return pltpu.make_async_remote_copy(src, dst, send, recv, device_id=dev, device_id_type=MESH)
+
+
+def each_filt_peer(body):
+    nf = lax.axis_size("filt")
+    me = lax.axis_index("filt")
+
+    def step(k, carry):
+        body(lax.rem(me + k, nf), lax.rem(me + nf - k, nf))
+        return carry
+
+    lax.fori_loop(1, nf, step, 0)
+
+
+def enter(with_filt):
+    nr = lax.axis_size("rows")
+    me = lax.axis_index("rows")
+    barrier = pltpu.get_barrier_semaphore()
+
+    @pl.when(me > 0)
+    def _():
+        pl.semaphore_signal(barrier, 1, device_id=row_dev(me - 1), device_id_type=MESH)
+
+    @pl.when(me < nr - 1)
+    def _():
+        pl.semaphore_signal(barrier, 1, device_id=row_dev(me + 1), device_id_type=MESH)
+
+    count = (me + nr - 1) // nr + (2 * nr - 2 - me) // nr
+    if with_filt:
+        each_filt_peer(lambda j, s: pl.semaphore_signal(barrier, 1, device_id=filt_dev(j), device_id_type=MESH))
+        count = count + lax.axis_size("filt") - 1
+    pl.semaphore_wait(barrier, count)
+
+
+class Halo:
+    def __init__(self, down_src, up_src, from_prev, from_next, sems):
+        self.nr = lax.axis_size("rows")
+        self.me = lax.axis_index("rows")
+        self.down = lambda j: rcopy(down_src, from_prev, sems.at[0], sems.at[1], row_dev(j))
+        self.up = lambda j: rcopy(up_src, from_next, sems.at[2], sems.at[3], row_dev(j))
+        me, nr = self.me, self.nr
+
+        @pl.when(me < nr - 1)
+        def _():
+            self.down(me + 1).start()
+
+        @pl.when(me > 0)
+        def _():
+            self.up(me - 1).start()
+
+        @pl.when(me == 0)
+        def _():
+            from_prev[...] = jnp.zeros(from_prev.shape, from_prev.dtype)
+
+        @pl.when(me == nr - 1)
+        def _():
+            from_next[...] = jnp.zeros(from_next.shape, from_next.dtype)
+
+    def arrived(self):
+        me, nr = self.me, self.nr
+
+        @pl.when(me > 0)
+        def _():
+            self.down(me - 1).wait_recv()
+
+        @pl.when(me < nr - 1)
+        def _():
+            self.up(me + 1).wait_recv()
+
+    def sent(self):
+        me, nr = self.me, self.nr
+
+        @pl.when(me > 0)
+        def _():
+            self.up(me - 1).wait_send()
+
+        @pl.when(me < nr - 1)
+        def _():
+            self.down(me + 1).wait_send()
+
+
+def hidden_kernel(p0, p2, p1, pre_ref, h_ref, from_prev, from_next, hsems, fsend, frecv):
+    mf = lax.axis_index("filt")
+    enter(True)
+    halo = Halo(p0, p2, from_prev, from_next, hsems)
+    halo.arrived()
+    pre = p1[...] + from_prev[...] + from_next[...]
+    pre_ref[...] = pre
+    h_ref[mf] = jnp.maximum(pre, 0.0).astype(h_ref.dtype)
+
+    def out(j, s):
+        return rcopy(h_ref.at[mf], h_ref.at[mf], fsend.at[j], frecv.at[mf], filt_dev(j))
+
+    def inc(j, s):
+        return rcopy(h_ref.at[s], h_ref.at[s], fsend.at[s], frecv.at[s], filt_dev(s))
+
+    each_filt_peer(lambda j, s: out(j, s).start())
+    each_filt_peer(lambda j, s: inc(j, s).wait_recv())
+    each_filt_peer(lambda j, s: out(j, s).wait_send())
+    halo.sent()
+
+
+def output_kernel(p0, p2, p1, feat, og, out_ref, gs_ref, gprev, gnext, from_prev, from_next, sems1, sems2):
+    enter(False)
+    halo = Halo(p0, p2, from_prev, from_next, sems1)
+    halo.arrived()
+    pre = p1[...] + from_prev[...] + from_next[...] + feat[...].astype(jnp.float32)
+    out_ref[...] = jnp.maximum(pre, 0.0).astype(out_ref.dtype)
+    gs_ref[...] = jnp.where(pre > 0, og[...].astype(jnp.float32), 0.0).astype(gs_ref.dtype)
+    halo2 = Halo(gs_ref, gs_ref, gprev, gnext, sems2)
+    halo2.arrived()
+    halo.sent()
+    halo2.sent()
+
+
+def first_grad_kernel(terms, pre_first, gf_ref, gprev, gnext, buf, fsend, frecv, hsems):
+    nf = lax.axis_size("filt")
+    mf = lax.axis_index("filt")
+    enter(True)
+
+    def out(j, s):
+        return rcopy(terms.at[j], buf.at[mf], fsend.at[j], frecv.at[mf], filt_dev(j))
+
+    def inc(j, s):
+        return rcopy(terms.at[s], buf.at[s], fsend.at[s], frecv.at[s], filt_dev(s))
+
+    each_filt_peer(lambda j, s: out(j, s).start())
+    each_filt_peer(lambda j, s: inc(j, s).wait_recv())
+    acc = terms[mf].astype(jnp.float32)
+
+    def add(k, acc):
+        return acc + buf[lax.rem(mf + k, nf)].astype(jnp.float32)
+
+    acc = lax.fori_loop(1, nf, add, acc)
+    gf_ref[...] = jnp.where(pre_first[...] > 0, acc, 0.0).astype(gf_ref.dtype)
+    halo = Halo(gf_ref, gf_ref, gprev, gnext, hsems)
+    halo.arrived()
+    each_filt_peer(lambda j, s: out(j, s).wait_send())
+    halo.sent()
+
+
+def call(kernel, args, outs, scratch, collective_id):
+    spec = pl.BlockSpec(memory_space=pltpu.VMEM)
+    return pl.pallas_call(
+        kernel,
+        out_shape=tuple(jax.ShapeDtypeStruct(shape, dtype) for shape, dtype in outs),
+        in_specs=[spec] * len(args),
+        out_specs=tuple(spec for _ in outs),
+        scratch_shapes=scratch,
+        compiler_params=pltpu.CompilerParams(collective_id=collective_id, has_side_effects=True),
+    )(*args)
 
 
 def exchange(x, axis, mode, collective_id, out_dtype=None):
@@ -206,30 +368,11 @@
     return jnp.pad(value[..., :offset], pad + [(-offset, 0)])
 
 
-def from_prev(value):
-    count = lax.axis_size("rows")
-    return lax.ppermute(value, "rows", [(i, i + 1) for i in range(count - 1)])
-
-
-def from_next(value):
-    count = lax.axis_size("rows")
-    return lax.ppermute(value, "rows", [(i + 1, i) for i in range(count - 1)])
-
-
 def conv_row(weight, row):
     o = weight.shape[0]
     flat = weight.reshape(o, 9, weight.shape[3])
     parts = jnp.einsum("oki,iw->kow", flat, row, preferred_element_type=jnp.float32)
     return [sum(shift_cols(parts[a * 3 + b], b - 1) for b in range(3)) for a in range(3)]
-
-
-def conv_forward(weight, row):
-    p0, p1, p2 = conv_row(weight, row)
-    return p1 + from_prev(p0) + from_next(p2)
-
-
-def grad_rows(grad):
-    return jnp.stack([from_next(grad), grad, from_prev(grad)])
 
 
 def weight_terms(rows3, full_row):
@@ -253,26 +396,44 @@
     feat = features[:, 0, :]
     og = out_grad[:, 0, :]
     n_filt = lax.axis_size("filt")
-    x_row = exchange(feat, "filt", "ag", 1).reshape(-1, feat.shape[1])
-    pre_first = conv_forward(first_weight, x_row)
-    hidden = jnp.maximum(pre_first, 0.0).astype(jnp.bfloat16)
-    h_row = exchange(hidden, "filt", "ag", 2).reshape(-1, hidden.shape[1])
-    pre_second = conv_forward(second_weight, h_row) + feat.astype(jnp.float32)
-    block_out = jnp.maximum(pre_second, 0.0).astype(jnp.bfloat16)
-    grad_second = jnp.where(pre_second > 0, og.astype(jnp.float32), 0.0).astype(jnp.bfloat16)
-    gs3 = grad_rows(grad_second)
-    terms = hidden_terms(second_weight, gs3)
-    hidden_grad = exchange(
-        terms.astype(jnp.bfloat16).reshape(n_filt, -1, terms.shape[1]), "filt", "rs", 3, jnp.float32
+    blk = feat.shape
+    f32, bf16 = jnp.float32, jnp.bfloat16
+    x_row = exchange(feat, "filt", "ag", 1).reshape(-1, blk[1])
+    p0, p1, p2 = conv_row(first_weight, x_row)
+    pre_first, h_all = call(
+        hidden_kernel,
+        (p0, p2, p1),
+        [(blk, f32), ((n_filt,) + blk, bf16)],
+        [pltpu.VMEM(blk, f32), pltpu.VMEM(blk, f32), pltpu.SemaphoreType.DMA((4,)),
+         pltpu.SemaphoreType.DMA((n_filt,)), pltpu.SemaphoreType.DMA((n_filt,))],
+        2,
     )
-    grad_first = jnp.where(pre_first > 0, hidden_grad, 0.0).astype(jnp.bfloat16)
-    gf3 = grad_rows(grad_first)
+    h_row = h_all.reshape(-1, blk[1])
+    q0, q1, q2 = conv_row(second_weight, h_row)
+    block_out, grad_second, gs_prev, gs_next = call(
+        output_kernel,
+        (q0, q2, q1, feat, og),
+        [(blk, bf16)] * 4,
+        [pltpu.VMEM(blk, f32), pltpu.VMEM(blk, f32), pltpu.SemaphoreType.DMA((4,)), pltpu.SemaphoreType.DMA((4,))],
+        3,
+    )
+    gs3 = jnp.stack([gs_next, grad_second, gs_prev])
+    terms = hidden_terms(second_weight, gs3).astype(bf16).reshape((n_filt,) + blk)
+    grad_first, gf_prev, gf_next = call(
+        first_grad_kernel,
+        (terms, pre_first),
+        [(blk, bf16)] * 3,
+        [pltpu.VMEM((n_filt,) + blk, bf16), pltpu.SemaphoreType.DMA((n_filt,)),
+         pltpu.SemaphoreType.DMA((n_filt,)), pltpu.SemaphoreType.DMA((4,))],
+        4,
+    )
+    gf3 = jnp.stack([gf_next, grad_first, gf_prev])
     second_local = weight_terms(gs3, h_row)
     first_local = weight_terms(gf3, x_row)
     both = jnp.stack([first_local, second_local])
     n_rows = lax.axis_size("rows")
-    summed = row_sum(both.astype(jnp.bfloat16).reshape(n_rows, -1, 128), 0)
-    first_grad, second_grad = summed.astype(jnp.float32).reshape(both.shape)
+    summed = row_sum(both.astype(bf16).reshape(n_rows, -1, 128), 0)
+    first_grad, second_grad = summed.astype(f32).reshape(both.shape)
     return (block_out[:, None, :], first_grad, second_grad)
 
 

time: 161 us -> 146 us (0.907)
  Pallas kernels: 107 us -> 127 us
  waiting for transfers between devices: 18.6 us -> 0 us
  starting transfers between devices: 18 us -> 0 us
  matrix products: 6.37 us -> 8.04 us
    pallas_call x0 -> x3, Pallas kernels: none -> 48.2 us  [call(): pl.pallas_call(kernel, out_shape=tuple((jax.ShapeDtypeStruct(shape, dtype...]
    pallas_call x3 -> x1, Pallas kernels: 48.2 us -> 18.4 us  [exchange(): pl.pallas_call(functools.partial(exchange_kernel, axis, n, mode), out_sha...]
    ppermute x8 -> x0, waiting for transfers between devices: 18.6 us -> none  [the longest x4 17.2 us: from_next(): return lax.ppermute(value, 'rows', [(i + 1, i) for i in range(count - 1)])]
    ppermute x8 -> x0, starting transfers between devices: 18 us -> none  [the longest x4 12.9 us: from_prev(): return lax.ppermute(value, 'rows', [(i, i + 1) for i in range(count - 1)])]
    dot_general x6, matrix products: 1.75 us -> 3.4 us  [weight_terms(): jnp.einsum('aow,iw->oai', moved, full_row, preferred_element_type=jnp.flo...]
    convert_element_type x3 -> x0, other arithmetic: 1.65 us -> none  [the longest x1 0.85 us: per_device(): grad_first = jnp.where(pre_first > 0, hidden_grad, 0.0).astype(jnp.bfloat16)]
    unnamed x14 -> x25, local copies, waits for them, and re-layouts: 2.03 us -> 3.61 us
  transfers between devices with their start and end apart: 8 -> 0, of which waited for: 6 -> 0; matrix products, arithmetic and copies ran while one was open for 1% -> 0% of each run, Pallas kernels for 0% -> 0%
where the time goes in v6:
time: 146 us
  Pallas kernels  127 us (87%)
  local copies, waits for them, and re-layouts  8.05 us (6%)
  matrix products  8.04 us (6%)
  other arithmetic  1.69 us (1%)
    pallas_call x1, Pallas kernels, row_sum(): pl.pallas_call(functools.partial(row_sum_kernel, n), out_shape=jax.ShapeD...  60.1 us
    pallas_call x3, Pallas kernels, call(): pl.pallas_call(kernel, out_shape=tuple((jax.ShapeDtypeStruct(shape, dtype...  48.2 us
    pallas_call x1, Pallas kernels, exchange(): pl.pallas_call(functools.partial(exchange_kernel, axis, n, mode), out_sha...  18.4 us
    unnamed x25, local copies, waits for them, and re-layouts  3.61 us
    dot_general x6, matrix products, weight_terms(): jnp.einsum('aow,iw->oai', moved, full_row, preferred_element_type=jnp.flo...  3.4 us

profile of v6, /device:TPU:6, one launch (start us, length us, event | category | flops | bytes accessed | tf_op | source)
XLA Modules:
  0.0 145.5 jit_solution(11967685033848148783)
XLA Ops:
  0.6 0.0 copy-start
  0.6 1.0 copy-done
  1.6 18.4 %shard_map.67 = bf16[16,32,512]{2,1,0:T(8,128)(2,1)} custom-call(bf16[32,512]{1,0:T(8,128)(2,1)} %bitcast.199), custom_call_target="tpu_custom_call" | custom-call | tf_op jit(solution)/shard_map/pallas_call | solution.py:352
  20.0 1.4 convolution_bitcast_fusion.4
  21.4 0.1 slice.172
  21.5 0.1 slice.167
  21.6 0.1 slice.162
  21.7 0.0 copy-start.6
  21.7 0.8 fusion.26
  22.5 16.8 %shard_map.68 = (f32[32,512]{1,0:T(8,128)}, bf16[16,32,512]{2,1,0:T(8,128)(2,1)}) custom-call(f32[32,512]{1,0:T(8,128)} %get-tuple-element.40.p0, f32[32,512]{1,0:T(8,128)} %get-tuple-element.39.p2, f32[32,512]{1,0:T(8,128)} %get-tuple-element.38.p1), custom_call_target="tpu_custom_call" | custom-call | tf_op jit(solution)/shard_map/pallas_call | solution.py:329
  39.3 0.0 copy-done.6
  39.3 1.4 convolution_bitcast_fusion.3
  40.7 0.1 slice.187
  40.8 0.1 slice.182
  40.9 0.1 slice.177
  41.0 0.0 copy-start.2
  41.0 0.8 fusion.20
  41.7 12.0 %shard_map.69 = (bf16[32,512]{1,0:T(8,128)(2,1)}, bf16[32,512]{1,0:T(8,128)(2,1)}, bf16[32,512]{1,0:T(8,128)(2,1)}, bf16[32,512]{1,0:T(8,128)(2,1)}) custom-call(f32[32,512]{1,0:T(8,128)} %get-tuple-element.31.p0, f32[32,512]{1,0:T(8,128)} %get-tuple-element.30.p2, f32[32,512]{1,0:T(8,128)} %get-tuple-element.29.p1, bf16[32,512]{1,0:T(8,128)(2,1)} %bitcast.200, ...), custom_call_target="tpu_custom_call" | custom-call | tf_op jit(solution)/shard_map/pallas_call | solution.py:329
  53.8 0.0 copy-done.2
  53.8 0.0 copy-start.3
  53.8 0.0 copy-start.4
  53.8 0.0 copy-start.5
  53.8 1.1 fusion.7
  54.9 0.0 copy-done.3
  54.9 0.0 copy-done.4
  55.0 0.0 copy-done.5
  55.0 0.1 fusion.37
  55.1 0.3 fusion.6
  55.4 0.3 fusion.8
  55.7 0.3 convolution_bitcast_fusion.2
  56.0 0.3 slice.188
  56.4 0.3 convolution_bitcast_fusion
  56.7 1.2 fusion.2
  57.9 0.0 copy-start.1
  57.9 19.4 %shard_map.70 = (bf16[32,512]{1,0:T(8,128)(2,1)}, bf16[32,512]{1,0:T(8,128)(2,1)}, bf16[32,512]{1,0:T(8,128)(2,1)}) custom-call(bf16[16,32,512]{2,1,0:T(8,128)(2,1)} %bitcast.170, f32[32,512]{1,0:T(8,128)} %get-tuple-element.17.pre_first), custom_call_target="tpu_custom_call" | custom-call | tf_op jit(solution)/shard_map/pallas_call | solution.py:329
  77.3 0.0 copy-done.1
  77.3 0.0 copy-start.7
  77.4 0.0 copy-start.8
  77.4 0.0 copy-start.9
  77.4 1.1 fusion.4
  78.5 0.0 copy-done.7
  78.5 0.0 copy-done.8
  78.5 0.0 copy-done.9
  78.6 0.1 fusion.36
  78.7 0.3 fusion.3
  79.0 0.3 fusion.5
  79.3 0.1 maximum_bitcast_fusion
  79.3 0.1 pad_maximum_fusion
  79.4 0.5 copy.16
  79.9 1.2 convert_element_type.36.x_ref
  81.2 60.1 %shard_map.71 = bf16[32,72,128]{2,1,0:T(8,128)(2,1)} custom-call(bf16[32,72,128]{2,1,0:T(8,128)(2,1)} %convert_element_type.36.x_ref), custom_call_target="tpu_custom_call" | custom-call | tf_op jit(solution)/shard_map/pallas_call | solution.py:162
  141.3 1.1 fusion.35
  142.4 0.2 unstack.15
  142.7 1.0 copy.18
  143.7 0.2 unstack.13
  143.9 0.0 copy-start.10
  143.9 1.0 copy.17
  144.9 0.0 copy-done.10
  144.9 0.6 copy.23
  (4 shorter events, 0.1 us)
Async XLA Ops:
  0.6 1.0 copy-start
  21.7 17.6 %copy-start.6 = (bf16[32,3,3,512]{3,0,2,1:T(8,128)(2,1)S(1)}, bf16[32,3,3,512]{3,0,2,1:T(8,128)(2,1)}, u32[]{:S(2)}) copy-start(bf16[32,3,3,512]{3,0,2,1:T(8,128)(2,1)} %param.6) | copy-start | bytes 884740
  41.0 12.8 %copy-start.2 = (bf16[16,32,512]{2,1,0:T(8,128)(2,1)S(1)}, bf16[16,32,512]{2,1,0:T(8,128)(2,1)}, u32[]{:S(2)}) copy-start(bf16[16,32,512]{2,1,0:T(8,128)(2,1)} %get-tuple-element.12) | copy-start | bytes 1572868
  53.8 1.2 copy-start.3
  53.8 1.2 copy-start.4
  53.8 1.2 copy-start.5
  57.9 19.4 %copy-start.1 = (bf16[16,32,512]{2,1,0:T(8,128)(2,1)S(1)}, bf16[16,32,512]{2,1,0:T(8,128)(2,1)}, u32[]{:S(2)}) copy-start(bf16[16,32,512]{2,1,0:T(8,128)(2,1)} %shard_map.67) | copy-start | bytes 1572868
  77.3 1.2 copy-start.7
  77.4 1.2 copy-start.8
  77.4 1.2 copy-start.9
  143.9 1.0 copy-start.10

commit v7 on v6

--- a/solution.py
+++ b/solution.py
@@ -87,7 +87,29 @@
         each_peer(lambda j, s: copy(j, s).wait_send())
 
 
+def row_sum_peers(n, signal):
+    zn = n // 2
+    me = lax.axis_index("rows")
+    my_z = lax.rem(me, zn)
+    mine = (me // zn) * zn
+    signal(lax.rem(me + zn, n))
+
+    def step(k, carry):
+        signal(mine + lax.rem(my_z + k, zn))
+        return carry
+
+    lax.fori_loop(1, zn, step, 0)
+    return zn
+
+
 def row_sum_kernel(n, x_ref, out_ref, half_buf, half_b, part_buf, sems):
+    barrier = pltpu.get_barrier_semaphore()
+    count = row_sum_peers(n, lambda j: pl.semaphore_signal(barrier, 1, device_id=(j, lax.axis_index("filt")), device_id_type=MESH))
+    pl.semaphore_wait(barrier, count)
+    row_sum_body(n, x_ref, out_ref, half_buf, half_b, part_buf, sems)
+
+
+def row_sum_body(n, x_ref, out_ref, half_buf, half_b, part_buf, sems, between=None):
     zn = n // 2
     me = lax.axis_index("rows")
     my_y, my_z = me // zn, lax.rem(me, zn)
@@ -104,16 +126,13 @@
 
         lax.fori_loop(1, zn, step, 0)
 
-    barrier = pltpu.get_barrier_semaphore()
-    pl.semaphore_signal(barrier, 1, device_id=dev(other), device_id_type=MESH)
-    each_z(lambda j, s: pl.semaphore_signal(barrier, 1, device_id=dev(mine + j), device_id_type=MESH))
-    pl.semaphore_wait(barrier, zn)
-
     def rcopy(src, dst, send, recv, j):
         return pltpu.make_async_remote_copy(src, dst, send, recv, device_id=dev(j), device_id_type=MESH)
 
     swap = rcopy(x_ref.at[pl.ds(theirs, zn)], half_buf, sems.at[0, 0], sems.at[0, 1], other)
     swap.start()
+    if between is not None:
+        between()
     swap.wait_recv()
 
     def add_half(t, carry):
@@ -197,7 +216,7 @@
     lax.fori_loop(1, nf, step, 0)
 
 
-def enter(with_filt):
+def enter(with_filt, with_row_sum=False):
     nr = lax.axis_size("rows")
     me = lax.axis_index("rows")
     barrier = pltpu.get_barrier_semaphore()
@@ -214,6 +233,10 @@
     if with_filt:
         each_filt_peer(lambda j, s: pl.semaphore_signal(barrier, 1, device_id=filt_dev(j), device_id_type=MESH))
         count = count + lax.axis_size("filt") - 1
+    if with_row_sum:
+        count = count + row_sum_peers(
+            nr, lambda j: pl.semaphore_signal(barrier, 1, device_id=row_dev(j), device_id_type=MESH)
+        )
     pl.semaphore_wait(barrier, count)
 
 
@@ -298,10 +321,10 @@
     halo2.sent()
 
 
-def first_grad_kernel(terms, pre_first, gf_ref, gprev, gnext, buf, fsend, frecv, hsems):
+def first_grad_kernel(terms, pre_first, xs, gf_ref, gprev, gnext, s_out, buf, fsend, frecv, hsems, *row_sum_refs):
     nf = lax.axis_size("filt")
     mf = lax.axis_index("filt")
-    enter(True)
+    enter(True, True)
 
     def out(j, s):
         return rcopy(terms.at[j], buf.at[mf], fsend.at[j], frecv.at[mf], filt_dev(j))
@@ -310,15 +333,21 @@
         return rcopy(terms.at[s], buf.at[s], fsend.at[s], frecv.at[s], filt_dev(s))
 
     each_filt_peer(lambda j, s: out(j, s).start())
-    each_filt_peer(lambda j, s: inc(j, s).wait_recv())
-    acc = terms[mf].astype(jnp.float32)
-
-    def add(k, acc):
-        return acc + buf[lax.rem(mf + k, nf)].astype(jnp.float32)
-
-    acc = lax.fori_loop(1, nf, add, acc)
-    gf_ref[...] = jnp.where(pre_first[...] > 0, acc, 0.0).astype(gf_ref.dtype)
-    halo = Halo(gf_ref, gf_ref, gprev, gnext, hsems)
+    halos = []
+
+    def reduce_filt():
+        each_filt_peer(lambda j, s: inc(j, s).wait_recv())
+        acc = terms[mf].astype(jnp.float32)
+
+        def add(k, acc):
+            return acc + buf[lax.rem(mf + k, nf)].astype(jnp.float32)
+
+        acc = lax.fori_loop(1, nf, add, acc)
+        gf_ref[...] = jnp.where(pre_first[...] > 0, acc, 0.0).astype(gf_ref.dtype)
+        halos.append(Halo(gf_ref, gf_ref, gprev, gnext, hsems))
+
+    row_sum_body(lax.axis_size("rows"), xs, s_out, *row_sum_refs, between=reduce_filt)
+    halo = halos[0]
     halo.arrived()
     each_filt_peer(lambda j, s: out(j, s).wait_send())
     halo.sent()
@@ -419,21 +448,24 @@
     )
     gs3 = jnp.stack([gs_next, grad_second, gs_prev])
     terms = hidden_terms(second_weight, gs3).astype(bf16).reshape((n_filt,) + blk)
-    grad_first, gf_prev, gf_next = call(
+    n_rows = lax.axis_size("rows")
+    second_local = weight_terms(gs3, h_row)
+    xs = second_local.astype(bf16).reshape(n_rows, -1, 128)
+    half = (n_rows // 2,) + xs.shape[1:]
+    grad_first, gf_prev, gf_next, second_sum = call(
         first_grad_kernel,
-        (terms, pre_first),
-        [(blk, bf16)] * 3,
+        (terms, pre_first, xs),
+        [(blk, bf16)] * 3 + [(xs.shape, bf16)],
         [pltpu.VMEM((n_filt,) + blk, bf16), pltpu.SemaphoreType.DMA((n_filt,)),
-         pltpu.SemaphoreType.DMA((n_filt,)), pltpu.SemaphoreType.DMA((4,))],
+         pltpu.SemaphoreType.DMA((n_filt,)), pltpu.SemaphoreType.DMA((4,)),
+         pltpu.VMEM(half, bf16), pltpu.VMEM(half, bf16), pltpu.VMEM(half, bf16), pltpu.SemaphoreType.DMA((6, half[0]))],
         4,
     )
     gf3 = jnp.stack([gf_next, grad_first, gf_prev])
-    second_local = weight_terms(gs3, h_row)
     first_local = weight_terms(gf3, x_row)
-    both = jnp.stack([first_local, second_local])
-    n_rows = lax.axis_size("rows")
-    summed = row_sum(both.astype(bf16).reshape(n_rows, -1, 128), 0)
-    first_grad, second_grad = summed.astype(f32).reshape(both.shape)
+    first_sum = row_sum(first_local.astype(bf16).reshape(n_rows, -1, 128), 0)
+    first_grad = first_sum.astype(f32).reshape(first_local.shape)
+    second_grad = second_sum.astype(f32).reshape(second_local.shape)
     return (block_out[:, None, :], first_grad, second_grad)
 
 

time: 146 us -> 160 us (1.096)
  Pallas kernels: 127 us -> 139 us
    pallas_call x3, Pallas kernels: 48.2 us -> 80.5 us  [call(): pl.pallas_call(kernel, out_shape=tuple((jax.ShapeDtypeStruct(shape, dtype...]
    pallas_call x1, Pallas kernels: 60.1 us -> 39.9 us  [row_sum(): pl.pallas_call(functools.partial(row_sum_kernel, n), out_shape=jax.ShapeD...]
    another operation x4 -> x2, local copies, waits for them, and re-layouts: 2.11 us -> 0.51 us  [weight_terms(): return jnp.stack(cols, axis=2)]
    unnamed x25 -> x27, local copies, waits for them, and re-layouts: 3.61 us -> 3.62 us
where the time goes in v7:
time: 160 us; the launch traced here: 158 us
  Pallas kernels  139 us (87%)
  local copies, waits for them, and re-layouts  8.72 us (5%)
  matrix products  8.03 us (5%)
  other arithmetic  1.65 us (1%)
    pallas_call x3, Pallas kernels, call(): pl.pallas_call(kernel, out_shape=tuple((jax.ShapeDtypeStruct(shape, dtype...  80.5 us
    pallas_call x1, Pallas kernels, row_sum(): pl.pallas_call(functools.partial(row_sum_kernel, n), out_shape=jax.ShapeD...  39.9 us
    pallas_call x1, Pallas kernels, exchange(): pl.pallas_call(functools.partial(exchange_kernel, axis, n, mode), out_sha...  18.4 us
    unnamed x27, local copies, waits for them, and re-layouts  3.62 us
    dot_general x6, matrix products, weight_terms(): jnp.einsum('aow,iw->oai', moved, full_row, preferred_element_type=jnp.flo...  3.4 us

profile of v7, /device:TPU:6, one launch (start us, length us, event | category | flops | bytes accessed | tf_op | source)
XLA Modules:
  0.0 158.2 jit_solution(7570029789215255499)
XLA Ops:
  0.6 0.0 copy-start
  0.6 1.0 copy-done
  1.6 18.4 %shard_map.67 = bf16[16,32,512]{2,1,0:T(8,128)(2,1)} custom-call(bf16[32,512]{1,0:T(8,128)(2,1)} %bitcast.195), custom_call_target="tpu_custom_call" | custom-call | tf_op jit(solution)/shard_map/pallas_call | solution.py:381
  20.0 1.4 convolution_bitcast_fusion.4
  21.4 0.1 slice.170
  21.5 0.1 slice.165
  21.6 0.1 slice.160
  21.7 0.0 copy-start.7
  21.7 0.8 fusion.26
  22.4 16.8 %shard_map.68 = (f32[32,512]{1,0:T(8,128)}, bf16[16,32,512]{2,1,0:T(8,128)(2,1)}) custom-call(f32[32,512]{1,0:T(8,128)} %get-tuple-element.40.p0, f32[32,512]{1,0:T(8,128)} %get-tuple-element.39.p2, f32[32,512]{1,0:T(8,128)} %get-tuple-element.38.p1), custom_call_target="tpu_custom_call" | custom-call | tf_op jit(solution)/shard_map/pallas_call | solution.py:358
  39.3 0.0 copy-done.7
  39.3 1.4 convolution_bitcast_fusion.3
  40.7 0.1 slice.185
  40.8 0.1 slice.180
  40.9 0.1 slice.175
  41.0 0.0 copy-start.2
  41.0 0.8 fusion.20
  41.7 12.0 %shard_map.69 = (bf16[32,512]{1,0:T(8,128)(2,1)}, bf16[32,512]{1,0:T(8,128)(2,1)}, bf16[32,512]{1,0:T(8,128)(2,1)}, bf16[32,512]{1,0:T(8,128)(2,1)}) custom-call(f32[32,512]{1,0:T(8,128)} %get-tuple-element.31.p0, f32[32,512]{1,0:T(8,128)} %get-tuple-element.30.p2, f32[32,512]{1,0:T(8,128)} %get-tuple-element.29.p1, bf16[32,512]{1,0:T(8,128)(2,1)} %bitcast.196, ...), custom_call_target="tpu_custom_call" | custom-call | tf_op jit(solution)/shard_map/pallas_call | solution.py:358
  53.8 0.0 copy-done.2
  53.8 0.0 copy-start.3
  53.8 0.0 copy-start.4
  53.8 0.0 copy-start.5
  53.8 1.1 fusion.4
  54.9 0.0 copy-done.3
  55.0 0.0 copy-done.4
  55.0 0.0 copy-done.5
  55.0 0.1 fusion.36
  55.1 0.3 fusion.3
  55.4 0.3 fusion.5
  55.7 0.3 copy.17
  56.0 1.0 convert_element_type.40.xs
  57.0 0.3 convolution_bitcast_fusion.2
  57.3 0.3 slice.186
  57.7 0.3 convolution_bitcast_fusion
  58.0 1.2 fusion.2
  59.2 0.0 copy-start.1
  59.2 51.6 %shard_map.70 = (bf16[32,512]{1,0:T(8,128)(2,1)}, bf16[32,512]{1,0:T(8,128)(2,1)}, bf16[32,512]{1,0:T(8,128)(2,1)}, bf16[32,36,128]{2,1,0:T(8,128)(2,1)}) custom-call(bf16[16,32,512]{2,1,0:T(8,128)(2,1)} %bitcast.166, f32[32,512]{1,0:T(8,128)} %get-tuple-element.18.pre_first, bf16[32,36,128]{2,1,0:T(8,128)(2,1)} %convert_element_type.40.xs), custom_call_target="tpu_custom_call" | custom-call | tf_op jit(solution)/shard_map/pallas_call | solution.py:358
  110.9 0.0 copy-done.1
  110.9 0.0 copy-start.8
  110.9 0.0 copy-start.9
  110.9 0.0 copy-start.10
  110.9 1.1 fusion.7
  112.0 0.0 copy-done.8
  112.0 0.0 copy-done.9
  112.0 0.0 copy-done.10
  112.1 0.1 fusion.35
  112.2 0.3 fusion.6
  112.5 0.3 fusion.8
  112.8 0.3 copy.18
  113.1 1.0 convert_element_type.41.x_ref
  114.1 39.9 %shard_map.71 = bf16[32,36,128]{2,1,0:T(8,128)(2,1)} custom-call(bf16[32,36,128]{2,1,0:T(8,128)(2,1)} %convert_element_type.41.x_ref), custom_call_target="tpu_custom_call" | custom-call | tf_op jit(solution)/shard_map/pallas_call | solution.py:181
  154.0 1.3 reshape.49
  155.3 0.0 copy-start.6
  155.3 1.0 copy.19
  156.3 0.0 copy-done.6
  156.3 0.2 reshape.51
  156.6 0.0 copy-start.11
  156.6 1.0 copy.20
  157.6 0.0 copy-done.11
  157.6 0.6 copy.25
  (6 shorter events, 0.2 us)
Async XLA Ops:
  0.6 1.0 copy-start
  21.7 17.6 %copy-start.7 = (bf16[32,3,3,512]{3,0,2,1:T(8,128)(2,1)S(1)}, bf16[32,3,3,512]{3,0,2,1:T(8,128)(2,1)}, u32[]{:S(2)}) copy-start(bf16[32,3,3,512]{3,0,2,1:T(8,128)(2,1)} %param.6) | copy-start | bytes 884740
  41.0 12.8 %copy-start.2 = (bf16[16,32,512]{2,1,0:T(8,128)(2,1)S(1)}, bf16[16,32,512]{2,1,0:T(8,128)(2,1)}, u32[]{:S(2)}) copy-start(bf16[16,32,512]{2,1,0:T(8,128)(2,1)} %get-tuple-element.13) | copy-start | bytes 1572868
  53.8 1.2 copy-start.3
  53.8 1.2 copy-start.4
  53.8 1.2 copy-start.5
  59.2 51.6 %copy-start.1 = (bf16[16,32,512]{2,1,0:T(8,128)(2,1)S(1)}, bf16[16,32,512]{2,1,0:T(8,128)(2,1)}, u32[]{:S(2)}) copy-start(bf16[16,32,512]{2,1,0:T(8,128)(2,1)} %shard_map.67) | copy-start | bytes 1572868
  110.9 1.2 copy-start.8
  110.9 1.2 copy-start.9
  110.9 1.2 copy-start.10
  155.3 1.0 copy-start.6
  156.6 1.0 copy-start.11

commit v8 on v6

--- a/solution.py
+++ b/solution.py
@@ -87,91 +87,155 @@
         each_peer(lambda j, s: copy(j, s).wait_send())
 
 
-def row_sum_kernel(n, x_ref, out_ref, half_buf, half_b, part_buf, sems):
-    zn = n // 2
-    me = lax.axis_index("rows")
-    my_y, my_z = me // zn, lax.rem(me, zn)
-    other = lax.rem(me + zn, n)
-    mine, theirs = my_y * zn, (1 - my_y) * zn
-
-    def dev(j):
-        return (j, lax.axis_index("filt"))
-
-    def each_z(body):
+class RowSum:
+    def __init__(self, n, x_ref, out_ref, half_buf, half_b, part_buf, sems):
+        self.zn = zn = n // 2
+        self.me = me = lax.axis_index("rows")
+        my_y, self.my_z = me // zn, lax.rem(me, zn)
+        self.other = lax.rem(me + zn, n)
+        self.mine, self.theirs = my_y * zn, (1 - my_y) * zn
+        self.x_ref, self.out_ref, self.half_buf, self.half_b, self.part_buf, self.sems = (
+            x_ref, out_ref, half_buf, half_b, part_buf, sems)
+
+    def rcopy(self, src, dst, send, recv, j):
+        return pltpu.make_async_remote_copy(
+            src, dst, send, recv, device_id=(j, lax.axis_index("filt")), device_id_type=MESH
+        )
+
+    def each_z(self, body):
+        zn, my_z = self.zn, self.my_z
+
         def step(k, carry):
             body(lax.rem(my_z + k, zn), lax.rem(my_z + zn - k, zn))
             return carry
 
         lax.fori_loop(1, zn, step, 0)
 
+    def swap(self):
+        return self.rcopy(self.x_ref.at[pl.ds(self.theirs, self.zn)], self.half_buf, self.sems.at[0, 0],
+                          self.sems.at[0, 1], self.other)
+
+    def part_out(self, j, s):
+        return self.rcopy(self.half_b.at[j], self.part_buf.at[self.my_z], self.sems.at[1, j],
+                          self.sems.at[2, self.my_z], self.mine + j)
+
+    def part_in(self, j, s):
+        return self.rcopy(self.half_b.at[s], self.part_buf.at[s], self.sems.at[1, s], self.sems.at[2, s],
+                          self.mine + s)
+
+    def sum_out(self, j, s):
+        me = self.me
+        return self.rcopy(self.out_ref.at[me], self.out_ref.at[me], self.sems.at[3, j], self.sems.at[4, self.my_z],
+                          self.mine + j)
+
+    def sum_in(self, j, s):
+        c = self.mine + s
+        return self.rcopy(self.out_ref.at[c], self.out_ref.at[c], self.sems.at[3, s], self.sems.at[4, s], c)
+
+    def back(self):
+        half = pl.ds(self.mine, self.zn)
+        return self.rcopy(self.out_ref.at[half], self.out_ref.at[half], self.sems.at[5, 0], self.sems.at[5, 1],
+                          self.other)
+
+    def s1_start(self):
+        self.swap().start()
+
+    def s1_finish(self):
+        self.swap().wait_recv()
+        x_ref, half_buf, half_b, mine = self.x_ref, self.half_buf, self.half_b, self.mine
+
+        def add_half(t, carry):
+            half_b[t] = (x_ref[mine + t].astype(jnp.float32) + half_buf[t].astype(jnp.float32)).astype(half_b.dtype)
+            return carry
+
+        lax.fori_loop(0, self.zn, add_half, 0)
+        self.swap().wait_send()
+
+    def s2_start(self):
+        self.each_z(lambda j, s: self.part_out(j, s).start())
+
+    def s2_finish(self):
+        self.each_z(lambda j, s: self.part_in(j, s).wait_recv())
+        zn, my_z, part_buf = self.zn, self.my_z, self.part_buf
+        acc = self.x_ref[self.me].astype(jnp.float32) + self.half_buf[my_z].astype(jnp.float32)
+
+        def add_part(k, acc):
+            return acc + part_buf[lax.rem(my_z + k, zn)].astype(jnp.float32)
+
+        acc = lax.fori_loop(1, zn, add_part, acc)
+        self.out_ref[self.me] = acc.astype(self.out_ref.dtype)
+        self.each_z(lambda j, s: self.part_out(j, s).wait_send())
+
+    def s3_start(self):
+        self.each_z(lambda j, s: self.sum_out(j, s).start())
+
+    def s3_finish(self):
+        self.each_z(lambda j, s: self.sum_in(j, s).wait_recv())
+        self.each_z(lambda j, s: self.sum_out(j, s).wait_send())
+
+    def s4_start(self):
+        self.back().start()
+
+    def s4_finish(self):
+        self.back().wait_recv()
+        self.back().wait_send()
+
+
+def row_sum_kernel(n, xa, xb, oa, ob, *scratch):
+    zn = n // 2
+    me = lax.axis_index("rows")
+    my_z = lax.rem(me, zn)
+    mine = (me // zn) * zn
+
+    def dev(j):
+        return (j, lax.axis_index("filt"))
+
     barrier = pltpu.get_barrier_semaphore()
-    pl.semaphore_signal(barrier, 1, device_id=dev(other), device_id_type=MESH)
-    each_z(lambda j, s: pl.semaphore_signal(barrier, 1, device_id=dev(mine + j), device_id_type=MESH))
+    pl.semaphore_signal(barrier, 1, device_id=dev(lax.rem(me + zn, n)), device_id_type=MESH)
+
+    def greet(k, carry):
+        pl.semaphore_signal(barrier, 1, device_id=dev(mine + lax.rem(my_z + k, zn)), device_id_type=MESH)
+        return carry
+
+    lax.fori_loop(1, zn, greet, 0)
     pl.semaphore_wait(barrier, zn)
-
-    def rcopy(src, dst, send, recv, j):
-        return pltpu.make_async_remote_copy(src, dst, send, recv, device_id=dev(j), device_id_type=MESH)
-
-    swap = rcopy(x_ref.at[pl.ds(theirs, zn)], half_buf, sems.at[0, 0], sems.at[0, 1], other)
-    swap.start()
-    swap.wait_recv()
-
-    def add_half(t, carry):
-        half_b[t] = (x_ref[mine + t].astype(jnp.float32) + half_buf[t].astype(jnp.float32)).astype(half_b.dtype)
-        return carry
-
-    lax.fori_loop(0, zn, add_half, 0)
-    swap.wait_send()
-
-    def part_out(j, s):
-        return rcopy(half_b.at[j], part_buf.at[my_z], sems.at[1, j], sems.at[2, my_z], mine + j)
-
-    def part_in(j, s):
-        return rcopy(half_b.at[s], part_buf.at[s], sems.at[1, s], sems.at[2, s], mine + s)
-
-    each_z(lambda j, s: part_out(j, s).start())
-    each_z(lambda j, s: part_in(j, s).wait_recv())
-    acc = (x_ref[me].astype(jnp.float32) + half_buf[my_z].astype(jnp.float32))
-
-    def add_part(k, acc):
-        return acc + part_buf[lax.rem(my_z + k, zn)].astype(jnp.float32)
-
-    acc = lax.fori_loop(1, zn, add_part, acc)
-    out_ref[me] = acc.astype(out_ref.dtype)
-    each_z(lambda j, s: part_out(j, s).wait_send())
-
-    def sum_out(j, s):
-        return rcopy(out_ref.at[me], out_ref.at[me], sems.at[3, j], sems.at[4, my_z], mine + j)
-
-    def sum_in(j, s):
-        return rcopy(out_ref.at[mine + s], out_ref.at[mine + s], sems.at[3, s], sems.at[4, s], mine + s)
-
-    each_z(lambda j, s: sum_out(j, s).start())
-    each_z(lambda j, s: sum_in(j, s).wait_recv())
-    each_z(lambda j, s: sum_out(j, s).wait_send())
-    back = rcopy(out_ref.at[pl.ds(mine, zn)], out_ref.at[pl.ds(mine, zn)], sems.at[5, 0], sems.at[5, 1], other)
-    back.start()
-    back.wait_recv()
-    back.wait_send()
-
-
-def row_sum(x, collective_id):
-    n = x.shape[0]
+    a = RowSum(n, xa, oa, *scratch[:4])
+    b = RowSum(n, xb, ob, *scratch[4:])
+    a.s1_start()
+    a.s1_finish()
+    a.s2_start()
+    b.s1_start()
+    b.s1_finish()
+    b.s2_start()
+    a.s2_finish()
+    a.s3_start()
+    b.s2_finish()
+    b.s3_start()
+    a.s3_finish()
+    a.s4_start()
+    b.s3_finish()
+    b.s4_start()
+    a.s4_finish()
+    b.s4_finish()
+
+
+def row_sum(xa, xb, collective_id):
+    n = xa.shape[0]
     zn = n // 2
-    blk = x.shape[1:]
+    spec = pl.BlockSpec(memory_space=pltpu.VMEM)
+    scratch = []
+    for x in (xa, xb):
+        blk = (zn,) + x.shape[1:]
+        scratch += [pltpu.VMEM(blk, x.dtype), pltpu.VMEM(blk, x.dtype), pltpu.VMEM(blk, x.dtype),
+                    pltpu.SemaphoreType.DMA((6, zn))]
     return pl.pallas_call(
         functools.partial(row_sum_kernel, n),
-        out_shape=jax.ShapeDtypeStruct(x.shape, x.dtype),
-        in_specs=[pl.BlockSpec(memory_space=pltpu.VMEM)],
-        out_specs=pl.BlockSpec(memory_space=pltpu.VMEM),
-        scratch_shapes=[
-            pltpu.VMEM((zn,) + blk, x.dtype),
-            pltpu.VMEM((zn,) + blk, x.dtype),
-            pltpu.VMEM((zn,) + blk, x.dtype),
-            pltpu.SemaphoreType.DMA((6, zn)),
-        ],
+        out_shape=(jax.ShapeDtypeStruct(xa.shape, xa.dtype), jax.ShapeDtypeStruct(xb.shape, xb.dtype)),
+        in_specs=[spec, spec],
+        out_specs=(spec, spec),
+        scratch_shapes=scratch,
         compiler_params=pltpu.CompilerParams(collective_id=collective_id, has_side_effects=True),
-    )(x)
+    )(xa, xb)
 
 
 def row_dev(j):
@@ -430,10 +494,12 @@
     gf3 = jnp.stack([gf_next, grad_first, gf_prev])
     second_local = weight_terms(gs3, h_row)
     first_local = weight_terms(gf3, x_row)
-    both = jnp.stack([first_local, second_local])
     n_rows = lax.axis_size("rows")
-    summed = row_sum(both.astype(bf16).reshape(n_rows, -1, 128), 0)
-    first_grad, second_grad = summed.astype(f32).reshape(both.shape)
+    summed_first, summed_second = row_sum(
+        first_local.astype(bf16).reshape(n_rows, -1, 128), second_local.astype(bf16).reshape(n_rows, -1, 128), 0
+    )
+    first_grad = summed_first.astype(f32).reshape(first_local.shape)
+    second_grad = summed_second.astype(f32).reshape(second_local.shape)
     return (block_out[:, None, :], first_grad, second_grad)
 
 

time: 146 us -> 147 us (level); the launches traced: 146 us -> 145 us
  Pallas kernels: 127 us -> 125 us
    another operation x4 -> x2, local copies, waits for them, and re-layouts: 2.11 us -> 0.51 us  [weight_terms(): return jnp.stack(cols, axis=2)]
    reshape x0 -> x2, local copies, waits for them, and re-layouts: none -> 1.56 us  [the longest x1 1.31 us: per_device(): first_grad = summed_first.astype(f32).reshape(first_local.shape)]
    pallas_call x1, Pallas kernels: 60.1 us -> 58.6 us  [row_sum(): pl.pallas_call(functools.partial(row_sum_kernel, n), out_shape=(jax.Shape...]
    unnamed x25 -> x27, local copies, waits for them, and re-layouts: 3.61 us -> 3.62 us
where the time goes in v8:
time: 147 us; the launch traced here: 145 us
  Pallas kernels  125 us (85%)
  local copies, waits for them, and re-layouts  8.72 us (6%)
  matrix products  8.03 us (5%)
  other arithmetic  1.65 us (1%)
    pallas_call x1, Pallas kernels, row_sum(): pl.pallas_call(functools.partial(row_sum_kernel, n), out_shape=(jax.Shape...  58.6 us
    pallas_call x3, Pallas kernels, call(): pl.pallas_call(kernel, out_shape=tuple((jax.ShapeDtypeStruct(shape, dtype...  48.2 us
    pallas_call x1, Pallas kernels, exchange(): pl.pallas_call(functools.partial(exchange_kernel, axis, n, mode), out_sha...  18.4 us
    unnamed x27, local copies, waits for them, and re-layouts  3.62 us
    dot_general x6, matrix products, weight_terms(): jnp.einsum('aow,iw->oai', moved, full_row, preferred_element_type=jnp.flo...  3.4 us

profile of v8, /device:TPU:6, one launch (start us, length us, event | category | flops | bytes accessed | tf_op | source)
XLA Modules:
  0.0 144.6 jit_solution(696319196106705801)
XLA Ops:
  0.6 0.0 copy-start
  0.6 1.0 copy-done
  1.6 18.4 %shard_map.67 = bf16[16,32,512]{2,1,0:T(8,128)(2,1)} custom-call(bf16[32,512]{1,0:T(8,128)(2,1)} %bitcast.195), custom_call_target="tpu_custom_call" | custom-call | tf_op jit(solution)/shard_map/pallas_call | solution.py:416
  20.0 1.4 convolution_bitcast_fusion.4
  21.4 0.1 slice.170
  21.5 0.1 slice.165
  21.6 0.1 slice.160
  21.7 0.0 copy-start.7
  21.7 0.8 fusion.26
  22.5 16.8 %shard_map.68 = (f32[32,512]{1,0:T(8,128)}, bf16[16,32,512]{2,1,0:T(8,128)(2,1)}) custom-call(f32[32,512]{1,0:T(8,128)} %get-tuple-element.42.p0, f32[32,512]{1,0:T(8,128)} %get-tuple-element.41.p2, f32[32,512]{1,0:T(8,128)} %get-tuple-element.40.p1), custom_call_target="tpu_custom_call" | custom-call | tf_op jit(solution)/shard_map/pallas_call | solution.py:393
  39.3 0.0 copy-done.7
  39.3 1.4 convolution_bitcast_fusion.3
  40.7 0.1 slice.185
  40.8 0.1 slice.180
  40.9 0.1 slice.175
  41.0 0.0 copy-start.2
  41.0 0.8 fusion.20
  41.7 12.0 %shard_map.69 = (bf16[32,512]{1,0:T(8,128)(2,1)}, bf16[32,512]{1,0:T(8,128)(2,1)}, bf16[32,512]{1,0:T(8,128)(2,1)}, bf16[32,512]{1,0:T(8,128)(2,1)}) custom-call(f32[32,512]{1,0:T(8,128)} %get-tuple-element.33.p0, f32[32,512]{1,0:T(8,128)} %get-tuple-element.32.p2, f32[32,512]{1,0:T(8,128)} %get-tuple-element.31.p1, bf16[32,512]{1,0:T(8,128)(2,1)} %bitcast.196, ...), custom_call_target="tpu_custom_call" | custom-call | tf_op jit(solution)/shard_map/pallas_call | solution.py:393
  53.8 0.0 copy-done.2
  53.8 0.0 copy-start.3
  53.8 0.0 copy-start.4
  53.8 0.0 copy-start.5
  53.8 1.1 fusion.7
  54.9 0.0 copy-done.3
  54.9 0.0 copy-done.4
  54.9 0.0 copy-done.5
  55.0 0.1 fusion.35
  55.1 0.3 fusion.6
  55.4 0.3 fusion.8
  55.7 0.3 copy.18
  56.0 1.0 convert_element_type.41.xb
  57.0 0.3 convolution_bitcast_fusion.2
  57.3 0.3 slice.186
  57.7 0.3 convolution_bitcast_fusion
  58.0 1.2 fusion.2
  59.2 0.0 copy-start.1
  59.2 19.4 %shard_map.70 = (bf16[32,512]{1,0:T(8,128)(2,1)}, bf16[32,512]{1,0:T(8,128)(2,1)}, bf16[32,512]{1,0:T(8,128)(2,1)}) custom-call(bf16[16,32,512]{2,1,0:T(8,128)(2,1)} %bitcast.166, f32[32,512]{1,0:T(8,128)} %get-tuple-element.19.pre_first), custom_call_target="tpu_custom_call" | custom-call | tf_op jit(solution)/shard_map/pallas_call | solution.py:393
  78.6 0.0 copy-done.1
  78.6 0.0 copy-start.8
  78.7 0.0 copy-start.9
  78.7 0.0 copy-start.10
  78.7 1.1 fusion.4
  79.8 0.0 copy-done.8
  79.8 0.0 copy-done.9
  79.8 0.0 copy-done.10
  79.8 0.1 fusion.36
  79.9 0.3 fusion.3
  80.2 0.3 fusion.5
  80.6 0.3 copy.17
  80.9 1.0 convert_element_type.40.xa
  81.8 58.6 %shard_map.71 = (bf16[32,36,128]{2,1,0:T(8,128)(2,1)}, bf16[32,36,128]{2,1,0:T(8,128)(2,1)}) custom-call(bf16[32,36,128]{2,1,0:T(8,128)(2,1)} %convert_element_type.40.xa, bf16[32,36,128]{2,1,0:T(8,128)(2,1)} %convert_element_type.41.xb), custom_call_target="tpu_custom_call" | custom-call | tf_op jit(solution)/shard_map/pallas_call | solution.py:231
  140.4 1.3 reshape.49
  141.7 0.0 copy-start.6
  141.8 1.0 copy.19
  142.7 0.0 copy-done.6
  142.8 0.2 reshape.51
  143.0 0.0 copy-start.11
  143.0 1.0 copy.20
  144.0 0.0 copy-done.11
  144.0 0.6 copy.25
  (6 shorter events, 0.2 us)
Async XLA Ops:
  0.6 1.0 copy-start
  21.7 17.6 %copy-start.7 = (bf16[32,3,3,512]{3,0,2,1:T(8,128)(2,1)S(1)}, bf16[32,3,3,512]{3,0,2,1:T(8,128)(2,1)}, u32[]{:S(2)}) copy-start(bf16[32,3,3,512]{3,0,2,1:T(8,128)(2,1)} %param.6) | copy-start | bytes 884740
  41.0 12.8 %copy-start.2 = (bf16[16,32,512]{2,1,0:T(8,128)(2,1)S(1)}, bf16[16,32,512]{2,1,0:T(8,128)(2,1)}, u32[]{:S(2)}) copy-start(bf16[16,32,512]{2,1,0:T(8,128)(2,1)} %get-tuple-element.14) | copy-start | bytes 1572868
  53.8 1.2 copy-start.3
  53.8 1.2 copy-start.4
  53.8 1.2 copy-start.5
  59.2 19.4 %copy-start.1 = (bf16[16,32,512]{2,1,0:T(8,128)(2,1)S(1)}, bf16[16,32,512]{2,1,0:T(8,128)(2,1)}, u32[]{:S(2)}) copy-start(bf16[16,32,512]{2,1,0:T(8,128)(2,1)} %shard_map.67) | copy-start | bytes 1572868
  78.6 1.1 copy-start.8
  78.7 1.1 copy-start.9
  78.7 1.1 copy-start.10
  141.7 1.0 copy-start.6
  143.0 1.0 copy-start.11

commit v9 on v8

--- a/solution.py
+++ b/solution.py
@@ -349,43 +349,58 @@
     halo.sent()
 
 
-def output_kernel(p0, p2, p1, feat, og, out_ref, gs_ref, gprev, gnext, from_prev, from_next, sems1, sems2):
-    enter(False)
-    halo = Halo(p0, p2, from_prev, from_next, sems1)
+def backward_kernel(q0, q2, q1, feat, og, w2t, pre_first, out_ref, gs_ref, gprev, gnext, gf_ref, fprev, fnext,
+                    from_prev, from_next, tbuf, rbuf, fsend, frecv, sems1, sems2, sems3):
+    nf = lax.axis_size("filt")
+    mf = lax.axis_index("filt")
+    enter(True)
+    halo = Halo(q0, q2, from_prev, from_next, sems1)
     halo.arrived()
-    pre = p1[...] + from_prev[...] + from_next[...] + feat[...].astype(jnp.float32)
+    pre = q1[...] + from_prev[...] + from_next[...] + feat[...].astype(jnp.float32)
     out_ref[...] = jnp.maximum(pre, 0.0).astype(out_ref.dtype)
     gs_ref[...] = jnp.where(pre > 0, og[...].astype(jnp.float32), 0.0).astype(gs_ref.dtype)
     halo2 = Halo(gs_ref, gs_ref, gprev, gnext, sems2)
     halo2.arrived()
+    rows3 = jnp.concatenate([gnext[...], gs_ref[...], gprev[...]], axis=0)
+    blk, width = tbuf.shape[1], tbuf.shape[2]
+    col = lax.broadcasted_iota(jnp.int32, (blk, width), 1)
+
+    def block(t, carry):
+        rows = pl.ds(pl.multiple_of(t * blk, blk), blk)
+        total = None
+        for b in range(3):
+            part = jnp.dot(w2t[b, rows, :], rows3, preferred_element_type=jnp.float32)
+            if b == 0:
+                part = jnp.where(col == width - 1, 0.0, pltpu.roll(part, width - 1, 1))
+            elif b == 2:
+                part = jnp.where(col == 0, 0.0, pltpu.roll(part, 1, 1))
+            total = part if total is None else total + part
+        tbuf[t] = total.astype(tbuf.dtype)
+        return carry
+
+    lax.fori_loop(0, nf, block, 0)
+
+    def out(j, s):
+        return rcopy(tbuf.at[j], rbuf.at[mf], fsend.at[j], frecv.at[mf], filt_dev(j))
+
+    def inc(j, s):
+        return rcopy(tbuf.at[s], rbuf.at[s], fsend.at[s], frecv.at[s], filt_dev(s))
+
+    each_filt_peer(lambda j, s: out(j, s).start())
+    each_filt_peer(lambda j, s: inc(j, s).wait_recv())
+    acc = tbuf[mf].astype(jnp.float32)
+
+    def add(k, acc):
+        return acc + rbuf[lax.rem(mf + k, nf)].astype(jnp.float32)
+
+    acc = lax.fori_loop(1, nf, add, acc)
+    gf_ref[...] = jnp.where(pre_first[...] > 0, acc, 0.0).astype(gf_ref.dtype)
+    halo3 = Halo(gf_ref, gf_ref, fprev, fnext, sems3)
+    halo3.arrived()
+    each_filt_peer(lambda j, s: out(j, s).wait_send())
     halo.sent()
     halo2.sent()
-
-
-def first_grad_kernel(terms, pre_first, gf_ref, gprev, gnext, buf, fsend, frecv, hsems):
-    nf = lax.axis_size("filt")
-    mf = lax.axis_index("filt")
-    enter(True)
-
-    def out(j, s):
-        return rcopy(terms.at[j], buf.at[mf], fsend.at[j], frecv.at[mf], filt_dev(j))
-
-    def inc(j, s):
-        return rcopy(terms.at[s], buf.at[s], fsend.at[s], frecv.at[s], filt_dev(s))
-
-    each_filt_peer(lambda j, s: out(j, s).start())
-    each_filt_peer(lambda j, s: inc(j, s).wait_recv())
-    acc = terms[mf].astype(jnp.float32)
-
-    def add(k, acc):
-        return acc + buf[lax.rem(mf + k, nf)].astype(jnp.float32)
-
-    acc = lax.fori_loop(1, nf, add, acc)
-    gf_ref[...] = jnp.where(pre_first[...] > 0, acc, 0.0).astype(gf_ref.dtype)
-    halo = Halo(gf_ref, gf_ref, gprev, gnext, hsems)
-    halo.arrived()
-    each_filt_peer(lambda j, s: out(j, s).wait_send())
-    halo.sent()
+    halo3.sent()
 
 
 def call(kernel, args, outs, scratch, collective_id):
@@ -474,23 +489,18 @@
     )
     h_row = h_all.reshape(-1, blk[1])
     q0, q1, q2 = conv_row(second_weight, h_row)
-    block_out, grad_second, gs_prev, gs_next = call(
-        output_kernel,
-        (q0, q2, q1, feat, og),
-        [(blk, bf16)] * 4,
-        [pltpu.VMEM(blk, f32), pltpu.VMEM(blk, f32), pltpu.SemaphoreType.DMA((4,)), pltpu.SemaphoreType.DMA((4,))],
+    o, _, _, i_ch = second_weight.shape
+    w2t = second_weight.transpose(2, 3, 1, 0).reshape(3, i_ch, 3 * o)
+    block_out, grad_second, gs_prev, gs_next, grad_first, gf_prev, gf_next = call(
+        backward_kernel,
+        (q0, q2, q1, feat, og, w2t, pre_first),
+        [(blk, bf16)] * 7,
+        [pltpu.VMEM(blk, f32), pltpu.VMEM(blk, f32), pltpu.VMEM((n_filt,) + blk, bf16),
+         pltpu.VMEM((n_filt,) + blk, bf16), pltpu.SemaphoreType.DMA((n_filt,)), pltpu.SemaphoreType.DMA((n_filt,)),
+         pltpu.SemaphoreType.DMA((4,)), pltpu.SemaphoreType.DMA((4,)), pltpu.SemaphoreType.DMA((4,))],
         3,
     )
     gs3 = jnp.stack([gs_next, grad_second, gs_prev])
-    terms = hidden_terms(second_weight, gs3).astype(bf16).reshape((n_filt,) + blk)
-    grad_first, gf_prev, gf_next = call(
-        first_grad_kernel,
-        (terms, pre_first),
-        [(blk, bf16)] * 3,
-        [pltpu.VMEM((n_filt,) + blk, bf16), pltpu.SemaphoreType.DMA((n_filt,)),
-         pltpu.SemaphoreType.DMA((n_filt,)), pltpu.SemaphoreType.DMA((4,))],
-        4,
-    )
     gf3 = jnp.stack([gf_next, grad_first, gf_prev])
     second_local = weight_terms(gs3, h_row)
     first_local = weight_terms(gf3, x_row)

time: 147 us -> 141 us (0.959)
  matrix products: 8.03 us -> 4.47 us
  Pallas kernels: 125 us -> 122 us
    pallas_call x1, Pallas kernels: 58.6 us -> 56.4 us  [row_sum(): pl.pallas_call(functools.partial(row_sum_kernel, n), out_shape=(jax.Shape...]
    dot_general x3 -> x0, matrix products: 1.9 us -> none  [hidden_terms(): jnp.einsum('oai,aow->iw', weight[:, :, b, :], rows3, preferred_element_ty...]
    dot_general x6, matrix products: 3.4 us -> 1.76 us  [weight_terms(): jnp.einsum('aow,iw->oai', moved, full_row, preferred_element_type=jnp.flo...]
    pallas_call x3 -> x2, Pallas kernels: 48.2 us -> 46.8 us  [call(): pl.pallas_call(kernel, out_shape=tuple((jax.ShapeDtypeStruct(shape, dtype...]
    unnamed x27 -> x28, local copies, waits for them, and re-layouts: 3.62 us -> 3.14 us
where the time goes in v9:
time: 141 us; the launch traced here: 138 us
  Pallas kernels  122 us (87%)
  local copies, waits for them, and re-layouts  8.84 us (6%)
  matrix products  4.47 us (3%)
  other arithmetic  2.46 us (2%)
    pallas_call x1, Pallas kernels, row_sum(): pl.pallas_call(functools.partial(row_sum_kernel, n), out_shape=(jax.Shape...  56.4 us
    pallas_call x2, Pallas kernels, call(): pl.pallas_call(kernel, out_shape=tuple((jax.ShapeDtypeStruct(shape, dtype...  46.8 us
    pallas_call x1, Pallas kernels, exchange(): pl.pallas_call(functools.partial(exchange_kernel, axis, n, mode), out_sha...  18.5 us
    unnamed x28, local copies, waits for them, and re-layouts  3.14 us

profile of v9, /device:TPU:6, one launch (start us, length us, event | category | flops | bytes accessed | tf_op | source)
XLA Modules:
  0.0 138.5 jit_solution(8558356734994828353)
XLA Ops:
  0.6 0.0 copy-start
  0.6 18.5 %shard_map.67 = bf16[16,32,512]{2,1,0:T(8,128)(2,1)} custom-call(bf16[32,512]{1,0:T(8,128)(2,1)} %bitcast.141), custom_call_target="tpu_custom_call" | custom-call | tf_op jit(solution)/shard_map/pallas_call | solution.py:431
  19.2 0.0 copy-done
  19.2 1.4 convolution_bitcast_fusion.1
  20.6 0.1 slice.140
  20.7 0.1 slice.145
  20.8 0.1 slice.150
  20.9 0.0 copy-start.4
  20.9 0.8 fusion.17
  21.6 16.8 %shard_map.68 = (f32[32,512]{1,0:T(8,128)}, bf16[16,32,512]{2,1,0:T(8,128)(2,1)}) custom-call(f32[32,512]{1,0:T(8,128)} %get-tuple-element.42.p0, f32[32,512]{1,0:T(8,128)} %get-tuple-element.41.p2, f32[32,512]{1,0:T(8,128)} %get-tuple-element.40.p1), custom_call_target="tpu_custom_call" | custom-call | tf_op jit(solution)/shard_map/pallas_call | solution.py:408
  38.5 0.0 copy-done.4
  38.5 1.4 convolution_bitcast_fusion
  39.9 0.1 slice.155
  40.0 0.1 slice.160
  40.0 0.1 slice.165
  40.1 0.8 fusion.11
  40.9 0.9 copy.13.w2t
  41.9 0.0 copy-start.2
  41.9 30.0 %shard_map.69 = (bf16[32,512]{1,0:T(8,128)(2,1)}, bf16[32,512]{1,0:T(8,128)(2,1)}, bf16[32,512]{1,0:T(8,128)(2,1)}, bf16[32,512]{1,0:T(8,128)(2,1)}, bf16[32,512...) custom-call(f32[32,512]{1,0:T(8,128)} %get-tuple-element.33.q0, f32[32,512]{1,0:T(8,128)} %get-tuple-element.32.q2, ...), custom_call_target="tpu_custom_call" | custom-call | tf_op jit(solution)/shard_map/pallas_call | solution.py:408
  71.8 0.8 pad_maximum_fusion.3
  72.6 0.1 fusion.26
  72.7 0.0 copy-done.2
  72.8 0.0 copy-start.9
  72.8 0.0 copy-start.10
  72.8 0.0 copy-start.11
  72.8 0.3 fusion.3
  73.1 0.4 copy-done.9
  73.5 0.0 copy-done.10
  73.5 0.0 copy-done.11
  73.6 0.3 fusion.4
  73.9 0.3 fusion.5
  74.2 0.3 copy.15
  74.5 0.0 copy-start.5
  74.5 0.0 copy-start.6
  74.5 0.0 copy-start.7
  74.5 0.0 copy-start.1
  74.5 1.0 convert_element_type.33.xb
  75.5 0.0 copy-done.5
  75.5 0.0 copy-done.6
  75.5 0.0 copy-done.7
  75.5 0.1 fusion.27
  75.6 0.0 copy-done.1
  75.6 0.3 fusion
  75.9 0.3 fusion.1
  76.2 0.3 fusion.2
  76.6 0.3 copy.14
  76.8 1.0 convert_element_type.32.xa
  77.8 56.4 %shard_map.70 = (bf16[32,36,128]{2,1,0:T(8,128)(2,1)}, bf16[32,36,128]{2,1,0:T(8,128)(2,1)}) custom-call(bf16[32,36,128]{2,1,0:T(8,128)(2,1)} %convert_element_type.32.xa, bf16[32,36,128]{2,1,0:T(8,128)(2,1)} %convert_element_type.33.xb), custom_call_target="tpu_custom_call" | custom-call | tf_op jit(solution)/shard_map/pallas_call | solution.py:231
  134.2 1.3 reshape.49
  135.6 0.0 copy-start.3
  135.6 1.0 copy.16
  136.6 0.0 copy-done.3
  136.6 0.2 reshape.51
  136.8 0.0 copy-start.8
  136.8 1.0 copy.17
  137.8 0.0 copy-done.8
  137.8 0.6 copy.19
  (6 shorter events, 0.2 us)
Async XLA Ops:
  0.6 18.6 %copy-start = (bf16[32,3,3,512]{3,0,2,1:T(8,128)(2,1)S(1)}, bf16[32,3,3,512]{3,0,2,1:T(8,128)(2,1)}, u32[]{:S(2)}) copy-start(bf16[32,3,3,512]{3,0,2,1:T(8,128)(2,1)} %param.5) | copy-start | bytes 884740
  20.9 17.6 %copy-start.4 = (bf16[32,3,3,512]{3,0,2,1:T(8,128)(2,1)S(1)}, bf16[32,3,3,512]{3,0,2,1:T(8,128)(2,1)}, u32[]{:S(2)}) copy-start(bf16[32,3,3,512]{3,0,2,1:T(8,128)(2,1)} %param.6) | copy-start | bytes 884740
  41.9 30.9 %copy-start.2 = (bf16[16,32,512]{2,1,0:T(8,128)(2,1)S(1)}, bf16[16,32,512]{2,1,0:T(8,128)(2,1)}, u32[]{:S(2)}) copy-start(bf16[16,32,512]{2,1,0:T(8,128)(2,1)} %get-tuple-element.14) | copy-start | bytes 1572868
  72.8 0.8 copy-start.9
  72.8 0.8 copy-start.10
  72.8 0.8 copy-start.11
  74.5 1.0 copy-start.5
  74.5 1.0 copy-start.6
  74.5 1.0 copy-start.7
  74.5 1.1 copy-start.1
  135.6 1.0 copy-start.3
  136.8 1.0 copy-start.8

commit v10 on v9

--- a/solution.py
+++ b/solution.py
@@ -328,12 +328,43 @@
             self.down(me + 1).wait_send()
 
 
-def hidden_kernel(p0, p2, p1, pre_ref, h_ref, from_prev, from_next, hsems, fsend, frecv):
+def lane_shift(part, offset):
+    width = part.shape[1]
+    col = lax.broadcasted_iota(jnp.int32, part.shape, 1)
+    if offset == 1:
+        return jnp.where(col == width - 1, 0.0, pltpu.roll(part, width - 1, 1))
+    return jnp.where(col == 0, 0.0, pltpu.roll(part, 1, 1))
+
+
+def forward_kernel(feat, w1r, x_ref, pre_ref, h_ref, p0s, p2s, from_prev, from_next, hsems, xsend, xrecv, fsend, frecv):
     mf = lax.axis_index("filt")
+    blk = feat.shape[0]
     enter(True)
-    halo = Halo(p0, p2, from_prev, from_next, hsems)
+
+    def xout(j, s):
+        return rcopy(feat, x_ref.at[pl.ds(mf * blk, blk)], xsend.at[j], xrecv.at[mf], filt_dev(j))
+
+    def xin(j, s):
+        return rcopy(feat, x_ref.at[pl.ds(s * blk, blk)], xsend.at[s], xrecv.at[s], filt_dev(s))
+
+    each_filt_peer(lambda j, s: xout(j, s).start())
+    x_ref[pl.ds(mf * blk, blk)] = feat[...]
+    each_filt_peer(lambda j, s: xin(j, s).wait_recv())
+    x = x_ref[...]
+    parts = []
+    for a in range(3):
+        total = None
+        for b in range(3):
+            part = jnp.dot(w1r[a * 3 + b], x, preferred_element_type=jnp.float32)
+            if b != 1:
+                part = lane_shift(part, b - 1)
+            total = part if total is None else total + part
+        parts.append(total)
+    p0s[...] = parts[0]
+    p2s[...] = parts[2]
+    halo = Halo(p0s, p2s, from_prev, from_next, hsems)
     halo.arrived()
-    pre = p1[...] + from_prev[...] + from_next[...]
+    pre = parts[1] + from_prev[...] + from_next[...]
     pre_ref[...] = pre
     h_ref[mf] = jnp.maximum(pre, 0.0).astype(h_ref.dtype)
 
@@ -345,6 +376,7 @@
 
     each_filt_peer(lambda j, s: out(j, s).start())
     each_filt_peer(lambda j, s: inc(j, s).wait_recv())
+    each_filt_peer(lambda j, s: xout(j, s).wait_send())
     each_filt_peer(lambda j, s: out(j, s).wait_send())
     halo.sent()
 
@@ -477,19 +509,18 @@
     n_filt = lax.axis_size("filt")
     blk = feat.shape
     f32, bf16 = jnp.float32, jnp.bfloat16
-    x_row = exchange(feat, "filt", "ag", 1).reshape(-1, blk[1])
-    p0, p1, p2 = conv_row(first_weight, x_row)
-    pre_first, h_all = call(
-        hidden_kernel,
-        (p0, p2, p1),
-        [(blk, f32), ((n_filt,) + blk, bf16)],
-        [pltpu.VMEM(blk, f32), pltpu.VMEM(blk, f32), pltpu.SemaphoreType.DMA((4,)),
-         pltpu.SemaphoreType.DMA((n_filt,)), pltpu.SemaphoreType.DMA((n_filt,))],
+    o, _, _, i_ch = first_weight.shape
+    w1r = first_weight.transpose(1, 2, 0, 3).reshape(9, o, i_ch)
+    sem = pltpu.SemaphoreType.DMA
+    x_row, pre_first, h_all = call(
+        forward_kernel,
+        (feat, w1r),
+        [((n_filt * blk[0], blk[1]), bf16), (blk, f32), ((n_filt,) + blk, bf16)],
+        [pltpu.VMEM(blk, f32)] * 4 + [sem((4,)), sem((n_filt,)), sem((n_filt,)), sem((n_filt,)), sem((n_filt,))],
         2,
     )
     h_row = h_all.reshape(-1, blk[1])
     q0, q1, q2 = conv_row(second_weight, h_row)
-    o, _, _, i_ch = second_weight.shape
     w2t = second_weight.transpose(2, 3, 1, 0).reshape(3, i_ch, 3 * o)
     block_out, grad_second, gs_prev, gs_next, grad_first, gf_prev, gf_next = call(
         backward_kernel,

time: 141 us -> 134 us (0.950)
  Pallas kernels: 122 us -> 118 us
    pallas_call x1 -> x0, Pallas kernels: 18.5 us -> none  [exchange(): pl.pallas_call(functools.partial(exchange_kernel, axis, n, mode), out_sha...]
    pallas_call x2, Pallas kernels: 46.8 us -> 62 us  [call(): pl.pallas_call(kernel, out_shape=tuple((jax.ShapeDtypeStruct(shape, dtype...]
    unnamed x28 -> x26, local copies, waits for them, and re-layouts: 3.14 us -> 3.13 us
where the time goes in v10:
time: 134 us; the launch traced here: 133 us
  Pallas kernels  118 us (88%)
  local copies, waits for them, and re-layouts  8.55 us (6%)
  matrix products  3.12 us (2%)
  other arithmetic  1.68 us (1%)
    pallas_call x2, Pallas kernels, call(): pl.pallas_call(kernel, out_shape=tuple((jax.ShapeDtypeStruct(shape, dtype...  62 us
    pallas_call x1, Pallas kernels, row_sum(): pl.pallas_call(functools.partial(row_sum_kernel, n), out_shape=(jax.Shape...  56.4 us
    unnamed x26, local copies, waits for them, and re-layouts  3.13 us

profile of v10, /device:TPU:6, one launch (start us, length us, event | category | flops | bytes accessed | tf_op | source)
XLA Modules:
  0.0 132.6 jit_solution(1356535898893093590)
XLA Ops:
  0.6 0.0 copy-start.3
  0.6 31.2 %shard_map.67 = (bf16[512,512]{1,0:T(8,128)(2,1)}, f32[32,512]{1,0:T(8,128)}, bf16[16,32,512]{2,1,0:T(8,128)(2,1)}) custom-call(bf16[32,512]{1,0:T(8,128)(2,1)} %bitcast.100, bf16[9,32,512]{2,1,0:T(8,128)(2,1)} %bitcast.95), custom_call_target="tpu_custom_call" | custom-call | tf_op jit(solution)/shard_map/pallas_call | solution.py:440
  31.9 0.0 copy-done.3
  31.9 1.4 %convolution_bitcast_fusion = f32[9,32,512]{2,1,0:T(8,128)S(1)} fusion(bf16[512,512,1]{1,0,2:T(8,128)(2,1)} %bitcast.90, bf16[32,9,512]{2,0,1:T(8,128)(2,1)S(1)} %bitcast.96), kind=kOutput, calls=%fused_computation | convolution fusion | flops 150994944 | bytes 1409024 | tf_op jit(solution)/shard_map/oki,iw->kow/dot_general | solution.py:485
  33.3 0.1 slice.80
  33.4 0.1 slice.85
  33.5 0.1 slice.90
  33.6 0.8 fusion.14
  34.4 0.9 copy.13.w2t
  35.3 0.0 copy-start.1
  35.3 30.8 %shard_map.68 = (bf16[32,512]{1,0:T(8,128)(2,1)}, bf16[32,512]{1,0:T(8,128)(2,1)}, bf16[32,512]{1,0:T(8,128)(2,1)}, bf16[32,512]{1,0:T(8,128)(2,1)}, bf16[32,512...) custom-call(f32[32,512]{1,0:T(8,128)} %get-tuple-element.35.q0, f32[32,512]{1,0:T(8,128)} %get-tuple-element.34.q2, ...), custom_call_target="tpu_custom_call" | custom-call | tf_op jit(solution)/shard_map/pallas_call | solution.py:440
  66.0 0.8 pad_maximum_fusion.3
  66.8 0.1 fusion.23
  66.9 0.0 copy-done.1
  67.0 0.0 copy-start.8
  67.0 0.0 copy-start.9
  67.0 0.0 copy-start.10
  67.0 0.3 fusion.3
  67.3 0.4 copy-done.8
  67.7 0.0 copy-done.9
  67.7 0.0 copy-done.10
  67.8 0.3 fusion.4
  68.0 0.3 fusion.5
  68.4 0.3 copy.15
  68.7 0.0 copy-start.5
  68.7 0.0 copy-start.6
  68.7 0.0 copy-start.7
  68.7 0.0 copy-start
  68.7 1.0 convert_element_type.27.xb
  69.7 0.0 copy-done.5
  69.7 0.0 copy-done.6
  69.7 0.0 copy-done.7
  69.7 0.1 fusion.24
  69.8 0.0 copy-done
  69.8 0.3 fusion
  70.1 0.3 fusion.1
  70.4 0.3 fusion.2
  70.8 0.3 copy.14
  71.0 1.0 convert_element_type.26.xa
  72.0 56.4 %shard_map.69 = (bf16[32,36,128]{2,1,0:T(8,128)(2,1)}, bf16[32,36,128]{2,1,0:T(8,128)(2,1)}) custom-call(bf16[32,36,128]{2,1,0:T(8,128)(2,1)} %convert_element_type.26.xa, bf16[32,36,128]{2,1,0:T(8,128)(2,1)} %convert_element_type.27.xb), custom_call_target="tpu_custom_call" | custom-call | tf_op jit(solution)/shard_map/pallas_call | solution.py:231
  128.4 1.3 reshape.45
  129.7 0.0 copy-start.2
  129.7 1.0 copy.16
  130.7 0.0 copy-done.2
  130.7 0.2 reshape.47
  131.0 0.0 copy-start.4
  131.0 1.0 copy.17
  132.0 0.0 copy-done.4
  132.0 0.6 copy.19
  (5 shorter events, 0.1 us)
Async XLA Ops:
  0.6 31.3 %copy-start.3 = (bf16[32,3,3,512]{3,0,2,1:T(8,128)(2,1)S(1)}, bf16[32,3,3,512]{3,0,2,1:T(8,128)(2,1)}, u32[]{:S(2)}) copy-start(bf16[32,3,3,512]{3,0,2,1:T(8,128)(2,1)} %param.6) | copy-start | bytes 884740
  35.3 31.7 %copy-start.1 = (bf16[16,32,512]{2,1,0:T(8,128)(2,1)S(1)}, bf16[16,32,512]{2,1,0:T(8,128)(2,1)}, u32[]{:S(2)}) copy-start(bf16[16,32,512]{2,1,0:T(8,128)(2,1)} %get-tuple-element.15) | copy-start | bytes 1572868
  67.0 0.8 copy-start.8
  67.0 0.8 copy-start.9
  67.0 0.8 copy-start.10
  68.7 1.0 copy-start.5
  68.7 1.0 copy-start.6
  68.7 1.0 copy-start.7
  68.7 1.1 copy-start
  129.7 1.0 copy-start.2
  131.0 1.0 copy-start.4

commit v11 on v10

--- a/solution.py
+++ b/solution.py
@@ -336,76 +336,71 @@
     return jnp.where(col == 0, 0.0, pltpu.roll(part, 1, 1))
 
 
-def forward_kernel(feat, w1r, x_ref, pre_ref, h_ref, p0s, p2s, from_prev, from_next, hsems, xsend, xrecv, fsend, frecv):
-    mf = lax.axis_index("filt")
-    blk = feat.shape[0]
-    enter(True)
-
-    def xout(j, s):
-        return rcopy(feat, x_ref.at[pl.ds(mf * blk, blk)], xsend.at[j], xrecv.at[mf], filt_dev(j))
-
-    def xin(j, s):
-        return rcopy(feat, x_ref.at[pl.ds(s * blk, blk)], xsend.at[s], xrecv.at[s], filt_dev(s))
-
-    each_filt_peer(lambda j, s: xout(j, s).start())
-    x_ref[pl.ds(mf * blk, blk)] = feat[...]
-    each_filt_peer(lambda j, s: xin(j, s).wait_recv())
-    x = x_ref[...]
+def conv_parts(w_ref, x):
     parts = []
     for a in range(3):
         total = None
         for b in range(3):
-            part = jnp.dot(w1r[a * 3 + b], x, preferred_element_type=jnp.float32)
+            part = jnp.dot(w_ref[a * 3 + b], x, preferred_element_type=jnp.float32)
             if b != 1:
                 part = lane_shift(part, b - 1)
             total = part if total is None else total + part
         parts.append(total)
+    return parts
+
+
+def filt_gather(src, dst, blk, send, recv):
+    mf = lax.axis_index("filt")
+
+    def out(j, s):
+        return rcopy(src, dst.at[pl.ds(mf * blk, blk)], send.at[j], recv.at[mf], filt_dev(j))
+
+    def inc(j, s):
+        return rcopy(src, dst.at[pl.ds(s * blk, blk)], send.at[s], recv.at[s], filt_dev(s))
+
+    each_filt_peer(lambda j, s: out(j, s).start())
+    dst[pl.ds(mf * blk, blk)] = src[...]
+    return (lambda: each_filt_peer(lambda j, s: inc(j, s).wait_recv()),
+            lambda: each_filt_peer(lambda j, s: out(j, s).wait_send()))
+
+
+def block_kernel(feat, og, w1r, w2r, w2t, x_ref, h_ref, out_ref, gs_ref, gprev, gnext, gf_ref, fprev, fnext,
+                 p0s, p2s, from_prev, from_next, q0s, q2s, qprev, qnext, hsrc, pre1, tbuf, rbuf,
+                 hsems, xsend, xrecv, fsend, frecv, sems1, sems2, sems3, tsend, trecv):
+    nf = lax.axis_size("filt")
+    mf = lax.axis_index("filt")
+    blk = feat.shape[0]
+    enter(True)
+    x_arrived, x_sent = filt_gather(feat, x_ref, blk, xsend, xrecv)
+    x_arrived()
+    parts = conv_parts(w1r, x_ref[...])
     p0s[...] = parts[0]
     p2s[...] = parts[2]
     halo = Halo(p0s, p2s, from_prev, from_next, hsems)
     halo.arrived()
-    pre = parts[1] + from_prev[...] + from_next[...]
-    pre_ref[...] = pre
-    h_ref[mf] = jnp.maximum(pre, 0.0).astype(h_ref.dtype)
-
-    def out(j, s):
-        return rcopy(h_ref.at[mf], h_ref.at[mf], fsend.at[j], frecv.at[mf], filt_dev(j))
-
-    def inc(j, s):
-        return rcopy(h_ref.at[s], h_ref.at[s], fsend.at[s], frecv.at[s], filt_dev(s))
-
-    each_filt_peer(lambda j, s: out(j, s).start())
-    each_filt_peer(lambda j, s: inc(j, s).wait_recv())
-    each_filt_peer(lambda j, s: xout(j, s).wait_send())
-    each_filt_peer(lambda j, s: out(j, s).wait_send())
-    halo.sent()
-
-
-def backward_kernel(q0, q2, q1, feat, og, w2t, pre_first, out_ref, gs_ref, gprev, gnext, gf_ref, fprev, fnext,
-                    from_prev, from_next, tbuf, rbuf, fsend, frecv, sems1, sems2, sems3):
-    nf = lax.axis_size("filt")
-    mf = lax.axis_index("filt")
-    enter(True)
-    halo = Halo(q0, q2, from_prev, from_next, sems1)
-    halo.arrived()
-    pre = q1[...] + from_prev[...] + from_next[...] + feat[...].astype(jnp.float32)
+    pre1[...] = parts[1] + from_prev[...] + from_next[...]
+    hsrc[...] = jnp.maximum(pre1[...], 0.0).astype(hsrc.dtype)
+    h_arrived, h_sent = filt_gather(hsrc, h_ref, blk, fsend, frecv)
+    h_arrived()
+    qs = conv_parts(w2r, h_ref[...])
+    q0s[...] = qs[0]
+    q2s[...] = qs[2]
+    halo1 = Halo(q0s, q2s, qprev, qnext, sems1)
+    halo1.arrived()
+    pre = qs[1] + qprev[...] + qnext[...] + feat[...].astype(jnp.float32)
     out_ref[...] = jnp.maximum(pre, 0.0).astype(out_ref.dtype)
     gs_ref[...] = jnp.where(pre > 0, og[...].astype(jnp.float32), 0.0).astype(gs_ref.dtype)
     halo2 = Halo(gs_ref, gs_ref, gprev, gnext, sems2)
     halo2.arrived()
     rows3 = jnp.concatenate([gnext[...], gs_ref[...], gprev[...]], axis=0)
-    blk, width = tbuf.shape[1], tbuf.shape[2]
-    col = lax.broadcasted_iota(jnp.int32, (blk, width), 1)
 
     def block(t, carry):
         rows = pl.ds(pl.multiple_of(t * blk, blk), blk)
         total = None
         for b in range(3):
             part = jnp.dot(w2t[b, rows, :], rows3, preferred_element_type=jnp.float32)
-            if b == 0:
-                part = jnp.where(col == width - 1, 0.0, pltpu.roll(part, width - 1, 1))
-            elif b == 2:
-                part = jnp.where(col == 0, 0.0, pltpu.roll(part, 1, 1))
+            if b != 1:
+                part = lane_shift(part, 1 - b)
             total = part if total is None else total + part
         tbuf[t] = total.astype(tbuf.dtype)
         return carry
@@ -413,10 +408,10 @@
     lax.fori_loop(0, nf, block, 0)
 
     def out(j, s):
-        return rcopy(tbuf.at[j], rbuf.at[mf], fsend.at[j], frecv.at[mf], filt_dev(j))
+        return rcopy(tbuf.at[j], rbuf.at[mf], tsend.at[j], trecv.at[mf], filt_dev(j))
 
     def inc(j, s):
-        return rcopy(tbuf.at[s], rbuf.at[s], fsend.at[s], frecv.at[s], filt_dev(s))
+        return rcopy(tbuf.at[s], rbuf.at[s], tsend.at[s], trecv.at[s], filt_dev(s))
 
     each_filt_peer(lambda j, s: out(j, s).start())
     each_filt_peer(lambda j, s: inc(j, s).wait_recv())
@@ -426,11 +421,14 @@
         return acc + rbuf[lax.rem(mf + k, nf)].astype(jnp.float32)
 
     acc = lax.fori_loop(1, nf, add, acc)
-    gf_ref[...] = jnp.where(pre_first[...] > 0, acc, 0.0).astype(gf_ref.dtype)
+    gf_ref[...] = jnp.where(pre1[...] > 0, acc, 0.0).astype(gf_ref.dtype)
     halo3 = Halo(gf_ref, gf_ref, fprev, fnext, sems3)
     halo3.arrived()
+    x_sent()
+    h_sent()
     each_filt_peer(lambda j, s: out(j, s).wait_send())
     halo.sent()
+    halo1.sent()
     halo2.sent()
     halo3.sent()
 
@@ -511,25 +509,18 @@
     f32, bf16 = jnp.float32, jnp.bfloat16
     o, _, _, i_ch = first_weight.shape
     w1r = first_weight.transpose(1, 2, 0, 3).reshape(9, o, i_ch)
+    w2r = second_weight.transpose(1, 2, 0, 3).reshape(9, o, i_ch)
+    w2t = second_weight.transpose(2, 3, 1, 0).reshape(3, i_ch, 3 * o)
     sem = pltpu.SemaphoreType.DMA
-    x_row, pre_first, h_all = call(
-        forward_kernel,
-        (feat, w1r),
-        [((n_filt * blk[0], blk[1]), bf16), (blk, f32), ((n_filt,) + blk, bf16)],
-        [pltpu.VMEM(blk, f32)] * 4 + [sem((4,)), sem((n_filt,)), sem((n_filt,)), sem((n_filt,)), sem((n_filt,))],
+    full = (n_filt * blk[0], blk[1])
+    x_row, h_row, block_out, grad_second, gs_prev, gs_next, grad_first, gf_prev, gf_next = call(
+        block_kernel,
+        (feat, og, w1r, w2r, w2t),
+        [(full, bf16), (full, bf16)] + [(blk, bf16)] * 7,
+        [pltpu.VMEM(blk, f32)] * 8 + [pltpu.VMEM(blk, bf16), pltpu.VMEM(blk, f32),
+                                      pltpu.VMEM((n_filt,) + blk, bf16), pltpu.VMEM((n_filt,) + blk, bf16)]
+        + [sem((4,))] + [sem((n_filt,))] * 4 + [sem((4,))] * 3 + [sem((n_filt,))] * 2,
         2,
-    )
-    h_row = h_all.reshape(-1, blk[1])
-    q0, q1, q2 = conv_row(second_weight, h_row)
-    w2t = second_weight.transpose(2, 3, 1, 0).reshape(3, i_ch, 3 * o)
-    block_out, grad_second, gs_prev, gs_next, grad_first, gf_prev, gf_next = call(
-        backward_kernel,
-        (q0, q2, q1, feat, og, w2t, pre_first),
-        [(blk, bf16)] * 7,
-        [pltpu.VMEM(blk, f32), pltpu.VMEM(blk, f32), pltpu.VMEM((n_filt,) + blk, bf16),
-         pltpu.VMEM((n_filt,) + blk, bf16), pltpu.SemaphoreType.DMA((n_filt,)), pltpu.SemaphoreType.DMA((n_filt,)),
-         pltpu.SemaphoreType.DMA((4,)), pltpu.SemaphoreType.DMA((4,)), pltpu.SemaphoreType.DMA((4,))],
-        3,
     )
     gs3 = jnp.stack([gs_next, grad_second, gs_prev])
     gf3 = jnp.stack([gf_next, grad_first, gf_prev])

time: 134 us -> 128 us (0.955)
  Pallas kernels: 118 us -> 114 us
  other arithmetic: 1.68 us -> 0.11 us
    pallas_call x2 -> x1, Pallas kernels: 62 us -> 56.9 us  [call(): pl.pallas_call(kernel, out_shape=tuple((jax.ShapeDtypeStruct(shape, dtype...]
    dot_general x1 -> x0, matrix products: 1.36 us -> none  [conv_row(): jnp.einsum('oki,iw->kow', flat, row, preferred_element_type=jnp.float32)]
    unnamed x26 -> x24, local copies, waits for them, and re-layouts: 3.13 us -> 4.36 us
where the time goes in v11:
time: 128 us
  Pallas kernels  114 us (89%)
  local copies, waits for them, and re-layouts  9.5 us (7%)
  matrix products  2.86 us (2%)
    pallas_call x1, Pallas kernels, row_sum(): pl.pallas_call(functools.partial(row_sum_kernel, n), out_shape=(jax.Shape...  57.5 us
    pallas_call x1, Pallas kernels, call(): pl.pallas_call(kernel, out_shape=tuple((jax.ShapeDtypeStruct(shape, dtype...  56.9 us
    unnamed x24, local copies, waits for them, and re-layouts  4.36 us
    dot_general x6, matrix products, weight_terms(): jnp.einsum('aow,iw->oai', moved, full_row, preferred_element_type=jnp.flo...  2.86 us

profile of v11, /device:TPU:6, one launch (start us, length us, event | category | flops | bytes accessed | tf_op | source)
XLA Modules:
  0.0 127.7 jit_solution(10527308948926524403)
XLA Ops:
  0.6 1.0 copy.12
  1.6 0.9 copy.13.w2t
  2.5 56.9 %shard_map.67 = (bf16[512,512]{1,0:T(8,128)(2,1)}, bf16[512,512]{1,0:T(8,128)(2,1)}, bf16[32,512]{1,0:T(8,128)(2,1)}, bf16[32,512]{1,0:T(8,128)(2,1)}, bf16[32,5...) custom-call(bf16[32,512]{1,0:T(8,128)(2,1)} %bitcast.59, ...), custom_call_target="tpu_custom_call" | custom-call | tf_op jit(solution)/shard_map/pallas_call | solution.py:438
  59.5 0.0 copy-start.1
  59.5 0.0 copy-start.7
  59.5 0.0 copy-start.8
  59.5 0.0 copy-start.9
  59.5 1.4 %fusion.1 = bf16[32,3,1,512]{3,0,1,2:T(8,128)(2,1)S(1)} fusion(bf16[512,512]{1,0:T(8,128)(2,1)} %get-tuple-element.15, bf16[1,32,512]{2,1,0:T(8,128)(2,1)} %bitcast.70, bf16[1,32,512]{2,1,0:T(8,128)(2,1)} %bitcast.68, bf16[1,32,512]{2,1,0:T(8,128)(2,1)} %bitcast.72), kind=kOutput, calls=%fused_computation.7 | convolution fusion | flops 50675712 | bytes 720896 | tf_op jit(solution)/shard_map/aow,iw->oai/dot_general | solution.py:491
  60.9 0.0 copy-done.7
  61.0 0.0 copy-done.8
  61.0 0.0 copy-done.9
  61.0 0.0 copy-start.4
  61.0 0.0 copy-start.5
  61.0 0.0 copy-start.6
  61.0 0.0 copy-done.1
  61.0 0.7 copy-done.4
  61.7 0.0 copy-done.5
  61.8 0.0 copy-done.6
  61.8 0.3 fusion.4
  62.1 0.1 fusion.20
  62.2 0.3 fusion.3
  62.5 0.3 fusion.5
  62.8 0.3 copy.15
  63.1 0.0 copy-start
  63.1 1.0 convert_element_type.19.xb
  64.1 0.1 fusion.21
  64.2 0.0 copy-done
  64.2 0.3 fusion
  64.5 0.3 fusion.2
  64.8 0.3 copy.14
  65.1 1.0 convert_element_type.18.xa
  66.1 57.5 %shard_map.68 = (bf16[32,36,128]{2,1,0:T(8,128)(2,1)}, bf16[32,36,128]{2,1,0:T(8,128)(2,1)}) custom-call(bf16[32,36,128]{2,1,0:T(8,128)(2,1)} %convert_element_type.18.xa, bf16[32,36,128]{2,1,0:T(8,128)(2,1)} %convert_element_type.19.xb), custom_call_target="tpu_custom_call" | custom-call | tf_op jit(solution)/shard_map/pallas_call | solution.py:231
  123.5 1.3 %reshape.41 = f32[32,3,3,512]{3,2,1,0:T(4,128)S(1)} reshape(bf16[32,36,128]{2,1,0:T(8,128)(2,1)} %get-tuple-element.23) | data formatting | bytes 884736 | tf_op jit(solution)/shard_map/reshape | solution.py:533
  124.9 0.0 copy-start.2
  124.9 1.0 copy.16
  125.9 0.0 copy-done.2
  125.9 0.2 reshape.43
  126.1 0.0 copy-start.3
  126.1 1.0 copy.17
  127.1 0.0 copy-done.3
  127.1 0.6 copy.19
  (4 shorter events, 0.1 us)
Async XLA Ops:
  59.5 1.5 %copy-start.1 = (bf16[512,512]{1,0:T(8,128)(2,1)S(1)}, bf16[512,512]{1,0:T(8,128)(2,1)}, u32[]{:S(2)}) copy-start(bf16[512,512]{1,0:T(8,128)(2,1)} %get-tuple-element.19) | copy-start | bytes 1572868
  59.5 1.4 %copy-start.7 = (bf16[32,512]{1,0:T(8,128)(2,1)S(1)}, bf16[32,512]{1,0:T(8,128)(2,1)}, u32[]{:S(2)}) copy-start(bf16[32,512]{1,0:T(8,128)(2,1)} %get-tuple-element.17) | copy-start | bytes 98308
  59.5 1.4 %copy-start.8 = (bf16[32,512]{1,0:T(8,128)(2,1)S(1)}, bf16[32,512]{1,0:T(8,128)(2,1)}, u32[]{:S(2)}) copy-start(bf16[32,512]{1,0:T(8,128)(2,1)} %get-tuple-element.18) | copy-start | bytes 98308
  59.5 1.4 %copy-start.9 = (bf16[32,512]{1,0:T(8,128)(2,1)S(1)}, bf16[32,512]{1,0:T(8,128)(2,1)}, u32[]{:S(2)}) copy-start(bf16[32,512]{1,0:T(8,128)(2,1)} %get-tuple-element.16) | copy-start | bytes 98308
  61.0 0.8 copy-start.4
  61.0 0.8 copy-start.5
  61.0 0.8 copy-start.6
  63.1 1.1 copy-start
  124.9 1.0 copy-start.2
  126.1 1.0 copy-start.3

commit v12 on v11

--- a/solution.py
+++ b/solution.py
@@ -252,10 +252,14 @@
 
 def each_filt_peer(body):
     nf = lax.axis_size("filt")
+    half = nf // 2
     me = lax.axis_index("filt")
 
     def step(k, carry):
-        body(lax.rem(me + k, nf), lax.rem(me + nf - k, nf))
+        far = (nf - k) // half
+        off = k - 1 - (half - 1) * (1 - far)
+        j = lax.rem(me // half + far, 2) * half + lax.rem(lax.rem(me, half) + off, half)
+        body(j, j)
         return carry
 
     lax.fori_loop(1, nf, step, 0)

time: 128 us -> 126 us (0.984)
    pallas_call x1, Pallas kernels: 56.9 us -> 55.4 us  [call(): pl.pallas_call(kernel, out_shape=tuple((jax.ShapeDtypeStruct(shape, dtype...]
where the time goes in v12:
time: 126 us
  Pallas kernels  113 us (90%)
  local copies, waits for them, and re-layouts  9.5 us (8%)
  matrix products  2.86 us (2%)
    pallas_call x1, Pallas kernels, row_sum(): pl.pallas_call(functools.partial(row_sum_kernel, n), out_shape=(jax.Shape...  57.4 us
    pallas_call x1, Pallas kernels, call(): pl.pallas_call(kernel, out_shape=tuple((jax.ShapeDtypeStruct(shape, dtype...  55.4 us
    unnamed x24, local copies, waits for them, and re-layouts  4.36 us
    dot_general x6, matrix products, weight_terms(): jnp.einsum('aow,iw->oai', moved, full_row, preferred_element_type=jnp.flo...  2.86 us

profile of v12, /device:TPU:6, one launch (start us, length us, event | category | flops | bytes accessed | tf_op | source)
XLA Modules:
  0.0 126.1 jit_solution(8964555748016537029)
XLA Ops:
  0.6 1.0 copy.12
  1.6 0.9 copy.13.w2t
  2.5 55.4 %shard_map.67 = (bf16[512,512]{1,0:T(8,128)(2,1)}, bf16[512,512]{1,0:T(8,128)(2,1)}, bf16[32,512]{1,0:T(8,128)(2,1)}, bf16[32,512]{1,0:T(8,128)(2,1)}, bf16[32,5...) custom-call(bf16[32,512]{1,0:T(8,128)(2,1)} %bitcast.59, ...), custom_call_target="tpu_custom_call" | custom-call | tf_op jit(solution)/shard_map/pallas_call | solution.py:442
  57.9 0.0 copy-start.1
  57.9 0.0 copy-start.7
  58.0 0.0 copy-start.8
  58.0 0.0 copy-start.9
  58.0 1.4 %fusion.1 = bf16[32,3,1,512]{3,0,1,2:T(8,128)(2,1)S(1)} fusion(bf16[512,512]{1,0:T(8,128)(2,1)} %get-tuple-element.15, bf16[1,32,512]{2,1,0:T(8,128)(2,1)} %bitcast.70, bf16[1,32,512]{2,1,0:T(8,128)(2,1)} %bitcast.68, bf16[1,32,512]{2,1,0:T(8,128)(2,1)} %bitcast.72), kind=kOutput, calls=%fused_computation.7 | convolution fusion | flops 50675712 | bytes 720896 | tf_op jit(solution)/shard_map/aow,iw->oai/dot_general | solution.py:495
  59.4 0.0 copy-done.7
  59.4 0.0 copy-done.8
  59.4 0.0 copy-done.9
  59.4 0.0 copy-start.4
  59.4 0.0 copy-start.5
  59.4 0.0 copy-start.6
  59.5 0.0 copy-done.1
  59.5 0.7 copy-done.4
  60.2 0.0 copy-done.5
  60.2 0.0 copy-done.6
  60.2 0.3 fusion.4
  60.5 0.1 fusion.20
  60.6 0.3 fusion.3
  60.9 0.3 fusion.5
  61.3 0.3 copy.15
  61.5 0.0 copy-start
  61.5 1.0 convert_element_type.19.xb
  62.5 0.1 fusion.21
  62.6 0.0 copy-done
  62.6 0.3 fusion
  62.9 0.3 fusion.2
  63.3 0.3 copy.14
  63.5 1.0 convert_element_type.18.xa
  64.5 57.4 %shard_map.68 = (bf16[32,36,128]{2,1,0:T(8,128)(2,1)}, bf16[32,36,128]{2,1,0:T(8,128)(2,1)}) custom-call(bf16[32,36,128]{2,1,0:T(8,128)(2,1)} %convert_element_type.18.xa, bf16[32,36,128]{2,1,0:T(8,128)(2,1)} %convert_element_type.19.xb), custom_call_target="tpu_custom_call" | custom-call | tf_op jit(solution)/shard_map/pallas_call | solution.py:231
  121.9 1.3 %reshape.41 = f32[32,3,3,512]{3,2,1,0:T(4,128)S(1)} reshape(bf16[32,36,128]{2,1,0:T(8,128)(2,1)} %get-tuple-element.23) | data formatting | bytes 884736 | tf_op jit(solution)/shard_map/reshape | solution.py:537
  123.3 0.0 copy-start.2
  123.3 1.0 copy.16
  124.3 0.0 copy-done.2
  124.3 0.2 reshape.43
  124.5 0.0 copy-start.3
  124.5 1.0 copy.17
  125.5 0.0 copy-done.3
  125.5 0.6 copy.19
  (4 shorter events, 0.1 us)
Async XLA Ops:
  57.9 1.5 %copy-start.1 = (bf16[512,512]{1,0:T(8,128)(2,1)S(1)}, bf16[512,512]{1,0:T(8,128)(2,1)}, u32[]{:S(2)}) copy-start(bf16[512,512]{1,0:T(8,128)(2,1)} %get-tuple-element.19) | copy-start | bytes 1572868
  57.9 1.4 %copy-start.7 = (bf16[32,512]{1,0:T(8,128)(2,1)S(1)}, bf16[32,512]{1,0:T(8,128)(2,1)}, u32[]{:S(2)}) copy-start(bf16[32,512]{1,0:T(8,128)(2,1)} %get-tuple-element.17) | copy-start | bytes 98308
  58.0 1.4 %copy-start.8 = (bf16[32,512]{1,0:T(8,128)(2,1)S(1)}, bf16[32,512]{1,0:T(8,128)(2,1)}, u32[]{:S(2)}) copy-start(bf16[32,512]{1,0:T(8,128)(2,1)} %get-tuple-element.18) | copy-start | bytes 98308
  58.0 1.4 %copy-start.9 = (bf16[32,512]{1,0:T(8,128)(2,1)S(1)}, bf16[32,512]{1,0:T(8,128)(2,1)}, u32[]{:S(2)}) copy-start(bf16[32,512]{1,0:T(8,128)(2,1)} %get-tuple-element.16) | copy-start | bytes 98308
  59.4 0.8 copy-start.4
  59.4 0.8 copy-start.5
  59.4 0.8 copy-start.6
  61.5 1.1 copy-start
  123.3 1.0 copy-start.2
  124.5 1.0 copy-start.3

commit v13 on v12

--- a/solution.py
+++ b/solution.py
@@ -105,8 +105,9 @@
     def each_z(self, body):
         zn, my_z = self.zn, self.my_z
 
-        def step(k, carry):
-            body(lax.rem(my_z + k, zn), lax.rem(my_z + zn - k, zn))
+        def step(t, carry):
+            j = lax.rem(my_z + zn // 2 + (t // 2) * (2 * lax.rem(t, 2) - 1), zn)
+            body(j, j)
             return carry
 
         lax.fori_loop(1, zn, step, 0)

time: 126 us -> 126 us (level); the launches traced: 126 us -> 125 us
    pallas_call x1, Pallas kernels: 57.4 us -> 56.1 us  [row_sum(): pl.pallas_call(functools.partial(row_sum_kernel, n), out_shape=(jax.Shape...]
where the time goes in v13:
time: 126 us; the launch traced here: 125 us
  Pallas kernels  112 us (89%)
  local copies, waits for them, and re-layouts  9.5 us (8%)
  matrix products  2.86 us (2%)
    pallas_call x1, Pallas kernels, row_sum(): pl.pallas_call(functools.partial(row_sum_kernel, n), out_shape=(jax.Shape...  56.1 us
    pallas_call x1, Pallas kernels, call(): pl.pallas_call(kernel, out_shape=tuple((jax.ShapeDtypeStruct(shape, dtype...  55.4 us
    unnamed x24, local copies, waits for them, and re-layouts  4.36 us
    dot_general x6, matrix products, weight_terms(): jnp.einsum('aow,iw->oai', moved, full_row, preferred_element_type=jnp.flo...  2.86 us

profile of v13, /device:TPU:6, one launch (start us, length us, event | category | flops | bytes accessed | tf_op | source)
XLA Modules:
  0.0 124.9 jit_solution(4749547953436653710)
XLA Ops:
  0.6 1.0 copy.12
  1.6 0.9 copy.13.w2t
  2.5 55.4 %shard_map.67 = (bf16[512,512]{1,0:T(8,128)(2,1)}, bf16[512,512]{1,0:T(8,128)(2,1)}, bf16[32,512]{1,0:T(8,128)(2,1)}, bf16[32,512]{1,0:T(8,128)(2,1)}, bf16[32,5...) custom-call(bf16[32,512]{1,0:T(8,128)(2,1)} %bitcast.59, ...), custom_call_target="tpu_custom_call" | custom-call | tf_op jit(solution)/shard_map/pallas_call | solution.py:443
  57.9 0.0 copy-start.1
  57.9 0.0 copy-start.7
  58.0 0.0 copy-start.8
  58.0 0.0 copy-start.9
  58.0 1.4 %fusion.1 = bf16[32,3,1,512]{3,0,1,2:T(8,128)(2,1)S(1)} fusion(bf16[512,512]{1,0:T(8,128)(2,1)} %get-tuple-element.15, bf16[1,32,512]{2,1,0:T(8,128)(2,1)} %bitcast.70, bf16[1,32,512]{2,1,0:T(8,128)(2,1)} %bitcast.68, bf16[1,32,512]{2,1,0:T(8,128)(2,1)} %bitcast.72), kind=kOutput, calls=%fused_computation.7 | convolution fusion | flops 50675712 | bytes 720896 | tf_op jit(solution)/shard_map/aow,iw->oai/dot_general | solution.py:496
  59.4 0.0 copy-done.7
  59.4 0.0 copy-done.8
  59.4 0.0 copy-done.9
  59.4 0.0 copy-start.4
  59.4 0.0 copy-start.5
  59.4 0.0 copy-start.6
  59.5 0.0 copy-done.1
  59.5 0.7 copy-done.4
  60.2 0.0 copy-done.5
  60.2 0.0 copy-done.6
  60.2 0.3 fusion.4
  60.5 0.1 fusion.20
  60.6 0.3 fusion.3
  60.9 0.3 fusion.5
  61.3 0.3 copy.15
  61.5 0.0 copy-start
  61.5 1.0 convert_element_type.19.xb
  62.5 0.1 fusion.21
  62.6 0.0 copy-done
  62.6 0.3 fusion
  62.9 0.3 fusion.2
  63.3 0.3 copy.14
  63.5 1.0 convert_element_type.18.xa
  64.5 56.1 %shard_map.68 = (bf16[32,36,128]{2,1,0:T(8,128)(2,1)}, bf16[32,36,128]{2,1,0:T(8,128)(2,1)}) custom-call(bf16[32,36,128]{2,1,0:T(8,128)(2,1)} %convert_element_type.18.xa, bf16[32,36,128]{2,1,0:T(8,128)(2,1)} %convert_element_type.19.xb), custom_call_target="tpu_custom_call" | custom-call | tf_op jit(solution)/shard_map/pallas_call | solution.py:232
  120.7 1.3 %reshape.41 = f32[32,3,3,512]{3,2,1,0:T(4,128)S(1)} reshape(bf16[32,36,128]{2,1,0:T(8,128)(2,1)} %get-tuple-element.23) | data formatting | bytes 884736 | tf_op jit(solution)/shard_map/reshape | solution.py:538
  122.0 0.0 copy-start.2
  122.0 1.0 copy.16
  123.0 0.0 copy-done.2
  123.0 0.2 reshape.43
  123.2 0.0 copy-start.3
  123.3 1.0 copy.17
  124.3 0.0 copy-done.3
  124.3 0.6 copy.19
  (4 shorter events, 0.1 us)
Async XLA Ops:
  57.9 1.5 %copy-start.1 = (bf16[512,512]{1,0:T(8,128)(2,1)S(1)}, bf16[512,512]{1,0:T(8,128)(2,1)}, u32[]{:S(2)}) copy-start(bf16[512,512]{1,0:T(8,128)(2,1)} %get-tuple-element.19) | copy-start | bytes 1572868
  57.9 1.4 %copy-start.7 = (bf16[32,512]{1,0:T(8,128)(2,1)S(1)}, bf16[32,512]{1,0:T(8,128)(2,1)}, u32[]{:S(2)}) copy-start(bf16[32,512]{1,0:T(8,128)(2,1)} %get-tuple-element.17) | copy-start | bytes 98308
  58.0 1.4 %copy-start.8 = (bf16[32,512]{1,0:T(8,128)(2,1)S(1)}, bf16[32,512]{1,0:T(8,128)(2,1)}, u32[]{:S(2)}) copy-start(bf16[32,512]{1,0:T(8,128)(2,1)} %get-tuple-element.18) | copy-start | bytes 98308
  58.0 1.4 %copy-start.9 = (bf16[32,512]{1,0:T(8,128)(2,1)S(1)}, bf16[32,512]{1,0:T(8,128)(2,1)}, u32[]{:S(2)}) copy-start(bf16[32,512]{1,0:T(8,128)(2,1)} %get-tuple-element.16) | copy-start | bytes 98308
  59.4 0.8 copy-start.4
  59.4 0.8 copy-start.5
  59.4 0.8 copy-start.6
  61.5 1.1 copy-start
  122.0 1.0 copy-start.2
  123.2 1.0 copy-start.3

commit v14 on v13

--- a/solution.py
+++ b/solution.py
@@ -369,8 +369,16 @@
             lambda: each_filt_peer(lambda j, s: out(j, s).wait_send()))
 
 
+def weight_rows(rows3, full, wt_ref):
+    for b in range(3):
+        moved = rows3
+        if b != 1:
+            moved = lane_shift(rows3.astype(jnp.float32), 1 - b).astype(rows3.dtype)
+        wt_ref[b] = lax.dot_general(moved, full, (((1,), (1,)), ((), ())), preferred_element_type=jnp.float32)
+
+
 def block_kernel(feat, og, w1r, w2r, w2t, x_ref, h_ref, out_ref, gs_ref, gprev, gnext, gf_ref, fprev, fnext,
-                 p0s, p2s, from_prev, from_next, q0s, q2s, qprev, qnext, hsrc, pre1, tbuf, rbuf,
+                 wt_first, wt_second, p0s, p2s, from_prev, from_next, q0s, q2s, qprev, qnext, hsrc, pre1, tbuf, rbuf,
                  hsems, xsend, xrecv, fsend, frecv, sems1, sems2, sems3, tsend, trecv):
     nf = lax.axis_size("filt")
     mf = lax.axis_index("filt")
@@ -415,6 +423,8 @@
     def out(j, s):
         return rcopy(tbuf.at[j], rbuf.at[mf], tsend.at[j], trecv.at[mf], filt_dev(j))
 
+    weight_rows(rows3, h_ref[...], wt_second)
+
     def inc(j, s):
         return rcopy(tbuf.at[s], rbuf.at[s], tsend.at[s], trecv.at[s], filt_dev(s))
 
@@ -429,6 +439,7 @@
     gf_ref[...] = jnp.where(pre1[...] > 0, acc, 0.0).astype(gf_ref.dtype)
     halo3 = Halo(gf_ref, gf_ref, fprev, fnext, sems3)
     halo3.arrived()
+    weight_rows(jnp.concatenate([fnext[...], gf_ref[...], fprev[...]], axis=0), x_ref[...], wt_first)
     x_sent()
     h_sent()
     each_filt_peer(lambda j, s: out(j, s).wait_send())
@@ -518,19 +529,18 @@
     w2t = second_weight.transpose(2, 3, 1, 0).reshape(3, i_ch, 3 * o)
     sem = pltpu.SemaphoreType.DMA
     full = (n_filt * blk[0], blk[1])
-    x_row, h_row, block_out, grad_second, gs_prev, gs_next, grad_first, gf_prev, gf_next = call(
+    wt = (3, 3 * o, i_ch)
+    _, _, block_out, _, _, _, _, _, _, wt_first, wt_second = call(
         block_kernel,
         (feat, og, w1r, w2r, w2t),
-        [(full, bf16), (full, bf16)] + [(blk, bf16)] * 7,
+        [(full, bf16), (full, bf16)] + [(blk, bf16)] * 7 + [(wt, f32), (wt, f32)],
         [pltpu.VMEM(blk, f32)] * 8 + [pltpu.VMEM(blk, bf16), pltpu.VMEM(blk, f32),
                                       pltpu.VMEM((n_filt,) + blk, bf16), pltpu.VMEM((n_filt,) + blk, bf16)]
         + [sem((4,))] + [sem((n_filt,))] * 4 + [sem((4,))] * 3 + [sem((n_filt,))] * 2,
         2,
     )
-    gs3 = jnp.stack([gs_next, grad_second, gs_prev])
-    gf3 = jnp.stack([gf_next, grad_first, gf_prev])
-    second_local = weight_terms(gs3, h_row)
-    first_local = weight_terms(gf3, x_row)
+    second_local = wt_second.reshape(3, 3, o, i_ch).transpose(2, 1, 0, 3)
+    first_local = wt_first.reshape(3, 3, o, i_ch).transpose(2, 1, 0, 3)
     n_rows = lax.axis_size("rows")
     summed_first, summed_second = row_sum(
         first_local.astype(bf16).reshape(n_rows, -1, 128), second_local.astype(bf16).reshape(n_rows, -1, 128), 0

time: 126 us -> 125 us (level)
  matrix products: 2.86 us -> 0 us
  Pallas kernels: 112 us -> 114 us
    dot_general x6 -> x0, matrix products: 2.86 us -> none  [weight_terms(): jnp.einsum('aow,iw->oai', moved, full_row, preferred_element_type=jnp.flo...]
    reshape x0 -> x2, local copies, waits for them, and re-layouts: none -> 1.96 us  [the longest x1 0.98 us: per_device(): first_local.astype(bf16).reshape(n_rows, -1, 128)]
    pallas_call x1, Pallas kernels: 55.4 us -> 57.1 us  [call(): pl.pallas_call(kernel, out_shape=tuple((jax.ShapeDtypeStruct(shape, dtype...]
    unnamed x24 -> x10, local copies, waits for them, and re-layouts: 4.36 us -> 3.6 us
where the time goes in v14:
time: 125 us; the launch traced here: 124 us
  Pallas kernels  114 us (91%)
  local copies, waits for them, and re-layouts  8.56 us (7%)
    pallas_call x1, Pallas kernels, call(): pl.pallas_call(kernel, out_shape=tuple((jax.ShapeDtypeStruct(shape, dtype...  57.1 us
    pallas_call x1, Pallas kernels, row_sum(): pl.pallas_call(functools.partial(row_sum_kernel, n), out_shape=(jax.Shape...  56.6 us
    unnamed x10, local copies, waits for them, and re-layouts  3.6 us

profile of v14, /device:TPU:6, one launch (start us, length us, event | category | flops | bytes accessed | tf_op | source)
XLA Modules:
  0.0 124.1 jit_solution(14155288074131721928)
XLA Ops:
  0.6 1.0 copy.12
  1.6 0.9 copy.13.w2t
  2.5 57.1 %shard_map.67 = (bf16[512,512]{1,0:T(8,128)(2,1)}, bf16[512,512]{1,0:T(8,128)(2,1)}, bf16[32,512]{1,0:T(8,128)(2,1)}, bf16[32,512]{1,0:T(8,128)(2,1)}, bf16[32,5...) custom-call(bf16[32,512]{1,0:T(8,128)(2,1)} %bitcast.27, ...), custom_call_target="tpu_custom_call" | custom-call | tf_op jit(solution)/shard_map/pallas_call | solution.py:454
  59.7 1.1 convert_element_type.20
  60.8 0.0 copy-start
  60.8 0.3 copy.21
  61.0 1.0 reshape.40.xa
  62.0 0.0 copy-done
  62.1 0.3 copy.20
  62.3 1.0 reshape.41.xb
  63.3 56.6 %shard_map.68 = (bf16[32,36,128]{2,1,0:T(8,128)(2,1)}, bf16[32,36,128]{2,1,0:T(8,128)(2,1)}) custom-call(bf16[32,36,128]{2,1,0:T(8,128)(2,1)} %reshape.40.xa, bf16[32,36,128]{2,1,0:T(8,128)(2,1)} %reshape.41.xb), custom_call_target="tpu_custom_call" | custom-call | tf_op jit(solution)/shard_map/pallas_call | solution.py:232
  119.9 1.3 %reshape.47 = f32[32,3,3,512]{3,2,1,0:T(4,128)S(1)} reshape(bf16[32,36,128]{2,1,0:T(8,128)(2,1)} %get-tuple-element.11) | data formatting | bytes 884736 | tf_op jit(solution)/shard_map/reshape | solution.py:548
  121.2 0.0 copy-start.1
  121.2 1.0 copy.16
  122.2 0.0 copy-done.1
  122.2 0.2 reshape.49
  122.5 0.0 copy-start.2
  122.5 1.0 copy.17
  123.5 0.0 copy-done.2
  123.5 0.6 copy.23
  (1 shorter events, 0.0 us)
Async XLA Ops:
  60.8 1.3 %copy-start = (f32[3,96,512]{2,1,0:T(8,128)S(1)}, f32[3,96,512]{2,1,0:T(8,128)}, u32[]{:S(2)}) copy-start(f32[3,96,512]{2,1,0:T(8,128)} %get-tuple-element.10) | copy-start | bytes 1769476
  121.2 1.0 copy-start.1
  122.5 1.0 copy-start.2

commit v15 on v14

--- a/solution.py
+++ b/solution.py
@@ -374,11 +374,13 @@
         moved = rows3
         if b != 1:
             moved = lane_shift(rows3.astype(jnp.float32), 1 - b).astype(rows3.dtype)
-        wt_ref[b] = lax.dot_general(moved, full, (((1,), (1,)), ((), ())), preferred_element_type=jnp.float32)
-
-
-def block_kernel(feat, og, w1r, w2r, w2t, x_ref, h_ref, out_ref, gs_ref, gprev, gnext, gf_ref, fprev, fnext,
-                 wt_first, wt_second, p0s, p2s, from_prev, from_next, q0s, q2s, qprev, qnext, hsrc, pre1, tbuf, rbuf,
+        wt_ref[b] = lax.dot_general(
+            moved, full, (((1,), (1,)), ((), ())), preferred_element_type=jnp.float32
+        ).astype(wt_ref.dtype)
+
+
+def block_kernel(feat, og, w1r, w2r, w2t, out_ref, gs_ref, gprev, gnext, gf_ref, fprev, fnext,
+                 wt_first, wt_second, x_ref, h_ref, p0s, p2s, from_prev, from_next, q0s, q2s, qprev, qnext, hsrc, pre1, tbuf, rbuf,
                  hsems, xsend, xrecv, fsend, frecv, sems1, sems2, sems3, tsend, trecv):
     nf = lax.axis_size("filt")
     mf = lax.axis_index("filt")
@@ -530,11 +532,11 @@
     sem = pltpu.SemaphoreType.DMA
     full = (n_filt * blk[0], blk[1])
     wt = (3, 3 * o, i_ch)
-    _, _, block_out, _, _, _, _, _, _, wt_first, wt_second = call(
+    block_out, _, _, _, _, _, _, wt_first, wt_second = call(
         block_kernel,
         (feat, og, w1r, w2r, w2t),
-        [(full, bf16), (full, bf16)] + [(blk, bf16)] * 7 + [(wt, f32), (wt, f32)],
-        [pltpu.VMEM(blk, f32)] * 8 + [pltpu.VMEM(blk, bf16), pltpu.VMEM(blk, f32),
+        [(blk, bf16)] * 7 + [(wt, bf16), (wt, bf16)],
+        [pltpu.VMEM(full, bf16), pltpu.VMEM(full, bf16)] + [pltpu.VMEM(blk, f32)] * 8 + [pltpu.VMEM(blk, bf16), pltpu.VMEM(blk, f32),
                                       pltpu.VMEM((n_filt,) + blk, bf16), pltpu.VMEM((n_filt,) + blk, bf16)]
         + [sem((4,))] + [sem((n_filt,))] * 4 + [sem((4,))] * 3 + [sem((n_filt,))] * 2,
         2,
@@ -543,7 +545,7 @@
     first_local = wt_first.reshape(3, 3, o, i_ch).transpose(2, 1, 0, 3)
     n_rows = lax.axis_size("rows")
     summed_first, summed_second = row_sum(
-        first_local.astype(bf16).reshape(n_rows, -1, 128), second_local.astype(bf16).reshape(n_rows, -1, 128), 0
+        first_local.reshape(n_rows, -1, 128), second_local.reshape(n_rows, -1, 128), 0
     )
     first_grad = summed_first.astype(f32).reshape(first_local.shape)
     second_grad = summed_second.astype(f32).reshape(second_local.shape)

time: 125 us -> 125 us (level)
    reshape x2 -> x4, local copies, waits for them, and re-layouts: 1.96 us -> 3.44 us  [the longest x1 1.22 us: per_device(): first_local = wt_first.reshape(3, 3, o, i_ch).transpose(2, 1, 0, 3)]
where the time goes in v15:
time: 125 us; the launch traced here: 123 us
  Pallas kernels  113 us (90%)
  local copies, waits for them, and re-layouts  9.52 us (8%)
    pallas_call x1, Pallas kernels, call(): pl.pallas_call(kernel, out_shape=tuple((jax.ShapeDtypeStruct(shape, dtype...  56.6 us
    pallas_call x1, Pallas kernels, row_sum(): pl.pallas_call(functools.partial(row_sum_kernel, n), out_shape=(jax.Shape...  56.5 us
    unnamed x10, local copies, waits for them, and re-layouts  3.6 us

profile of v15, /device:TPU:6, one launch (start us, length us, event | category | flops | bytes accessed | tf_op | source)
XLA Modules:
  0.0 123.4 jit_solution(13100242855183014488)
XLA Ops:
  0.6 1.0 copy.12
  1.6 0.9 copy.13.w2t
  2.5 56.6 %shard_map.67 = (bf16[32,512]{1,0:T(8,128)(2,1)}, bf16[32,512]{1,0:T(8,128)(2,1)}, bf16[32,512]{1,0:T(8,128)(2,1)}, bf16[32,512]{1,0:T(8,128)(2,1)}, bf16[32,512...) custom-call(bf16[32,512]{1,0:T(8,128)(2,1)} %bitcast.27, ...), custom_call_target="tpu_custom_call" | custom-call | tf_op jit(solution)/shard_map/pallas_call | solution.py:456
  59.2 1.2 copy.21
  60.4 0.0 copy-start.1
  60.4 1.0 reshape.43.xa
  61.4 0.0 copy-done.1
  61.4 0.3 copy.20
  61.6 1.0 reshape.45.xb
  62.6 56.5 %shard_map.68 = (bf16[32,36,128]{2,1,0:T(8,128)(2,1)}, bf16[32,36,128]{2,1,0:T(8,128)(2,1)}) custom-call(bf16[32,36,128]{2,1,0:T(8,128)(2,1)} %reshape.43.xa, bf16[32,36,128]{2,1,0:T(8,128)(2,1)} %reshape.45.xb), custom_call_target="tpu_custom_call" | custom-call | tf_op jit(solution)/shard_map/pallas_call | solution.py:232
  119.2 1.3 %reshape.51 = f32[32,3,3,512]{3,2,1,0:T(4,128)S(1)} reshape(bf16[32,36,128]{2,1,0:T(8,128)(2,1)} %get-tuple-element.11) | data formatting | bytes 884736 | tf_op jit(solution)/shard_map/reshape | solution.py:550
  120.5 0.0 copy-start
  120.5 1.0 copy.16
  121.5 0.0 copy-done
  121.5 0.2 reshape.53
  121.7 0.0 copy-start.2
  121.8 1.0 copy.17
  122.7 0.0 copy-done.2
  122.8 0.6 copy.23
Async XLA Ops:
  60.4 1.0 copy-start.1
  120.5 1.0 copy-start
  121.7 1.0 copy-start.2

commit v16 on v15

--- a/solution.py
+++ b/solution.py
@@ -182,7 +182,7 @@
         self.back().wait_send()
 
 
-def row_sum_kernel(n, xa, xb, oa, ob, *scratch):
+def row_sum_kernel(n, xa, xb, fa, fb, oa, ob, *scratch):
     zn = n // 2
     me = lax.axis_index("rows")
     my_z = lax.rem(me, zn)
@@ -219,19 +219,26 @@
     a.s4_finish()
     b.s4_finish()
 
+    def widen(c, carry):
+        fa[c] = oa[c].astype(fa.dtype)
+        fb[c] = ob[c].astype(fb.dtype)
+        return carry
+
+    lax.fori_loop(0, n, widen, 0)
+
 
 def row_sum(xa, xb, collective_id):
     n = xa.shape[0]
     zn = n // 2
     spec = pl.BlockSpec(memory_space=pltpu.VMEM)
-    scratch = []
+    scratch = [pltpu.VMEM(xa.shape, xa.dtype), pltpu.VMEM(xb.shape, xb.dtype)]
     for x in (xa, xb):
         blk = (zn,) + x.shape[1:]
         scratch += [pltpu.VMEM(blk, x.dtype), pltpu.VMEM(blk, x.dtype), pltpu.VMEM(blk, x.dtype),
                     pltpu.SemaphoreType.DMA((6, zn))]
     return pl.pallas_call(
         functools.partial(row_sum_kernel, n),
-        out_shape=(jax.ShapeDtypeStruct(xa.shape, xa.dtype), jax.ShapeDtypeStruct(xb.shape, xb.dtype)),
+        out_shape=(jax.ShapeDtypeStruct(xa.shape, jnp.float32), jax.ShapeDtypeStruct(xb.shape, jnp.float32)),
         in_specs=[spec, spec],
         out_specs=(spec, spec),
         scratch_shapes=scratch,
@@ -547,8 +554,8 @@
     summed_first, summed_second = row_sum(
         first_local.reshape(n_rows, -1, 128), second_local.reshape(n_rows, -1, 128), 0
     )
-    first_grad = summed_first.astype(f32).reshape(first_local.shape)
-    second_grad = summed_second.astype(f32).reshape(second_local.shape)
+    first_grad = summed_first.reshape(first_local.shape)
+    second_grad = summed_second.reshape(second_local.shape)
     return (block_out[:, None, :], first_grad, second_grad)
 
 

time: 125 us -> 125 us (level)
  no operation moved by 1% of the time
where the time goes in v16:
time: 125 us; the launch traced here: 124 us
  Pallas kernels  114 us (91%)
  local copies, waits for them, and re-layouts  9.64 us (8%)
    pallas_call x1, Pallas kernels, row_sum(): pl.pallas_call(functools.partial(row_sum_kernel, n), out_shape=(jax.Shape...  57.1 us
    pallas_call x1, Pallas kernels, call(): pl.pallas_call(kernel, out_shape=tuple((jax.ShapeDtypeStruct(shape, dtype...  56.6 us
    unnamed x10, local copies, waits for them, and re-layouts  3.68 us

profile of v16, /device:TPU:6, one launch (start us, length us, event | category | flops | bytes accessed | tf_op | source)
XLA Modules:
  0.0 124.0 jit_solution(3887170780742671443)
XLA Ops:
  0.6 1.0 copy.12
  1.6 0.9 copy.13.w2t
  2.5 56.6 %shard_map.67 = (bf16[32,512]{1,0:T(8,128)(2,1)}, bf16[32,512]{1,0:T(8,128)(2,1)}, bf16[32,512]{1,0:T(8,128)(2,1)}, bf16[32,512]{1,0:T(8,128)(2,1)}, bf16[32,512...) custom-call(bf16[32,512]{1,0:T(8,128)(2,1)} %bitcast.27, ...), custom_call_target="tpu_custom_call" | custom-call | tf_op jit(solution)/shard_map/pallas_call | solution.py:463
  59.2 1.2 copy.21
  60.4 0.0 copy-start.1
  60.4 1.0 reshape.37.xa
  61.4 0.0 copy-done.1
  61.4 0.3 copy.20
  61.6 1.0 reshape.39.xb
  62.6 57.1 %shard_map.68 = (f32[32,36,128]{2,1,0:T(8,128)}, f32[32,36,128]{2,1,0:T(8,128)}) custom-call(bf16[32,36,128]{2,1,0:T(8,128)(2,1)} %reshape.37.xa, bf16[32,36,128]{2,1,0:T(8,128)(2,1)} %reshape.39.xb), custom_call_target="tpu_custom_call" | custom-call | tf_op jit(solution)/shard_map/pallas_call | solution.py:239
  119.7 1.4 %reshape.40 = f32[32,3,3,512]{3,2,1,0:T(4,128)S(1)} reshape(f32[32,36,128]{2,1,0:T(8,128)} %get-tuple-element.11) | data formatting | bytes 1179648 | tf_op jit(solution)/shard_map/reshape | solution.py:557
  121.1 0.0 copy-start
  121.1 1.0 copy.16
  122.1 0.1 copy-done
  122.2 0.2 reshape.41
  122.4 0.0 copy-start.2
  122.4 1.0 copy.17
  123.4 0.0 copy-done.2
  123.4 0.6 copy.23
Async XLA Ops:
  60.4 1.0 copy-start.1
  121.1 1.1 copy-start
  122.4 1.0 copy-start.2

commit v17 on v15

--- a/solution.py
+++ b/solution.py
@@ -541,14 +541,12 @@
         + [sem((4,))] + [sem((n_filt,))] * 4 + [sem((4,))] * 3 + [sem((n_filt,))] * 2,
         2,
     )
-    second_local = wt_second.reshape(3, 3, o, i_ch).transpose(2, 1, 0, 3)
-    first_local = wt_first.reshape(3, 3, o, i_ch).transpose(2, 1, 0, 3)
     n_rows = lax.axis_size("rows")
     summed_first, summed_second = row_sum(
-        first_local.reshape(n_rows, -1, 128), second_local.reshape(n_rows, -1, 128), 0
+        wt_first.reshape(n_rows, -1, 128), wt_second.reshape(n_rows, -1, 128), 0
     )
-    first_grad = summed_first.astype(f32).reshape(first_local.shape)
-    second_grad = summed_second.astype(f32).reshape(second_local.shape)
+    first_grad = summed_first.astype(f32).reshape(3, 3, o, i_ch).transpose(2, 1, 0, 3)
+    second_grad = summed_second.astype(f32).reshape(3, 3, o, i_ch).transpose(2, 1, 0, 3)
     return (block_out[:, None, :], first_grad, second_grad)
 
 

time: 125 us -> 124 us (level)
    reshape x6 -> x2, local copies, waits for them, and re-layouts: 5 us -> 2.94 us  [the longest x1 1.97 us: per_device(): wt_first.reshape(n_rows, -1, 128)]
    transpose x0 -> x2, local copies, waits for them, and re-layouts: none -> 1.42 us  [the longest x1 1.2 us: per_device(): summed_first.astype(f32).reshape(3, 3, o, i_ch).transpose(2, 1, 0, 3)]
where the time goes in v17:
time: 124 us; the launch traced here: 123 us
  Pallas kernels  113 us (91%)
  local copies, waits for them, and re-layouts  8.74 us (7%)
    pallas_call x1, Pallas kernels, call(): pl.pallas_call(kernel, out_shape=tuple((jax.ShapeDtypeStruct(shape, dtype...  56.6 us
    pallas_call x1, Pallas kernels, row_sum(): pl.pallas_call(functools.partial(row_sum_kernel, n), out_shape=(jax.Shape...  56.5 us
    unnamed x10, local copies, waits for them, and re-layouts  3.47 us

profile of v17, /device:TPU:6, one launch (start us, length us, event | category | flops | bytes accessed | tf_op | source)
XLA Modules:
  0.0 122.6 jit_solution(9794876433216764924)
XLA Ops:
  0.6 1.0 copy.10
  1.6 0.9 copy.11.w2t
  2.5 56.6 %shard_map.67 = (bf16[32,512]{1,0:T(8,128)(2,1)}, bf16[32,512]{1,0:T(8,128)(2,1)}, bf16[32,512]{1,0:T(8,128)(2,1)}, bf16[32,512]{1,0:T(8,128)(2,1)}, bf16[32,512...) custom-call(bf16[32,512]{1,0:T(8,128)(2,1)} %bitcast.19, ...), custom_call_target="tpu_custom_call" | custom-call | tf_op jit(solution)/shard_map/pallas_call | solution.py:456
  59.2 0.0 copy-start.1
  59.2 2.0 %reshape.32.xa = bf16[32,36,128]{2,1,0:T(8,128)(2,1)} reshape(bf16[3,96,512]{2,1,0:T(8,128)(2,1)} %get-tuple-element.9) | data formatting | bytes 589824 | tf_op jit(solution)/shard_map/reshape | solution.py:546
  61.1 0.0 copy-done.1
  61.1 1.0 reshape.33.xb
  62.1 56.5 %shard_map.68 = (bf16[32,36,128]{2,1,0:T(8,128)(2,1)}, bf16[32,36,128]{2,1,0:T(8,128)(2,1)}) custom-call(bf16[32,36,128]{2,1,0:T(8,128)(2,1)} %reshape.32.xa, bf16[32,36,128]{2,1,0:T(8,128)(2,1)} %reshape.33.xb), custom_call_target="tpu_custom_call" | custom-call | tf_op jit(solution)/shard_map/pallas_call | solution.py:232
  118.7 1.2 reshape.36
  119.9 0.0 copy-start
  119.9 0.9 copy.12
  120.7 0.1 copy-done
  120.9 0.2 reshape.37
  121.1 0.0 copy-start.2
  121.1 0.9 copy.13
  122.0 0.0 copy-done.2
  122.0 0.6 copy.15
Async XLA Ops:
  59.2 2.0 %copy-start.1 = (bf16[3,96,512]{2,1,0:T(8,128)(2,1)S(1)}, bf16[3,96,512]{2,1,0:T(8,128)(2,1)}, u32[]{:S(2)}) copy-start(bf16[3,96,512]{2,1,0:T(8,128)(2,1)} %get-tuple-element.10) | copy-start | bytes 884740
  119.9 1.0 copy-start
  121.1 0.9 copy-start.2

commit v18 on v17

--- a/solution.py
+++ b/solution.py
@@ -182,7 +182,7 @@
         self.back().wait_send()
 
 
-def row_sum_kernel(n, xa, xb, oa, ob, *scratch):
+def row_sum_kernel(n, split, x32, f32_out, xa, xb, oa, ob, *scratch):
     zn = n // 2
     me = lax.axis_index("rows")
     my_z = lax.rem(me, zn)
@@ -191,6 +191,12 @@
     def dev(j):
         return (j, lax.axis_index("filt"))
 
+    def narrow(c, carry):
+        xa[c] = x32[c, pl.ds(0, split), :].astype(xa.dtype)
+        xb[c] = x32[c, pl.ds(split, x32.shape[1] - split), :].astype(xb.dtype)
+        return carry
+
+    lax.fori_loop(0, n, narrow, 0)
     barrier = pltpu.get_barrier_semaphore()
     pl.semaphore_signal(barrier, 1, device_id=dev(lax.rem(me + zn, n)), device_id_type=MESH)
 
@@ -219,24 +225,32 @@
     a.s4_finish()
     b.s4_finish()
 
-
-def row_sum(xa, xb, collective_id):
-    n = xa.shape[0]
+    def widen(c, carry):
+        f32_out[c, pl.ds(0, split), :] = oa[c].astype(f32_out.dtype)
+        f32_out[c, pl.ds(split, x32.shape[1] - split), :] = ob[c].astype(f32_out.dtype)
+        return carry
+
+    lax.fori_loop(0, n, widen, 0)
+
+
+def row_sum(x, collective_id):
+    n, k, _ = x.shape
     zn = n // 2
+    split = 8 * (k // 16)
     spec = pl.BlockSpec(memory_space=pltpu.VMEM)
-    scratch = []
-    for x in (xa, xb):
-        blk = (zn,) + x.shape[1:]
-        scratch += [pltpu.VMEM(blk, x.dtype), pltpu.VMEM(blk, x.dtype), pltpu.VMEM(blk, x.dtype),
-                    pltpu.SemaphoreType.DMA((6, zn))]
+    halves = [(n, split, 128), (n, k - split, 128)]
+    scratch = [pltpu.VMEM(h, jnp.bfloat16) for h in halves] * 2
+    for h in halves:
+        blk = (zn,) + h[1:]
+        scratch += [pltpu.VMEM(blk, jnp.bfloat16)] * 3 + [pltpu.SemaphoreType.DMA((6, zn))]
     return pl.pallas_call(
-        functools.partial(row_sum_kernel, n),
-        out_shape=(jax.ShapeDtypeStruct(xa.shape, xa.dtype), jax.ShapeDtypeStruct(xb.shape, xb.dtype)),
-        in_specs=[spec, spec],
-        out_specs=(spec, spec),
+        functools.partial(row_sum_kernel, n, split),
+        out_shape=jax.ShapeDtypeStruct(x.shape, jnp.float32),
+        in_specs=[spec],
+        out_specs=spec,
         scratch_shapes=scratch,
         compiler_params=pltpu.CompilerParams(collective_id=collective_id, has_side_effects=True),
-    )(xa, xb)
+    )(x)
 
 
 def row_dev(j):
@@ -369,18 +383,20 @@
             lambda: each_filt_peer(lambda j, s: out(j, s).wait_send()))
 
 
-def weight_rows(rows3, full, wt_ref):
+def weight_rows(rows3, full, wt_ref, base):
+    nq = full.shape[0] // 128
+    ao = rows3.shape[0]
     for b in range(3):
         moved = rows3
         if b != 1:
             moved = lane_shift(rows3.astype(jnp.float32), 1 - b).astype(rows3.dtype)
-        wt_ref[b] = lax.dot_general(
-            moved, full, (((1,), (1,)), ((), ())), preferred_element_type=jnp.float32
-        ).astype(wt_ref.dtype)
+        part = lax.dot_general(moved, full, (((1,), (1,)), ((), ())), preferred_element_type=jnp.float32)
+        for q in range(nq):
+            wt_ref[pl.ds(base + (b * nq + q) * ao, ao), :] = part[:, q * 128:(q + 1) * 128]
 
 
 def block_kernel(feat, og, w1r, w2r, w2t, out_ref, gs_ref, gprev, gnext, gf_ref, fprev, fnext,
-                 wt_first, wt_second, x_ref, h_ref, p0s, p2s, from_prev, from_next, q0s, q2s, qprev, qnext, hsrc, pre1, tbuf, rbuf,
+                 wt_all, x_ref, h_ref, p0s, p2s, from_prev, from_next, q0s, q2s, qprev, qnext, hsrc, pre1, tbuf, rbuf,
                  hsems, xsend, xrecv, fsend, frecv, sems1, sems2, sems3, tsend, trecv):
     nf = lax.axis_size("filt")
     mf = lax.axis_index("filt")
@@ -425,7 +441,7 @@
     def out(j, s):
         return rcopy(tbuf.at[j], rbuf.at[mf], tsend.at[j], trecv.at[mf], filt_dev(j))
 
-    weight_rows(rows3, h_ref[...], wt_second)
+    weight_rows(rows3, h_ref[...], wt_all, wt_all.shape[0] // 2)
 
     def inc(j, s):
         return rcopy(tbuf.at[s], rbuf.at[s], tsend.at[s], trecv.at[s], filt_dev(s))
@@ -441,7 +457,7 @@
     gf_ref[...] = jnp.where(pre1[...] > 0, acc, 0.0).astype(gf_ref.dtype)
     halo3 = Halo(gf_ref, gf_ref, fprev, fnext, sems3)
     halo3.arrived()
-    weight_rows(jnp.concatenate([fnext[...], gf_ref[...], fprev[...]], axis=0), x_ref[...], wt_first)
+    weight_rows(jnp.concatenate([fnext[...], gf_ref[...], fprev[...]], axis=0), x_ref[...], wt_all, 0)
     x_sent()
     h_sent()
     each_filt_peer(lambda j, s: out(j, s).wait_send())
@@ -531,22 +547,21 @@
     w2t = second_weight.transpose(2, 3, 1, 0).reshape(3, i_ch, 3 * o)
     sem = pltpu.SemaphoreType.DMA
     full = (n_filt * blk[0], blk[1])
-    wt = (3, 3 * o, i_ch)
-    block_out, _, _, _, _, _, _, wt_first, wt_second = call(
+    nq = i_ch // 128
+    wt = (2 * 3 * nq * 3 * o, 128)
+    block_out, _, _, _, _, _, _, wt_all = call(
         block_kernel,
         (feat, og, w1r, w2r, w2t),
-        [(blk, bf16)] * 7 + [(wt, bf16), (wt, bf16)],
+        [(blk, bf16)] * 7 + [(wt, f32)],
         [pltpu.VMEM(full, bf16), pltpu.VMEM(full, bf16)] + [pltpu.VMEM(blk, f32)] * 8 + [pltpu.VMEM(blk, bf16), pltpu.VMEM(blk, f32),
                                       pltpu.VMEM((n_filt,) + blk, bf16), pltpu.VMEM((n_filt,) + blk, bf16)]
         + [sem((4,))] + [sem((n_filt,))] * 4 + [sem((4,))] * 3 + [sem((n_filt,))] * 2,
         2,
     )
     n_rows = lax.axis_size("rows")
-    summed_first, summed_second = row_sum(
-        wt_first.reshape(n_rows, -1, 128), wt_second.reshape(n_rows, -1, 128), 0
-    )
-    first_grad = summed_first.astype(f32).reshape(3, 3, o, i_ch).transpose(2, 1, 0, 3)
-    second_grad = summed_second.astype(f32).reshape(3, 3, o, i_ch).transpose(2, 1, 0, 3)
+    summed = row_sum(wt_all.reshape(n_rows, -1, 128), 0)
+    grads = summed.reshape(2, 3, nq, 3, o, 128).transpose(0, 4, 3, 1, 2, 5).reshape(2, o, 3, 3, i_ch)
+    first_grad, second_grad = grads[0], grads[1]
     return (block_out[:, None, :], first_grad, second_grad)
 
 

time: 124 us -> 119 us (0.960)
  Pallas kernels: 113 us -> 111 us
  local copies, waits for them, and re-layouts: 8.74 us -> 6.75 us
    reshape x2 -> x0, local copies, waits for them, and re-layouts: 2.94 us -> none  [the longest x1 1.97 us: per_device(): wt_first.reshape(n_rows, -1, 128)]
    pallas_call x1, Pallas kernels: 56.5 us -> 54 us  [row_sum(): pl.pallas_call(functools.partial(row_sum_kernel, n, split), out_shape=jax...]
    slice x0 -> x3, local copies, waits for them, and re-layouts: none -> 2.12 us  [per_device(): first_grad, second_grad = (grads[0], grads[1])]
    squeeze x0 -> x2, local copies, waits for them, and re-layouts: none -> 2.1 us  [per_device(): first_grad, second_grad = (grads[0], grads[1])]
    unnamed x10 -> x4, local copies, waits for them, and re-layouts: 3.47 us -> 1.6 us
    transpose x2 -> x0, local copies, waits for them, and re-layouts: 1.42 us -> none  [the longest x1 1.2 us: per_device(): summed_first.astype(f32).reshape(3, 3, o, i_ch).transpose(2, 1, 0, 3)]
where the time goes in v18:
time: 119 us; the launch traced here: 118 us
  Pallas kernels  111 us (93%)
  local copies, waits for them, and re-layouts  6.75 us (6%)
    pallas_call x1, Pallas kernels, call(): pl.pallas_call(kernel, out_shape=tuple((jax.ShapeDtypeStruct(shape, dtype...  56.8 us
    pallas_call x1, Pallas kernels, row_sum(): pl.pallas_call(functools.partial(row_sum_kernel, n, split), out_shape=jax...  54 us

profile of v18, /device:TPU:6, one launch (start us, length us, event | category | flops | bytes accessed | tf_op | source)
XLA Modules:
  0.0 118.3 jit_solution(4259710418436569731)
XLA Ops:
  0.6 1.0 copy.10
  1.6 0.9 copy.11.w2t
  2.5 56.8 %shard_map.67 = (bf16[32,512]{1,0:T(8,128)(2,1)}, bf16[32,512]{1,0:T(8,128)(2,1)}, bf16[32,512]{1,0:T(8,128)(2,1)}, bf16[32,512]{1,0:T(8,128)(2,1)}, bf16[32,512...) custom-call(bf16[32,512]{1,0:T(8,128)(2,1)} %bitcast.25, ...), custom_call_target="tpu_custom_call" | custom-call | tf_op jit(solution)/shard_map/pallas_call | solution.py:472
  59.3 54.0 %shard_map.68 = f32[32,72,128]{2,1,0:T(8,128)} custom-call(f32[32,72,128]{2,1,0:T(8,128)} %bitcast.21), custom_call_target="tpu_custom_call" | custom-call | tf_op jit(solution)/shard_map/pallas_call | solution.py:246
  113.4 1.4 %fusion = (f32[1,32,3,3,4,128]{5,1,2,4,3,0:T(8,128)S(1)}, f32[1,32,3,3,4,128]{5,1,2,4,3,0:T(8,128)S(1)}) fusion(f32[2,32,3,3,4,128]{5,1,2,4,3,0:T(8,128)} %bitcast.20), kind=kLoop, calls=%fused_computation | loop fusion | bytes 2359296 | tf_op jit(solution)/shard_map/slice | solution.py:564
  114.8 0.4 copy.13
  115.1 1.1 squeeze.15
  116.2 0.0 copy-start
  116.2 0.4 copy.12
  116.6 1.1 squeeze.14
  117.6 0.0 copy-done
  117.6 0.6 copy.15
Async XLA Ops:
  116.2 1.4 %copy-start = (bf16[32,512]{1,0:T(8,128)(2,1)S(1)}, bf16[32,512]{1,0:T(8,128)(2,1)}, u32[]{:S(2)}) copy-start(bf16[32,512]{1,0:T(8,128)(2,1)} %get-tuple-element.5) | copy-start | bytes 98308

commit v19 on v18

--- a/solution.py
+++ b/solution.py
@@ -560,8 +560,10 @@
     )
     n_rows = lax.axis_size("rows")
     summed = row_sum(wt_all.reshape(n_rows, -1, 128), 0)
-    grads = summed.reshape(2, 3, nq, 3, o, 128).transpose(0, 4, 3, 1, 2, 5).reshape(2, o, 3, 3, i_ch)
-    first_grad, second_grad = grads[0], grads[1]
+    first_grad, second_grad = (
+        half.reshape(3, nq, 3, o, 128).transpose(3, 2, 0, 1, 4).reshape(o, 3, 3, i_ch)
+        for half in (summed[: n_rows // 2], summed[n_rows // 2:])
+    )
     return (block_out[:, None, :], first_grad, second_grad)
 
 

time: 119 us -> 119 us (level)
    squeeze x2 -> x0, local copies, waits for them, and re-layouts: 2.1 us -> none  [per_device(): first_grad, second_grad = (grads[0], grads[1])]
    reshape x0 -> x2, local copies, waits for them, and re-layouts: none -> 2.1 us  [per_device(): half.reshape(3, nq, 3, o, 128).transpose(3, 2, 0, 1, 4)]
where the time goes in v19:
time: 119 us; the launch traced here: 118 us
  Pallas kernels  111 us (93%)
  local copies, waits for them, and re-layouts  6.72 us (6%)
    pallas_call x1, Pallas kernels, call(): pl.pallas_call(kernel, out_shape=tuple((jax.ShapeDtypeStruct(shape, dtype...  56.8 us
    pallas_call x1, Pallas kernels, row_sum(): pl.pallas_call(functools.partial(row_sum_kernel, n, split), out_shape=jax...  54 us

profile of v19, /device:TPU:6, one launch (start us, length us, event | category | flops | bytes accessed | tf_op | source)
XLA Modules:
  0.0 118.2 jit_solution(5116288903940216826)
XLA Ops:
  0.6 1.0 copy.10
  1.6 0.9 copy.11.w2t
  2.5 56.8 %shard_map.67 = (bf16[32,512]{1,0:T(8,128)(2,1)}, bf16[32,512]{1,0:T(8,128)(2,1)}, bf16[32,512]{1,0:T(8,128)(2,1)}, bf16[32,512]{1,0:T(8,128)(2,1)}, bf16[32,512...) custom-call(bf16[32,512]{1,0:T(8,128)(2,1)} %bitcast.29, ...), custom_call_target="tpu_custom_call" | custom-call | tf_op jit(solution)/shard_map/pallas_call | solution.py:472
  59.3 54.0 %shard_map.68 = f32[32,72,128]{2,1,0:T(8,128)} custom-call(f32[32,72,128]{2,1,0:T(8,128)} %bitcast.25), custom_call_target="tpu_custom_call" | custom-call | tf_op jit(solution)/shard_map/pallas_call | solution.py:246
  113.4 1.3 %fusion = (f32[16,72,128]{2,1,0:T(8,128)S(1)}, f32[16,72,128]{2,1,0:T(8,128)S(1)}) fusion(f32[32,72,128]{2,1,0:T(8,128)} %shard_map.68), kind=kLoop, calls=%fused_computation | loop fusion | bytes 2359296 | tf_op jit(solution)/shard_map/slice | solution.py:565
  114.7 0.4 copy.13
  115.1 1.1 reshape.37
  116.2 0.0 copy-start
  116.2 0.4 copy.12
  116.6 1.1 reshape.35
  117.6 0.0 copy-done
  117.6 0.6 copy.15
Async XLA Ops:
  116.2 1.4 %copy-start = (bf16[32,512]{1,0:T(8,128)(2,1)S(1)}, bf16[32,512]{1,0:T(8,128)(2,1)}, u32[]{:S(2)}) copy-start(bf16[32,512]{1,0:T(8,128)(2,1)} %get-tuple-element.5) | copy-start | bytes 98308

commit v20 on v19

--- a/solution.py
+++ b/solution.py
@@ -395,7 +395,7 @@
             wt_ref[pl.ds(base + (b * nq + q) * ao, ao), :] = part[:, q * 128:(q + 1) * 128]
 
 
-def block_kernel(feat, og, w1r, w2r, w2t, out_ref, gs_ref, gprev, gnext, gf_ref, fprev, fnext,
+def block_kernel(feat, og, w1r, w2r, out_ref, gs_ref, gprev, gnext, gf_ref, fprev, fnext,
                  wt_all, x_ref, h_ref, p0s, p2s, from_prev, from_next, q0s, q2s, qprev, qnext, hsrc, pre1, tbuf, rbuf,
                  hsems, xsend, xrecv, fsend, frecv, sems1, sems2, sems3, tsend, trecv):
     nf = lax.axis_size("filt")
@@ -424,19 +424,17 @@
     halo2 = Halo(gs_ref, gs_ref, gprev, gnext, sems2)
     halo2.arrived()
     rows3 = jnp.concatenate([gnext[...], gs_ref[...], gprev[...]], axis=0)
-
-    def block(t, carry):
-        rows = pl.ds(pl.multiple_of(t * blk, blk), blk)
+    per = 128 // blk
+    for q in range(w2r.shape[2] // 128):
         total = None
         for b in range(3):
-            part = jnp.dot(w2t[b, rows, :], rows3, preferred_element_type=jnp.float32)
+            lhs = jnp.concatenate([w2r[a * 3 + b, :, q * 128:(q + 1) * 128] for a in range(3)], axis=0)
+            part = lax.dot_general(lhs, rows3, (((0,), (0,)), ((), ())), preferred_element_type=jnp.float32)
             if b != 1:
                 part = lane_shift(part, 1 - b)
             total = part if total is None else total + part
-        tbuf[t] = total.astype(tbuf.dtype)
-        return carry
-
-    lax.fori_loop(0, nf, block, 0)
+        for u in range(per):
+            tbuf[q * per + u] = total[u * blk:(u + 1) * blk].astype(tbuf.dtype)
 
     def out(j, s):
         return rcopy(tbuf.at[j], rbuf.at[mf], tsend.at[j], trecv.at[mf], filt_dev(j))
@@ -544,14 +542,13 @@
     o, _, _, i_ch = first_weight.shape
     w1r = first_weight.transpose(1, 2, 0, 3).reshape(9, o, i_ch)
     w2r = second_weight.transpose(1, 2, 0, 3).reshape(9, o, i_ch)
-    w2t = second_weight.transpose(2, 3, 1, 0).reshape(3, i_ch, 3 * o)
     sem = pltpu.SemaphoreType.DMA
     full = (n_filt * blk[0], blk[1])
     nq = i_ch // 128
     wt = (2 * 3 * nq * 3 * o, 128)
     block_out, _, _, _, _, _, _, wt_all = call(
         block_kernel,
-        (feat, og, w1r, w2r, w2t),
+        (feat, og, w1r, w2r),
         [(blk, bf16)] * 7 + [(wt, f32)],
         [pltpu.VMEM(full, bf16), pltpu.VMEM(full, bf16)] + [pltpu.VMEM(blk, f32)] * 8 + [pltpu.VMEM(blk, bf16), pltpu.VMEM(blk, f32),
                                       pltpu.VMEM((n_filt,) + blk, bf16), pltpu.VMEM((n_filt,) + blk, bf16)]

time: 119 us -> 114 us (0.958)
  Pallas kernels: 111 us -> 108 us
  local copies, waits for them, and re-layouts: 6.72 us -> 4.82 us
    pallas_call x1, Pallas kernels: 56.8 us -> 53.2 us  [call(): pl.pallas_call(kernel, out_shape=tuple((jax.ShapeDtypeStruct(shape, dtype...]
where the time goes in v20:
time: 114 us; the launch traced here: 113 us
  Pallas kernels  108 us (95%)
  local copies, waits for them, and re-layouts  4.82 us (4%)
    pallas_call x1, Pallas kernels, row_sum(): pl.pallas_call(functools.partial(row_sum_kernel, n, split), out_shape=jax...  54.7 us
    pallas_call x1, Pallas kernels, call(): pl.pallas_call(kernel, out_shape=tuple((jax.ShapeDtypeStruct(shape, dtype...  53.2 us

profile of v20, /device:TPU:6, one launch (start us, length us, event | category | flops | bytes accessed | tf_op | source)
XLA Modules:
  0.0 113.4 jit_solution(9379695815680881235)
XLA Ops:
  0.6 53.2 %shard_map.67 = (bf16[32,512]{1,0:T(8,128)(2,1)}, bf16[32,512]{1,0:T(8,128)(2,1)}, bf16[32,512]{1,0:T(8,128)(2,1)}, bf16[32,512]{1,0:T(8,128)(2,1)}, bf16[32,512...) custom-call(bf16[32,512]{1,0:T(8,128)(2,1)} %bitcast.25, ...), custom_call_target="tpu_custom_call" | custom-call | tf_op jit(solution)/shard_map/pallas_call | solution.py:470
  53.8 54.7 %shard_map.68 = f32[32,72,128]{2,1,0:T(8,128)} custom-call(f32[32,72,128]{2,1,0:T(8,128)} %bitcast.22), custom_call_target="tpu_custom_call" | custom-call | tf_op jit(solution)/shard_map/pallas_call | solution.py:246
  108.6 1.3 %fusion = (f32[16,72,128]{2,1,0:T(8,128)S(1)}, f32[16,72,128]{2,1,0:T(8,128)S(1)}) fusion(f32[32,72,128]{2,1,0:T(8,128)} %shard_map.68), kind=kLoop, calls=%fused_computation | loop fusion | bytes 2359296 | tf_op jit(solution)/shard_map/slice | solution.py:562
  109.9 0.4 copy.8
  110.3 1.1 reshape.33
  111.3 0.0 copy-start
  111.3 0.4 copy.7
  111.7 1.1 reshape.31
  112.8 0.0 copy-done
  112.8 0.6 copy.10
Async XLA Ops:
  111.3 1.4 %copy-start = (bf16[32,512]{1,0:T(8,128)(2,1)S(1)}, bf16[32,512]{1,0:T(8,128)(2,1)}, u32[]{:S(2)}) copy-start(bf16[32,512]{1,0:T(8,128)(2,1)} %get-tuple-element.5) | copy-start | bytes 98308

commit v21 on v20

--- a/solution.py
+++ b/solution.py
@@ -356,11 +356,14 @@
 
 
 def conv_parts(w_ref, x):
+    nk, o, i_ch = w_ref.shape
+    every = jnp.dot(w_ref[...].reshape(nk * o, i_ch), x, preferred_element_type=jnp.float32)
     parts = []
     for a in range(3):
         total = None
         for b in range(3):
-            part = jnp.dot(w_ref[a * 3 + b], x, preferred_element_type=jnp.float32)
+            k = a * 3 + b
+            part = every[k * o:(k + 1) * o]
             if b != 1:
                 part = lane_shift(part, b - 1)
             total = part if total is None else total + part
@@ -386,11 +389,17 @@
 def weight_rows(rows3, full, wt_ref, base):
     nq = full.shape[0] // 128
     ao = rows3.shape[0]
+    shifted = []
     for b in range(3):
         moved = rows3
         if b != 1:
             moved = lane_shift(rows3.astype(jnp.float32), 1 - b).astype(rows3.dtype)
-        part = lax.dot_general(moved, full, (((1,), (1,)), ((), ())), preferred_element_type=jnp.float32)
+        shifted.append(moved)
+    every = lax.dot_general(
+        jnp.concatenate(shifted, axis=0), full, (((1,), (1,)), ((), ())), preferred_element_type=jnp.float32
+    )
+    for b in range(3):
+        part = every[b * ao:(b + 1) * ao]
         for q in range(nq):
             wt_ref[pl.ds(base + (b * nq + q) * ao, ao), :] = part[:, q * 128:(q + 1) * 128]
 

time: 114 us -> 112 us (0.982)
  Pallas kernels: 108 us -> 105 us
    pallas_call x1, Pallas kernels: 53.2 us -> 51.6 us  [call(): pl.pallas_call(kernel, out_shape=tuple((jax.ShapeDtypeStruct(shape, dtype...]
    pallas_call x1, Pallas kernels: 54.7 us -> 53.4 us  [row_sum(): pl.pallas_call(functools.partial(row_sum_kernel, n, split), out_shape=jax...]
where the time goes in v21:
time: 112 us; the launch traced here: 110 us
  Pallas kernels  105 us (94%)
  local copies, waits for them, and re-layouts  4.82 us (4%)
    pallas_call x1, Pallas kernels, row_sum(): pl.pallas_call(functools.partial(row_sum_kernel, n, split), out_shape=jax...  53.4 us
    pallas_call x1, Pallas kernels, call(): pl.pallas_call(kernel, out_shape=tuple((jax.ShapeDtypeStruct(shape, dtype...  51.6 us

profile of v21, /device:TPU:6, one launch (start us, length us, event | category | flops | bytes accessed | tf_op | source)
XLA Modules:
  0.0 110.5 jit_solution(1549076114439991063)
XLA Ops:
  0.6 51.6 %shard_map.67 = (bf16[32,512]{1,0:T(8,128)(2,1)}, bf16[32,512]{1,0:T(8,128)(2,1)}, bf16[32,512]{1,0:T(8,128)(2,1)}, bf16[32,512]{1,0:T(8,128)(2,1)}, bf16[32,512...) custom-call(bf16[32,512]{1,0:T(8,128)(2,1)} %bitcast.25, ...), custom_call_target="tpu_custom_call" | custom-call | tf_op jit(solution)/shard_map/pallas_call | solution.py:479
  52.2 53.4 %shard_map.68 = f32[32,72,128]{2,1,0:T(8,128)} custom-call(f32[32,72,128]{2,1,0:T(8,128)} %bitcast.22), custom_call_target="tpu_custom_call" | custom-call | tf_op jit(solution)/shard_map/pallas_call | solution.py:246
  105.7 1.3 %fusion = (f32[16,72,128]{2,1,0:T(8,128)S(1)}, f32[16,72,128]{2,1,0:T(8,128)S(1)}) fusion(f32[32,72,128]{2,1,0:T(8,128)} %shard_map.68), kind=kLoop, calls=%fused_computation | loop fusion | bytes 2359296 | tf_op jit(solution)/shard_map/slice | solution.py:571
  107.0 0.4 copy.8
  107.4 1.1 reshape.33
  108.4 0.0 copy-start
  108.4 0.4 copy.7
  108.8 1.1 reshape.31
  109.9 0.0 copy-done
  109.9 0.6 copy.10
Async XLA Ops:
  108.4 1.4 %copy-start = (bf16[32,512]{1,0:T(8,128)(2,1)S(1)}, bf16[32,512]{1,0:T(8,128)(2,1)}, u32[]{:S(2)}) copy-start(bf16[32,512]{1,0:T(8,128)(2,1)} %get-tuple-element.5) | copy-start | bytes 98308

commit v22 on v21

--- a/solution.py
+++ b/solution.py
@@ -436,9 +436,13 @@
     per = 128 // blk
     for q in range(w2r.shape[2] // 128):
         total = None
+        lhs = jnp.concatenate(
+            [jnp.concatenate([w2r[a * 3 + b, :, q * 128:(q + 1) * 128] for a in range(3)], axis=0) for b in range(3)],
+            axis=1,
+        )
+        every = lax.dot_general(lhs, rows3, (((0,), (0,)), ((), ())), preferred_element_type=jnp.float32)
         for b in range(3):
-            lhs = jnp.concatenate([w2r[a * 3 + b, :, q * 128:(q + 1) * 128] for a in range(3)], axis=0)
-            part = lax.dot_general(lhs, rows3, (((0,), (0,)), ((), ())), preferred_element_type=jnp.float32)
+            part = every[b * 128:(b + 1) * 128]
             if b != 1:
                 part = lane_shift(part, 1 - b)
             total = part if total is None else total + part

time: 112 us -> 112 us (level)
  no operation moved by 1% of the time
where the time goes in v22:
time: 112 us; the launch traced here: 111 us
  Pallas kernels  105 us (94%)
  local copies, waits for them, and re-layouts  4.82 us (4%)
    pallas_call x1, Pallas kernels, row_sum(): pl.pallas_call(functools.partial(row_sum_kernel, n, split), out_shape=jax...  53.7 us
    pallas_call x1, Pallas kernels, call(): pl.pallas_call(kernel, out_shape=tuple((jax.ShapeDtypeStruct(shape, dtype...  51.6 us

profile of v22, /device:TPU:6, one launch (start us, length us, event | category | flops | bytes accessed | tf_op | source)
XLA Modules:
  0.0 110.8 jit_solution(11475341333438706133)
XLA Ops:
  0.6 51.6 %shard_map.67 = (bf16[32,512]{1,0:T(8,128)(2,1)}, bf16[32,512]{1,0:T(8,128)(2,1)}, bf16[32,512]{1,0:T(8,128)(2,1)}, bf16[32,512]{1,0:T(8,128)(2,1)}, bf16[32,512...) custom-call(bf16[32,512]{1,0:T(8,128)(2,1)} %bitcast.25, ...), custom_call_target="tpu_custom_call" | custom-call | tf_op jit(solution)/shard_map/pallas_call | solution.py:483
  52.2 53.7 %shard_map.68 = f32[32,72,128]{2,1,0:T(8,128)} custom-call(f32[32,72,128]{2,1,0:T(8,128)} %bitcast.22), custom_call_target="tpu_custom_call" | custom-call | tf_op jit(solution)/shard_map/pallas_call | solution.py:246
  105.9 1.3 %fusion = (f32[16,72,128]{2,1,0:T(8,128)S(1)}, f32[16,72,128]{2,1,0:T(8,128)S(1)}) fusion(f32[32,72,128]{2,1,0:T(8,128)} %shard_map.68), kind=kLoop, calls=%fused_computation | loop fusion | bytes 2359296 | tf_op jit(solution)/shard_map/slice | solution.py:575
  107.2 0.4 copy.8
  107.6 1.1 reshape.33
  108.7 0.0 copy-start
  108.7 0.4 copy.7
  109.1 1.1 reshape.31
  110.1 0.0 copy-done
  110.1 0.6 copy.10
Async XLA Ops:
  108.7 1.4 %copy-start = (bf16[32,512]{1,0:T(8,128)(2,1)S(1)}, bf16[32,512]{1,0:T(8,128)(2,1)}, u32[]{:S(2)}) copy-start(bf16[32,512]{1,0:T(8,128)(2,1)} %get-tuple-element.5) | copy-start | bytes 98308

commit v23 on v21

--- a/solution.py
+++ b/solution.py
@@ -182,7 +182,7 @@
         self.back().wait_send()
 
 
-def row_sum_kernel(n, split, x32, f32_out, xa, xb, oa, ob, *scratch):
+def row_sum_kernel(n, split, x32, f_lo, f_hi, xa, xb, oa, ob, *scratch):
     zn = n // 2
     me = lax.axis_index("rows")
     my_z = lax.rem(me, zn)
@@ -225,12 +225,16 @@
     a.s4_finish()
     b.s4_finish()
 
-    def widen(c, carry):
-        f32_out[c, pl.ds(0, split), :] = oa[c].astype(f32_out.dtype)
-        f32_out[c, pl.ds(split, x32.shape[1] - split), :] = ob[c].astype(f32_out.dtype)
-        return carry
-
-    lax.fori_loop(0, n, widen, 0)
+    def widen(f_ref, base):
+        def body(c, carry):
+            f_ref[c, pl.ds(0, split), :] = oa[base + c].astype(f_ref.dtype)
+            f_ref[c, pl.ds(split, x32.shape[1] - split), :] = ob[base + c].astype(f_ref.dtype)
+            return carry
+
+        lax.fori_loop(0, f_ref.shape[0], body, 0)
+
+    widen(f_lo, 0)
+    widen(f_hi, f_lo.shape[0])
 
 
 def row_sum(x, collective_id):
@@ -245,9 +249,9 @@
         scratch += [pltpu.VMEM(blk, jnp.bfloat16)] * 3 + [pltpu.SemaphoreType.DMA((6, zn))]
     return pl.pallas_call(
         functools.partial(row_sum_kernel, n, split),
-        out_shape=jax.ShapeDtypeStruct(x.shape, jnp.float32),
+        out_shape=(jax.ShapeDtypeStruct((zn,) + x.shape[1:], jnp.float32),) * 2,
         in_specs=[spec],
-        out_specs=spec,
+        out_specs=(spec, spec),
         scratch_shapes=scratch,
         compiler_params=pltpu.CompilerParams(collective_id=collective_id, has_side_effects=True),
     )(x)
@@ -568,7 +572,7 @@
     summed = row_sum(wt_all.reshape(n_rows, -1, 128), 0)
     first_grad, second_grad = (
         half.reshape(3, nq, 3, o, 128).transpose(3, 2, 0, 1, 4).reshape(o, 3, 3, i_ch)
-        for half in (summed[: n_rows // 2], summed[n_rows // 2:])
+        for half in summed
     )
     return (block_out[:, None, :], first_grad, second_grad)
 

time: 112 us -> 112 us (level)
    slice x1 -> x0, local copies, waits for them, and re-layouts: 1.32 us -> none  [per_device(): summed[n_rows // 2:]]
    transpose x2, local copies, waits for them, and re-layouts: 0.77 us -> 1.9 us  [per_device(): half.reshape(3, nq, 3, o, 128).transpose(3, 2, 0, 1, 4)]
where the time goes in v23:
time: 112 us; the launch traced here: 111 us
  Pallas kernels  105 us (94%)
  local copies, waits for them, and re-layouts  4.62 us (4%)
    pallas_call x1, Pallas kernels, row_sum(): pl.pallas_call(functools.partial(row_sum_kernel, n, split), out_shape=(ja...  53.7 us
    pallas_call x1, Pallas kernels, call(): pl.pallas_call(kernel, out_shape=tuple((jax.ShapeDtypeStruct(shape, dtype...  51.6 us

profile of v23, /device:TPU:6, one launch (start us, length us, event | category | flops | bytes accessed | tf_op | source)
XLA Modules:
  0.0 110.6 jit_solution(382133079666844496)
XLA Ops:
  0.6 51.6 %shard_map.67 = (bf16[32,512]{1,0:T(8,128)(2,1)}, bf16[32,512]{1,0:T(8,128)(2,1)}, bf16[32,512]{1,0:T(8,128)(2,1)}, bf16[32,512]{1,0:T(8,128)(2,1)}, bf16[32,512...) custom-call(bf16[32,512]{1,0:T(8,128)(2,1)} %bitcast.25, ...), custom_call_target="tpu_custom_call" | custom-call | tf_op jit(solution)/shard_map/pallas_call | solution.py:483
  52.2 53.7 %shard_map.68 = (f32[16,72,128]{2,1,0:T(8,128)}, f32[16,72,128]{2,1,0:T(8,128)}) custom-call(f32[32,72,128]{2,1,0:T(8,128)} %bitcast.20), custom_call_target="tpu_custom_call" | custom-call | tf_op jit(solution)/shard_map/pallas_call | solution.py:250
  106.0 0.0 copy-start
  106.0 1.5 %copy.7 = f32[32,3,3,4,128]{4,3,0,2,1:T(4,128)S(1)} copy(f32[32,3,3,4,128]{4,0,1,3,2:T(8,128)} %bitcast.22) | data formatting | bytes 1179648 | tf_op jit(solution)/shard_map/transpose | solution.py:574
  107.5 1.1 reshape.31
  108.5 0.0 copy-done
  108.5 0.0 copy-start.1
  108.5 0.4 copy.8
  108.9 1.1 reshape.33
  110.0 0.0 copy-done.1
  110.0 0.6 copy.10
Async XLA Ops:
  106.0 2.6 %copy-start = (f32[16,72,128]{2,1,0:T(8,128)S(1)}, f32[16,72,128]{2,1,0:T(8,128)}, u32[]{:S(2)}) copy-start(f32[16,72,128]{2,1,0:T(8,128)} %get-tuple-element.10) | copy-start | bytes 1769476
  108.5 1.4 %copy-start.1 = (bf16[32,512]{1,0:T(8,128)(2,1)S(1)}, bf16[32,512]{1,0:T(8,128)(2,1)}, u32[]{:S(2)}) copy-start(bf16[32,512]{1,0:T(8,128)(2,1)} %get-tuple-element.7) | copy-start | bytes 98308

commit v24 on v21

--- a/solution.py
+++ b/solution.py
@@ -196,7 +196,6 @@
         xb[c] = x32[c, pl.ds(split, x32.shape[1] - split), :].astype(xb.dtype)
         return carry
 
-    lax.fori_loop(0, n, narrow, 0)
     barrier = pltpu.get_barrier_semaphore()
     pl.semaphore_signal(barrier, 1, device_id=dev(lax.rem(me + zn, n)), device_id_type=MESH)
 
@@ -205,6 +204,7 @@
         return carry
 
     lax.fori_loop(1, zn, greet, 0)
+    lax.fori_loop(0, n, narrow, 0)
     pl.semaphore_wait(barrier, zn)
     a = RowSum(n, xa, oa, *scratch[:4])
     b = RowSum(n, xb, ob, *scratch[4:])

time: 112 us -> 112 us (level)
  no operation moved by 1% of the time
where the time goes in v24:
time: 112 us; the launch traced here: 111 us
  Pallas kernels  105 us (94%)
  local copies, waits for them, and re-layouts  4.82 us (4%)
    pallas_call x1, Pallas kernels, row_sum(): pl.pallas_call(functools.partial(row_sum_kernel, n, split), out_shape=jax...  53.5 us
    pallas_call x1, Pallas kernels, call(): pl.pallas_call(kernel, out_shape=tuple((jax.ShapeDtypeStruct(shape, dtype...  51.6 us

profile of v24, /device:TPU:6, one launch (start us, length us, event | category | flops | bytes accessed | tf_op | source)
XLA Modules:
  0.0 110.6 jit_solution(11809952453229109409)
XLA Ops:
  0.6 51.6 %shard_map.67 = (bf16[32,512]{1,0:T(8,128)(2,1)}, bf16[32,512]{1,0:T(8,128)(2,1)}, bf16[32,512]{1,0:T(8,128)(2,1)}, bf16[32,512]{1,0:T(8,128)(2,1)}, bf16[32,512...) custom-call(bf16[32,512]{1,0:T(8,128)(2,1)} %bitcast.25, ...), custom_call_target="tpu_custom_call" | custom-call | tf_op jit(solution)/shard_map/pallas_call | solution.py:479
  52.2 53.5 %shard_map.68 = f32[32,72,128]{2,1,0:T(8,128)} custom-call(f32[32,72,128]{2,1,0:T(8,128)} %bitcast.22), custom_call_target="tpu_custom_call" | custom-call | tf_op jit(solution)/shard_map/pallas_call | solution.py:246
  105.7 1.3 %fusion = (f32[16,72,128]{2,1,0:T(8,128)S(1)}, f32[16,72,128]{2,1,0:T(8,128)S(1)}) fusion(f32[32,72,128]{2,1,0:T(8,128)} %shard_map.68), kind=kLoop, calls=%fused_computation | loop fusion | bytes 2359296 | tf_op jit(solution)/shard_map/slice | solution.py:571
  107.0 0.4 copy.8
  107.4 1.1 reshape.33
  108.5 0.0 copy-start
  108.5 0.4 copy.7
  108.9 1.1 reshape.31
  109.9 0.0 copy-done
  109.9 0.6 copy.10
Async XLA Ops:
  108.5 1.4 %copy-start = (bf16[32,512]{1,0:T(8,128)(2,1)S(1)}, bf16[32,512]{1,0:T(8,128)(2,1)}, u32[]{:S(2)}) copy-start(bf16[32,512]{1,0:T(8,128)(2,1)} %get-tuple-element.5) | copy-start | bytes 98308
